TPU v7x, 128 devices: a whole 4x4x4 slice. The times are simulated.
128 devices in a mesh: row: 8 (over z, core), col: 16 (over x, y).
Axes of the slice: x: 4, y: 4, z: 4, core: 2. Of those that a mesh axis runs over, the one named last changes fastest.
Arguments:
- nodes: bfloat16 [65536, 512], P(('row', 'col')), may hold values from -6 to 6
- cotangent: bfloat16 [65536, 512], P(('row', 'col')), may hold values from -6 to 6
- edge_source: int32 [262144], P(('row', 'col')), may hold values from 0 to 639
- edge_target: int32 [262144], P(('row', 'col')), may hold values from 0 to 511
- halo_lists: int32 [128, 4, 32], P(('row', 'col')), may hold values from 0 to 511
- pool_owner: int32 [65536], P(('row', 'col')), may hold values from 0 to 127, as said below
- pool_table: int32 [128, 1024], P(('row', 'col')), may hold values from -1 to 127, as said below
- source_weight: bfloat16 [512, 512], replicated, may hold values from -0.25 to 0.25
- target_weight: bfloat16 [512, 512], replicated, may hold values from -0.25 to 0.25
- edge_weight: bfloat16 [512, 512], replicated, may hold values from -0.25 to 0.25
- inner_weight: bfloat16 [1024, 512], replicated, may hold values from -0.1875 to 0.1875
- outer_weight: bfloat16 [512, 512], replicated, may hold values from -0.25 to 0.25
- coarse_weight: bfloat16 [512, 512], replicated, may hold values from -0.5 to 0.5
Outputs:
- updated: bfloat16 [65536, 512], P(('row', 'col'))
- node_gradient: float32 [65536, 512], P(('row', 'col'))
- source_gradient: float32 [512, 512], replicated
- target_gradient: float32 [512, 512], replicated
- edge_gradient: float32 [512, 512], replicated
- inner_gradient: float32 [1024, 512], replicated
- outer_gradient: float32 [512, 512], replicated
- coarse_gradient: float32 [512, 512], replicated
Inputs may be any that keep to these rules, and one draw needn't show every extreme that they name: `edge_source`: rows below 512 are the partition's own nodes; row 512 + k * 32 + j is row j of halo block k. `pool_owner`: at most 8 nodes of one partition name the same owner; one owner is named by exactly 8 nodes of every partition. `pool_table`: entry [o, q * 8 + k] is the coarse row of owner o for the node of rank k among the nodes of partition q that name o, and -1 where q names o fewer than k + 1 times.
All inputs are finite; a program needn't handle non-finite values.
Results may differ from a plain program's by a relative error of at most 0.014.
Values may be sent and summed in bfloat16 or wider, within the bound.
No kernel may reach another device: no remote copies, remote signals or barrier semaphores. Data moves between devices by JAX's collectives and lax.ppermute only.
A program may use at most 128 MiB of HBM per device.

v0:
```python
import math

import jax
import jax.numpy as jnp
from jax import lax
from jax.sharding import PartitionSpec as P


def passed_along(value, axis, steps):
    count = lax.axis_size(axis)
    initial, last = (max(0, -steps), min(count, count - steps))
    return lax.ppermute(value, axis, [(source, source + steps) for source in range(initial, last)])


def product(first, second):
    return jnp.dot(first, second, preferred_element_type=jnp.float32)


def left_product(first, second):
    return lax.dot_general(
        first, second, (((0,), (0,)), ((), ())), preferred_element_type=jnp.float32
    )


def right_product(first, second):
    return lax.dot_general(
        first, second, (((1,), (1,)), ((), ())), preferred_element_type=jnp.float32
    )


def silu_slope(value):
    sigma = jax.nn.sigmoid(value)
    return sigma * (1.0 + value * (1.0 - sigma))


def trade_halo(blocks, flip):
    moved = []
    for number, offset in enumerate((1, -1)):
        moved.append(passed_along(blocks[number], "row", offset * flip))
    for number, offset in enumerate((1, -1)):
        moved.append(passed_along(blocks[2 + number], "col", offset * flip))
    return moved


def trade_slots(buffer):
    return lax.all_to_all(buffer, ("row", "col"), split_axis=0, concat_axis=0, tiled=True)


def toward_owners(values, slot, devices, capacity, trader):
    width = values.shape[1]
    outgoing = jnp.zeros((devices * capacity, width), values.dtype).at[slot].set(values)
    arrived = trader(outgoing.reshape(devices, capacity, width))
    return arrived.reshape(devices * capacity, width)


def toward_sources(coarse_values, table, slot, devices, capacity, trader):
    width = coarse_values.shape[1]
    picked = jnp.take(coarse_values, jnp.maximum(table, 0), axis=0)
    picked = jnp.where((table >= 0)[:, None], picked, jnp.zeros_like(picked))
    returned = trader(picked.reshape(devices, capacity, width)).reshape(devices * capacity, width)
    return jnp.take(returned, slot, axis=0)


def local(
    nodes,
    cotangent,
    edge_source,
    edge_target,
    halo_lists,
    pool_owner,
    pool_table,
    source_weight,
    target_weight,
    edge_weight,
    inner_weight,
    outer_weight,
    coarse_weight,
):
    devices = lax.axis_size("row") * lax.axis_size("col")
    count_rows, width = nodes.shape
    lists = halo_lists[0]
    halo_rows = lists.shape[1]
    table = pool_table[0]
    capacity = table.shape[0] // devices
    coarse_rows = count_rows // 4
    scale = 1.0 / math.sqrt(count_rows * devices)
    received = trade_halo([jnp.take(nodes, lists[number], axis=0) for number in range(4)], 1)
    extended = jnp.concatenate([nodes] + received, axis=0)
    source_side = product(extended, source_weight)
    target_side = product(nodes, target_weight)
    edge_linear = jnp.take(source_side, edge_source, axis=0) + jnp.take(
        target_side, edge_target, axis=0
    )
    edge_hidden = jax.nn.silu(edge_linear).astype(jnp.bfloat16)
    message_linear = product(edge_hidden, edge_weight)
    aggregate = jax.ops.segment_sum(jax.nn.silu(message_linear), edge_target, count_rows).astype(
        jnp.bfloat16
    )
    joined = jnp.concatenate([nodes, aggregate], axis=1)
    node_linear = product(joined, inner_weight)
    node_hidden = jax.nn.silu(node_linear).astype(jnp.bfloat16)
    refined = (nodes.astype(jnp.float32) + product(node_hidden, outer_weight)).astype(jnp.bfloat16)
    owner_hot = (pool_owner[:, None] == jnp.arange(devices, dtype=jnp.int32)[None, :]).astype(
        jnp.bfloat16
    )
    positions = jnp.arange(count_rows, dtype=jnp.int32)
    lower = (positions[:, None] > positions[None, :]).astype(jnp.bfloat16)
    rank = jnp.sum(product(lower, owner_hot) * owner_hot, axis=1).astype(jnp.int32)
    slot = pool_owner * capacity + rank
    member = (jnp.arange(coarse_rows, dtype=jnp.int32)[:, None] == table[None, :]).astype(
        jnp.bfloat16
    )
    count = jnp.maximum(jnp.sum(member, axis=1, dtype=jnp.float32), 1.0)[:, None]
    arrived = toward_owners(refined, slot, devices, capacity, trade_slots)
    coarse = (product(member, arrived) / count).astype(jnp.bfloat16)
    coarse_linear = product(coarse, coarse_weight)
    coarse_update = jax.nn.silu(coarse_linear).astype(jnp.bfloat16)
    parent_rows = toward_sources(coarse_update, table, slot, devices, capacity, trade_slots)
    arrived_grad = toward_owners(cotangent, slot, devices, capacity, trade_slots)
    grad_coarse = (product(member, arrived_grad) * silu_slope(coarse_linear)).astype(jnp.bfloat16)
    coarse_share = (right_product(grad_coarse, coarse_weight) / count).astype(jnp.bfloat16)
    share_rows = toward_sources(coarse_share, table, slot, devices, capacity, trade_slots)
    updated = (refined.astype(jnp.float32) + parent_rows.astype(jnp.float32)).astype(jnp.bfloat16)
    coarse_gradient = left_product(coarse, grad_coarse)
    grad_refined = cotangent.astype(jnp.float32) + share_rows.astype(jnp.float32)
    refined_low = grad_refined.astype(jnp.bfloat16)
    outer_gradient = left_product(node_hidden, refined_low)
    grad_hidden = (right_product(refined_low, outer_weight) * silu_slope(node_linear)).astype(
        jnp.bfloat16
    )
    inner_gradient = left_product(joined, grad_hidden)
    grad_joined = right_product(grad_hidden, inner_weight)
    grad_aggregate = grad_joined[:, width:].astype(jnp.bfloat16)
    grad_message = (
        jnp.take(grad_aggregate, edge_target, axis=0) * silu_slope(message_linear)
    ).astype(jnp.bfloat16)
    edge_gradient = left_product(edge_hidden, grad_message)
    grad_edges = right_product(grad_message, edge_weight) * silu_slope(edge_linear)
    grad_sources = jax.ops.segment_sum(grad_edges, edge_source, extended.shape[0]).astype(
        jnp.bfloat16
    )
    grad_targets = jax.ops.segment_sum(grad_edges, edge_target, count_rows).astype(jnp.bfloat16)
    source_gradient = left_product(extended, grad_sources)
    target_gradient = left_product(nodes, grad_targets)
    (
        source_gradient,
        target_gradient,
        edge_gradient,
        inner_gradient,
        outer_gradient,
        coarse_gradient,
    ) = lax.psum(
        (
            source_gradient,
            target_gradient,
            edge_gradient,
            inner_gradient,
            outer_gradient,
            coarse_gradient,
        ),
        ("row", "col"),
    )
    grad_extended = right_product(grad_sources, source_weight)
    back_blocks = grad_extended[count_rows:].astype(jnp.bfloat16).reshape(4, halo_rows, width)
    returned = trade_halo([back_blocks[number] for number in range(4)], -1)
    node_gradient = (
        grad_refined
        + grad_joined[:, :width]
        + right_product(grad_targets, target_weight)
        + grad_extended[:count_rows]
    )
    node_gradient = node_gradient.at[lists.reshape(-1)].add(
        jnp.concatenate(returned, axis=0).astype(jnp.float32)
    )
    return (
        updated,
        node_gradient,
        source_gradient * scale,
        target_gradient * scale,
        edge_gradient * scale,
        inner_gradient * scale,
        outer_gradient * scale,
        coarse_gradient * scale,
    )


def solution(mesh):
    in_specs = (
        P(("row", "col"), None),
        P(("row", "col"), None),
        P(("row", "col")),
        P(("row", "col")),
        P(("row", "col"), None, None),
        P(("row", "col")),
        P(("row", "col"), None),
        P(),
        P(),
        P(),
        P(),
        P(),
        P(),
    )
    out_specs = (P(("row", "col"), None), P(("row", "col"), None), P(), P(), P(), P(), P(), P())
    return jax.shard_map(local, mesh=mesh, in_specs=in_specs, out_specs=out_specs, check_vma=False)
```

profile of v0, /device:TPU:1, one launch (start us, length us, event | category | flops | bytes accessed | tf_op | source)
XLA Modules:
  0.0 423.6 jit_solution(16720933355326291041)
XLA Ops:
  8.1 1.7 gather_fusion.3
  9.9 4.9 %collective-permute-start = (bf16[32,512]{1,0:T(8,128)(2,1)S(1)}, bf16[32,512]{1,0:T(8,128)(2,1)S(1)}, u32[]{:S(2)}, u32[]{:S(2)}) collective-permute-start(bf16[32,512]{1,0:T(8,128)(2,1)S(1)} %broadcast_select_fusion.4), channel_id=1, source_target_pairs={{0,16},{16,32},{32,48},{48,64},{64,80},{80,96},{96,112},{1,17},{17... | collective-permute-start | bytes 98312 | tf_op jit(solution)/shard_map/ppermute | solution.py:12
  14.8 1.7 gather_fusion.4
  16.7 1.9 collective-permute-start.1
  18.6 1.7 gather_fusion.5
  20.4 3.2 collective-permute-start.2
  23.6 1.7 gather_fusion.6
  28.8 1.6 fusion.57
  32.1 8.9 %gather_fusion.1 = f32[2048,512]{1,0:T(8,128)} fusion(f32[512,512]{1,0:T(8,128)S(1)} %fusion.57, s32[2048]{0:T(1024)S(1)} %get-tuple-element.46), kind=kCustom, calls=%fused_computation.9 | custom fusion | bytes 8396800 | tf_op jit(solution)/shard_map/jit(_take)/gather | solution.py:91
  42.6 8.9 %gather_fusion = f32[2048,512]{1,0:T(8,128)} fusion(f32[640,512]{1,0:T(8,128)S(1)} %fusion.56, s32[2048]{0:T(1024)S(1)} %get-tuple-element.45), kind=kCustom, calls=%fused_computation.8 | custom fusion | bytes 8396800 | tf_op jit(solution)/shard_map/jit(_take)/gather | solution.py:91
  51.6 4.2 %multiply_convert_fusion.1 = bf16[2048,512]{1,0:T(8,128)(2,1)S(1)} fusion(f32[2048,512]{1,0:T(8,128)} %gather_fusion.1, pred[2048]{0:T(1024)(128)(4,1)} %get-tuple-element.47, f32[2048,512]{1,0:T(8,128)} %gather_fusion, pred[2048]{0:T(1024)(128)(4,1)} %get-tuple-element.48), kind=kLoop, calls=%fused_computation.22 | loop fusion | flops 8388608 | bytes 10489856 | tf_op jit(solution)/shard_map/convert_element_type | solution.py:94
  57.1 3.3 fusion.58
  60.4 14.6 %scatter_custom_fusion = f32[512,512]{1,0:T(8,128)S(1)} fusion(s32[2048]{0:T(1024)} %param.22, f32[2048,512]{1,0:T(8,128)} %fusion.58, f32[]{:T(128)} %constant.62.clone.1, f32[]{:T(128)} %constant.52.clone.1), kind=kCustom, calls=%fused_computation.19 | custom fusion | flops 5242880 | bytes 5243904 | tf_op jit(solution)/shard_map/scatter-add | solution.py:96
  77.2 3.6 scatter_custom_fusion.1
  80.8 11.6 %all-to-all-start = ((bf16[128,8,512]{2,1,0:T(8,128)(2,1)}), bf16[128,8,512]{2,1,0:T(8,128)(2,1)S(1)}, u32[]{:S(2)}, u32[]{:S(2)}) async-start(bf16[128,8,512]{2,1,0:T(8,128)(2,1)} %bitcast.5), calls=%async_computation | async-start | bytes 2097152 | tf_op jit(solution)/shard_map/all_to_all | solution.py:46
  92.4 4.0 scatter_custom_fusion.2
  96.4 14.7 %all-to-all-done = bf16[128,8,512]{2,1,0:T(8,128)(2,1)S(1)} async-done(((bf16[128,8,512]{2,1,0:T(8,128)(2,1)}), bf16[128,8,512]{2,1,0:T(8,128)(2,1)S(1)}, u32[]{:S(2)}, u32[]{:S(2)}) %all-to-all-start) | async-done | bytes 1048608 | tf_op jit(solution)/shard_map/all_to_all | solution.py:46
  111.2 5.7 %all-to-all-start.2 = ((bf16[128,8,512]{2,1,0:T(8,128)(2,1)}), bf16[128,8,512]{2,1,0:T(8,128)(2,1)}, u32[]{:S(2)}, u32[]{:S(2)}) async-start(bf16[128,8,512]{2,1,0:T(8,128)(2,1)} %bitcast.9), calls=%async_computation.2 | async-start | bytes 2097152 | tf_op jit(solution)/shard_map/all_to_all | solution.py:46
  119.2 16.3 %all-to-all-done.2 = bf16[128,8,512]{2,1,0:T(8,128)(2,1)} async-done(((bf16[128,8,512]{2,1,0:T(8,128)(2,1)}), bf16[128,8,512]{2,1,0:T(8,128)(2,1)}, u32[]{:S(2)}, u32[]{:S(2)}) %all-to-all-start.2) | async-done | bytes 1048608 | tf_op jit(solution)/shard_map/all_to_all | solution.py:46
  139.1 4.0 gather_fusion.9
  143.1 5.1 %gather_fusion.7 = bf16[1024,512]{1,0:T(8,128)(2,1)} fusion(bf16[128,512]{1,0:T(8,128)(2,1)S(1)} %get-tuple-element.41, s32[1024]{0:T(1024)S(1)} %maximum_clamp_fusion), kind=kCustom, calls=%fused_computation.1.clone | custom fusion | bytes 2101248 | tf_op jit(solution)/shard_map/jit(_take)/gather | solution.py:58
  148.2 2.9 fusion.12
  151.1 4.8 %all-to-all-start.3 = ((bf16[128,8,512]{2,1,0:T(8,128)(2,1)}), bf16[128,8,512]{2,1,0:T(8,128)(2,1)S(1)}, u32[]{:S(2)}, u32[]{:S(2)}) async-start(bf16[128,8,512]{2,1,0:T(8,128)(2,1)} %get-tuple-element.33), calls=%async_computation.3 | async-start | bytes 2097152 | tf_op jit(solution)/shard_map/all_to_all | solution.py:46
  156.0 2.3 fusion.61
  158.3 16.6 %all-to-all-done.3 = bf16[128,8,512]{2,1,0:T(8,128)(2,1)S(1)} async-done(((bf16[128,8,512]{2,1,0:T(8,128)(2,1)}), bf16[128,8,512]{2,1,0:T(8,128)(2,1)S(1)}, u32[]{:S(2)}, u32[]{:S(2)}) %all-to-all-start.3) | async-done | bytes 1048608 | tf_op jit(solution)/shard_map/all_to_all | solution.py:46
  174.9 2.6 gather_fusion.10
  177.5 2.4 fusion.5
  182.1 9.2 %gather_fusion.2 = bf16[2048,512]{1,0:T(8,128)(2,1)} fusion(bf16[512,512]{1,0:T(8,128)(2,1)S(1)} %slice.97, s32[2048]{0:T(1024)S(1)} %get-tuple-element.46), kind=kCustom, calls=%fused_computation.10 | custom fusion | bytes 4202496 | tf_op jit(solution)/shard_map/jit(_take)/gather | solution.py:135
  191.3 3.8 multiply_convert_fusion
  197.4 4.3 %multiply_multiply_fusion = f32[2048,512]{1,0:T(8,128)} fusion(bf16[2048,512]{1,0:T(8,128)(2,1)S(1)} %multiply_convert_fusion, bf16[512,512]{1,0:T(8,128)(2,1)S(1)} %copy-done.20, f32[2048,512]{1,0:T(8,128)S(1)} %copy-done.2, pred[2048]{0:T(1024)(128)(4,1)S(1)} %copy-done.31, f32[2048,512]{1,0:T(8,128)S(1)} %copy-done.3, pred[2048]{0:T(1024)(128)(4,1)S(1)} %copy-done.32), kind=kOutput, calls=%fused_computation.17 | convolution fusion | flops 1085276160 | bytes 15208448 | tf_op jit(solution)/shard_map/dot_general | solution.py:26
  201.6 13.6 %scatter_custom_fusion.4 = f32[640,512]{1,0:T(8,128)S(1)} fusion(s32[2048]{0:T(1024)} %param.21, f32[2048,512]{1,0:T(8,128)} %multiply_multiply_fusion, f32[]{:T(128)} %constant.52.clone.1), kind=kCustom, calls=%fused_computation.59 | custom fusion | flops 1048576 | bytes 1311232 | tf_op jit(solution)/shard_map/scatter-add | solution.py:139
  215.2 13.7 %scatter_custom_fusion.3 = f32[512,512]{1,0:T(8,128)S(1)} fusion(s32[2048]{0:T(1024)} %param.22, f32[2048,512]{1,0:T(8,128)} %multiply_multiply_fusion, f32[]{:T(128)} %constant.52.clone.1), kind=kCustom, calls=%fused_computation.73 | custom fusion | flops 1048576 | bytes 1049088 | tf_op jit(solution)/shard_map/scatter-add | solution.py:142
  229.0 4.9 %fusion.60 = f32[512,512]{1,0:T(8,128)} fusion(bf16[2048,512]{1,0:T(8,128)(2,1)} %copy-done.5, bf16[2048,512]{1,0:T(8,128)(2,1)} %copy-done.10), kind=kOutput, calls=%fused_computation.144 | convolution fusion | flops 1073741824 | bytes 5242880 | tf_op jit(solution)/shard_map/dot_general | solution.py:20
  233.9 2.1 fusion.15
  236.0 1.7 fusion.51
  237.6 1.6 fusion.27
  240.7 4.7 %all-to-all-start.1 = ((bf16[128,8,512]{2,1,0:T(8,128)(2,1)}), bf16[128,8,512]{2,1,0:T(8,128)(2,1)S(1)}, u32[]{:S(2)}, u32[]{:S(2)}) async-start(bf16[128,8,512]{2,1,0:T(8,128)(2,1)} %get-tuple-element.34), calls=%async_computation.1 | async-start | bytes 2097152 | tf_op jit(solution)/shard_map/all_to_all | solution.py:46
  245.5 22.7 %all-to-all-done.1 = bf16[128,8,512]{2,1,0:T(8,128)(2,1)S(1)} async-done(((bf16[128,8,512]{2,1,0:T(8,128)(2,1)}), bf16[128,8,512]{2,1,0:T(8,128)(2,1)S(1)}, u32[]{:S(2)}, u32[]{:S(2)}) %all-to-all-start.1) | async-done | bytes 1048608 | tf_op jit(solution)/shard_map/all_to_all | solution.py:46
  268.2 2.0 gather_fusion.8
  270.3 1.7 fusion.55
  272.0 2.4 collective-permute-start.7
  275.7 3.1 collective-permute-start.5
  278.8 1.9 collective-permute-start.4
  280.8 1.6 fusion.3
  284.1 1.8 scatter_custom_fusion.5
  285.9 121.3 %all-reduce.3.cloned.1.call-done = (f32[512,512]{1,0:T(8,128)}, f32[512,512]{1,0:T(8,128)}, f32[512,512]{1,0:T(8,128)}, f32[1024,512]{1,0:T(8,128)}, f32[512,512]{1,0:T(8,128)}, /*index=5*/f32[512,512]{1,0:T(8,128)}) async-done(((f32[512,512]{1,0:T(8,128)}, f32[512,512]{1,0:T(8,128)}, f32[512,512]{1,0:T(8,128)}, f32[1024,512]{1,0:T(8,128)}, f32[512,512]{1,0:T(8,128)}, /*index=5*/f32[512,512]{1,0:T(8,128)}), ...) | async-done | bytes 7340048 | tf_op jit(solution)/shard_map/psum | solution.py:152
  407.2 2.4 broadcast_multiply_fusion.5
  409.6 2.4 broadcast_multiply_fusion.4
  (142 shorter events, 31.0 us)
Async XLA Ops:
  7.2 68.0 %copy-start = (bf16[1024,512]{1,0:T(8,128)(2,1)S(1)}, bf16[1024,512]{1,0:T(8,128)(2,1)}, u32[]{:S(2)}) copy-start(bf16[1024,512]{1,0:T(8,128)(2,1)} %param.29) | copy-start | bytes 3145732
  7.2 24.9 %copy-start.4 = (bf16[512,512]{1,0:T(8,128)(2,1)S(1)}, bf16[512,512]{1,0:T(8,128)(2,1)}, u32[]{:S(2)}) copy-start(bf16[512,512]{1,0:T(8,128)(2,1)} %param.19) | copy-start | bytes 1572868
  7.2 24.3 %copy-start.39 = (s32[512]{0:T(512)S(1)}, s32[512]{0:T(512)}, u32[]{:S(2)}) copy-start(s32[512]{0:T(512)} %param.24) | copy-start | bytes 6148
  9.9 31.1 %collective-permute-start = (bf16[32,512]{1,0:T(8,128)(2,1)S(1)}, bf16[32,512]{1,0:T(8,128)(2,1)S(1)}, u32[]{:S(2)}, u32[]{:S(2)}) collective-permute-start(bf16[32,512]{1,0:T(8,128)(2,1)S(1)} %broadcast_select_fusion.4), channel_id=1, source_target_pairs={{0,16},{16,32},{32,48},{48,64},{64,80},{80,96},{96,112},{1,17},{17... | collective-permute-start | bytes 98312 | tf_op jit(solution)/shard_map/ppermute | solution.py:12
  16.7 24.4 %collective-permute-start.1 = (bf16[32,512]{1,0:T(8,128)(2,1)S(1)}, bf16[32,512]{1,0:T(8,128)(2,1)S(1)}, u32[]{:S(2)}, u32[]{:S(2)}) collective-permute-start(bf16[32,512]{1,0:T(8,128)(2,1)S(1)} %broadcast_select_fusion.3), channel_id=1, source_target_pairs={{16,0},{32,16},{48,32},{64,48},{80,64},{96,80},{112,96},{17,1},{33... | collective-permute-start | bytes 98312 | tf_op jit(solution)/shard_map/ppermute | solution.py:12
  20.4 20.6 %collective-permute-start.2 = (bf16[32,512]{1,0:T(8,128)(2,1)S(1)}, bf16[32,512]{1,0:T(8,128)(2,1)S(1)}, u32[]{:S(2)}, u32[]{:S(2)}) collective-permute-start(bf16[32,512]{1,0:T(8,128)(2,1)S(1)} %broadcast_select_fusion.2), channel_id=1, source_target_pairs={{0,1},{1,2},{2,3},{3,4},{4,5},{5,6},{6,7},{7,8},{8,9},{9,10},{10,1... | collective-permute-start | bytes 98312 | tf_op jit(solution)/shard_map/ppermute | solution.py:12
  25.5 15.6 %collective-permute-start.3 = (bf16[32,512]{1,0:T(8,128)(2,1)S(1)}, bf16[32,512]{1,0:T(8,128)(2,1)S(1)}, u32[]{:S(2)}, u32[]{:S(2)}) collective-permute-start(bf16[32,512]{1,0:T(8,128)(2,1)S(1)} %broadcast_select_fusion.1), channel_id=1, source_target_pairs={{1,0},{2,1},{3,2},{4,3},{5,4},{6,5},{7,6},{8,7},{9,8},{10,9},{11,1... | collective-permute-start | bytes 98312 | tf_op jit(solution)/shard_map/ppermute | solution.py:12
  51.6 5.5 %copy-start.19 = (bf16[512,512]{1,0:T(8,128)(2,1)S(1)}, bf16[512,512]{1,0:T(8,128)(2,1)}, u32[]{:S(2)}) copy-start(bf16[512,512]{1,0:T(8,128)(2,1)} %param.28) | copy-start | bytes 1572868
  76.2 20.1 %copy-start.30 = (s32[1,1024]{1,0:T(1,128)S(1)}, s32[1,1024]{1,0:T(1,128)}, u32[]{:S(2)}) copy-start(s32[1,1024]{1,0:T(1,128)} %param.25) | copy-start | bytes 12292
  80.8 30.4 %all-to-all-start = ((bf16[128,8,512]{2,1,0:T(8,128)(2,1)}), bf16[128,8,512]{2,1,0:T(8,128)(2,1)S(1)}, u32[]{:S(2)}, u32[]{:S(2)}) async-start(bf16[128,8,512]{2,1,0:T(8,128)(2,1)} %bitcast.5), calls=%async_computation | async-start | bytes 2097152 | tf_op jit(solution)/shard_map/all_to_all | solution.py:46
  111.2 24.4 %all-to-all-start.2 = ((bf16[128,8,512]{2,1,0:T(8,128)(2,1)}), bf16[128,8,512]{2,1,0:T(8,128)(2,1)}, u32[]{:S(2)}, u32[]{:S(2)}) async-start(bf16[128,8,512]{2,1,0:T(8,128)(2,1)} %bitcast.9), calls=%async_computation.2 | async-start | bytes 2097152 | tf_op jit(solution)/shard_map/all_to_all | solution.py:46
  116.9 18.6 %copy-start.41 = (f32[128]{0:T(128)}, f32[128]{0:T(128)S(1)}, u32[]{:S(2)}) copy-start(f32[128]{0:T(128)S(1)} %broadcast_maximum_fusion) | copy-start | bytes 1540
  117.8 19.2 %copy-start.28 = (bf16[128,512]{1,0:T(8,128)(2,1)}, bf16[128,512]{1,0:T(8,128)(2,1)S(1)}, u32[]{:S(2)}) copy-start(bf16[128,512]{1,0:T(8,128)(2,1)S(1)} %fusion.7) | copy-start | bytes 393220
  143.1 5.1 %copy-start.37 = (pred[1024]{0:T(1024)(128)(4,1)S(1)}, pred[1024]{0:T(1024)(128)(4,1)}, u32[]{:S(2)}) copy-start(pred[1024]{0:T(1024)(128)(4,1)} %get-tuple-element.31) | copy-start | bytes 3076
  143.1 5.1 %copy-start.38 = (pred[1024]{0:T(1024)(128)(4,1)S(1)}, pred[1024]{0:T(1024)(128)(4,1)}, u32[]{:S(2)}) copy-start(pred[1024]{0:T(1024)(128)(4,1)} %get-tuple-element.32) | copy-start | bytes 3076
  148.2 7.8 %copy-start.34 = (s32[512]{0:T(512)S(1)}, s32[512]{0:T(512)}, u32[]{:S(2)}) copy-start(s32[512]{0:T(512)} %get-tuple-element.18) | copy-start | bytes 6148
  151.1 26.4 %copy-start.35 = (pred[512]{0:T(512)(128)(4,1)S(1)}, pred[512]{0:T(512)(128)(4,1)}, u32[]{:S(2)}) copy-start(pred[512]{0:T(512)(128)(4,1)} %get-tuple-element.17) | copy-start | bytes 1540
  151.1 23.8 %all-to-all-start.3 = ((bf16[128,8,512]{2,1,0:T(8,128)(2,1)}), bf16[128,8,512]{2,1,0:T(8,128)(2,1)S(1)}, u32[]{:S(2)}, u32[]{:S(2)}) async-start(bf16[128,8,512]{2,1,0:T(8,128)(2,1)} %get-tuple-element.33), calls=%async_computation.3 | async-start | bytes 2097152 | tf_op jit(solution)/shard_map/all_to_all | solution.py:46
  155.9 251.3 %all-reduce.3.cloned.1.call-start = ((), (), s32[]{:S(2)}) async-start(), calls=%async_computation.4 | async-start | bytes 14680064 | tf_op jit(solution)/shard_map/psum | solution.py:152
  182.1 9.2 %copy-start.31 = (pred[2048]{0:T(1024)(128)(4,1)S(1)}, pred[2048]{0:T(1024)(128)(4,1)}, u32[]{:S(2)}) copy-start(pred[2048]{0:T(1024)(128)(4,1)} %get-tuple-element.47) | copy-start | bytes 6148
  182.1 14.4 %copy-start.20 = (bf16[512,512]{1,0:T(8,128)(2,1)S(1)}, bf16[512,512]{1,0:T(8,128)(2,1)}, u32[]{:S(2)}) copy-start(bf16[512,512]{1,0:T(8,128)(2,1)} %param.28) | copy-start | bytes 1572868
  191.3 5.1 %copy-start.2 = (f32[2048,512]{1,0:T(8,128)S(1)}, f32[2048,512]{1,0:T(8,128)}, u32[]{:S(2)}) copy-start(f32[2048,512]{1,0:T(8,128)} %gather_fusion.1) | copy-start | bytes 12582916
  191.3 6.1 %copy-start.3 = (f32[2048,512]{1,0:T(8,128)S(1)}, f32[2048,512]{1,0:T(8,128)}, u32[]{:S(2)}) copy-start(f32[2048,512]{1,0:T(8,128)} %gather_fusion) | copy-start | bytes 12582916
  191.3 6.1 %copy-start.32 = (pred[2048]{0:T(1024)(128)(4,1)S(1)}, pred[2048]{0:T(1024)(128)(4,1)}, u32[]{:S(2)}) copy-start(pred[2048]{0:T(1024)(128)(4,1)} %get-tuple-element.48) | copy-start | bytes 6148
  228.9 10.3 %copy-start.6 = (f32[512,512]{1,0:T(8,128)}, f32[512,512]{1,0:T(8,128)S(1)}, u32[]{:S(2)}) copy-start(f32[512,512]{1,0:T(8,128)S(1)} %scatter_custom_fusion.3) | copy-start | bytes 3145732
  228.9 4.9 %copy-start.23 = (bf16[512,512]{1,0:T(8,128)(2,1)S(1)}, bf16[512,512]{1,0:T(8,128)(2,1)}, u32[]{:S(2)}) copy-start(bf16[512,512]{1,0:T(8,128)(2,1)} %copy-done.22) | copy-start | bytes 1572868
  228.9 4.9 %copy-start.25 = (bf16[512,512]{1,0:T(8,128)(2,1)S(1)}, bf16[512,512]{1,0:T(8,128)(2,1)}, u32[]{:S(2)}) copy-start(bf16[512,512]{1,0:T(8,128)(2,1)} %copy-done.24) | copy-start | bytes 1572868
  229.0 7.0 %copy-start.11 = (bf16[512,512]{1,0:T(8,128)(2,1)S(1)}, bf16[512,512]{1,0:T(8,128)(2,1)}, u32[]{:S(2)}) copy-start(bf16[512,512]{1,0:T(8,128)(2,1)} %gather_fusion.10) | copy-start | bytes 1572868
  229.0 7.0 %copy-start.21 = (bf16[512,512]{1,0:T(8,128)(2,1)S(1)}, bf16[512,512]{1,0:T(8,128)(2,1)}, u32[]{:S(2)}) copy-start(bf16[512,512]{1,0:T(8,128)(2,1)} %param.20) | copy-start | bytes 1572868
  229.0 7.0 %copy-start.36 = (pred[512]{0:T(512)(128)(4,1)S(1)}, pred[512]{0:T(512)(128)(4,1)}, u32[]{:S(2)}) copy-start(pred[512]{0:T(512)(128)(4,1)} %get-tuple-element.17) | copy-start | bytes 1540
  229.0 7.0 %copy-start.43 = (f32[512,512]{1,0:T(8,128)S(1)}, f32[512,512]{1,0:T(8,128)}, u32[]{:S(2)}) copy-start(f32[512,512]{1,0:T(8,128)} %copy-done.42) | copy-start | bytes 3145732
  240.7 4.7 %copy-start.33 = (s32[1,4,32]{2,1,0:T(4,128)S(1)}, s32[1,4,32]{2,1,0:T(4,128)}, u32[]{:S(2)}) copy-start(s32[1,4,32]{2,1,0:T(4,128)} %param.23) | copy-start | bytes 1540
  240.7 27.5 %all-to-all-start.1 = ((bf16[128,8,512]{2,1,0:T(8,128)(2,1)}), bf16[128,8,512]{2,1,0:T(8,128)(2,1)S(1)}, u32[]{:S(2)}, u32[]{:S(2)}) async-start(bf16[128,8,512]{2,1,0:T(8,128)(2,1)} %get-tuple-element.34), calls=%async_computation.1 | async-start | bytes 2097152 | tf_op jit(solution)/shard_map/all_to_all | solution.py:46
  268.2 12.5 %copy-start.12 = (bf16[512,512]{1,0:T(8,128)(2,1)S(1)}, bf16[512,512]{1,0:T(8,128)(2,1)}, u32[]{:S(2)}) copy-start(bf16[512,512]{1,0:T(8,128)(2,1)} %gather_fusion.10) | copy-start | bytes 1572868
  270.2 10.6 %copy-start.7 = (f32[512,512]{1,0:T(8,128)S(1)}, f32[512,512]{1,0:T(8,128)}, u32[]{:S(2)}) copy-start(f32[512,512]{1,0:T(8,128)} %copy-done.6) | copy-start | bytes 3145732
  270.2 10.6 %copy-start.9 = (f32[512,1024]{1,0:T(8,128)S(1)}, f32[512,1024]{1,0:T(8,128)}, u32[]{:S(2)}) copy-start(f32[512,1024]{1,0:T(8,128)} %copy-done.8) | copy-start | bytes 6291460
  270.2 10.6 %copy-start.14 = (bf16[512,512]{1,0:T(8,128)(2,1)S(1)}, bf16[512,512]{1,0:T(8,128)(2,1)}, u32[]{:S(2)}) copy-start(bf16[512,512]{1,0:T(8,128)(2,1)} %param.27) | copy-start | bytes 1572868
  270.2 12.2 %copy-start.27 = (bf16[512,512]{1,0:T(8,128)(2,1)S(1)}, bf16[512,512]{1,0:T(8,128)(2,1)}, u32[]{:S(2)}) copy-start(bf16[512,512]{1,0:T(8,128)(2,1)} %copy-done.26) | copy-start | bytes 1572868
  272.0 11.5 %collective-permute-start.7 = (bf16[32,512]{1,0:T(8,128)(2,1)S(1)}, bf16[32,512]{1,0:T(8,128)(2,1)S(1)}, u32[]{:S(2)}, u32[]{:S(2)}) collective-permute-start(bf16[32,512]{1,0:T(8,128)(2,1)S(1)} %get-tuple-element.28), channel_id=1, source_target_pairs={{0,1},{1,2},{2,3},{3,4},{4,5},{5,6},{6,7},{7,8},{8,9},{9,10},{10,1... | collective-permute-start | bytes 98312 | tf_op jit(solution)/shard_map/ppermute | solution.py:12
  274.4 9.1 %collective-permute-start.6 = (bf16[32,512]{1,0:T(8,128)(2,1)S(1)}, bf16[32,512]{1,0:T(8,128)(2,1)S(1)}, u32[]{:S(2)}, u32[]{:S(2)}) collective-permute-start(bf16[32,512]{1,0:T(8,128)(2,1)S(1)} %get-tuple-element.29), channel_id=1, source_target_pairs={{1,0},{2,1},{3,2},{4,3},{5,4},{6,5},{7,6},{8,7},{9,8},{10,9},{11,1... | collective-permute-start | bytes 98312 | tf_op jit(solution)/shard_map/ppermute | solution.py:12
  275.7 7.8 %collective-permute-start.5 = (bf16[32,512]{1,0:T(8,128)(2,1)S(1)}, bf16[32,512]{1,0:T(8,128)(2,1)S(1)}, u32[]{:S(2)}, u32[]{:S(2)}) collective-permute-start(bf16[32,512]{1,0:T(8,128)(2,1)S(1)} %get-tuple-element.30), channel_id=1, source_target_pairs={{0,16},{16,32},{32,48},{48,64},{64,80},{80,96},{96,112},{1,17},{17... | collective-permute-start | bytes 98312 | tf_op jit(solution)/shard_map/ppermute | solution.py:12
  278.8 5.2 %collective-permute-start.4 = (bf16[32,512]{1,0:T(8,128)(2,1)S(1)}, bf16[32,512]{1,0:T(8,128)(2,1)S(1)}, u32[]{:S(2)}, u32[]{:S(2)}) collective-permute-start(bf16[32,512]{1,0:T(8,128)(2,1)S(1)} %get-tuple-element.27), channel_id=1, source_target_pairs={{16,0},{32,16},{48,32},{64,48},{80,64},{96,80},{112,96},{17,1},{33... | collective-permute-start | bytes 98312 | tf_op jit(solution)/shard_map/ppermute | solution.py:12
  285.8 128.8 %copy-start.18 = (f32[512,512]{1,0:T(8,128)}, f32[512,512]{1,0:T(8,128)S(1)}, u32[]{:S(2)}) copy-start(f32[512,512]{1,0:T(8,128)S(1)} %scatter_custom_fusion.5) | copy-start | bytes 3145732
  407.2 4.8 %copy-start.17 = (f32[512,512]{1,0:T(8,128)S(1)}, f32[512,512]{1,0:T(8,128)}, u32[]{:S(2)}) copy-start(f32[512,512]{1,0:T(8,128)} %get-tuple-element.13) | copy-start | bytes 3145732
  407.2 5.9 %copy-start.13 = (f32[1024,512]{1,0:T(8,128)S(1)}, f32[1024,512]{1,0:T(8,128)}, u32[]{:S(2)}) copy-start(f32[1024,512]{1,0:T(8,128)} %get-tuple-element.14) | copy-start | bytes 6291460
  409.6 5.0 %copy-start.16 = (f32[512,512]{1,0:T(8,128)S(1)}, f32[512,512]{1,0:T(8,128)}, u32[]{:S(2)}) copy-start(f32[512,512]{1,0:T(8,128)} %get-tuple-element.15) | copy-start | bytes 3145732
  412.0 3.7 copy-start.15
  413.1 3.7 copy-start.1
  (9 other events, 12.6 us)
Sparse Core Ops, SparseCore 0:
  240.8 166.3 all-reduce.2
where the time goes:
time: 425 us; the launch traced here: 424 us
  waiting for transfers between devices  192 us (45%)
  other arithmetic  69.8 us (16%)
  local copies, waits for them, and re-layouts  62 us (15%)
  starting transfers between devices  46.9 us (11%)
  matrix products  38 us (9%)
  between operations  14.8 us (3%)
    psum x1, waiting for transfers between devices, local(): lax.psum((source_gradient, target_gradient, edge_gradient, inner_gradient...  121 us
    all_to_all x4, waiting for transfers between devices, trade_slots(): lax.all_to_all(buffer, ('row', 'col'), split_axis=0, concat_axis=0, tiled...  70.4 us
    all_to_all x4, starting transfers between devices, trade_slots(): lax.all_to_all(buffer, ('row', 'col'), split_axis=0, concat_axis=0, tiled...  26.8 us
    ppermute x8, starting transfers between devices, passed_along(): lax.ppermute(value, axis, [(source, source + steps) for source in range(i...  20 us
    scatter-add x1, other arithmetic, local(): jax.ops.segment_sum(jax.nn.silu(message_linear), edge_target, count_rows)  14.6 us
    dot_general x6, matrix products, left_product(): lax.dot_general(first, second, (((0,), (0,)), ((), ())), preferred_elemen...  13.9 us
    scatter-add x1, other arithmetic, local(): jax.ops.segment_sum(grad_edges, edge_target, count_rows)  13.7 us
    scatter-add x1, other arithmetic, local(): jax.ops.segment_sum(grad_edges, edge_source, extended.shape[0])  13.6 us
  transfers between devices with their start and end apart: 13, of which 6 were waited for; matrix products, arithmetic and copies ran while one was open for 9% of the time, Pallas kernels for 0%

commit v1 on v0

v1 whole, which is shorter than its diff:
```python
import math

import jax
import jax.numpy as jnp
from jax import lax
from jax.experimental import pallas as pl
from jax.experimental.pallas import tpu as pltpu
from jax.sharding import PartitionSpec as P

BF = jnp.bfloat16
F32 = jnp.float32
F16 = jnp.float16
LANES = 128
CHUNK = 512
CAPACITY = 8
LOW = 2.0 ** -10
HIGH = 2.0 ** 15


def dot(first, second):
    return jnp.dot(first, second, preferred_element_type=F32)


def left_dot(first, second):
    return lax.dot_general(
        first, second, (((0,), (0,)), ((), ())), preferred_element_type=F32
    )


def right_dot(first, second):
    return lax.dot_general(
        first, second, (((1,), (1,)), ((), ())), preferred_element_type=F32
    )


def iota(shape, axis):
    return lax.broadcasted_iota(jnp.int32, shape, axis)


def column(row):
    square = (LANES, LANES)
    eye = iota(square, 0) == iota(square, 1)
    spread = jnp.broadcast_to(row.astype(F32), square)
    return jnp.sum(jnp.where(eye, spread, 0.0), axis=1, keepdims=True).astype(jnp.int32)


def hot(mask):
    return jnp.where(mask, 1.0, 0.0).astype(BF)


def wide_column(row):
    return jnp.concatenate(
        [column(row[:, k : k + LANES]) for k in range(0, row.shape[1], LANES)], axis=0
    )


def wide_row(ref):
    return jnp.concatenate([ref[k : k + 1, :] for k in range(ref.shape[0])], axis=1)


def gates(value):
    sigma = 0.5 * jnp.tanh(0.5 * value) + 0.5
    active = value * sigma
    return active, sigma + active * (1.0 - sigma)


def halo_kernel(nodes, lists, out):
    picks = hot(column(lists[...]) == iota((LANES, nodes.shape[0]), 1))
    out[...] = dot(picks, nodes[...]).astype(BF)


def prepare_kernel(owner, cotangent, nodes, source_weight, target_weight, slot_out, sent, own_source, target_side):
    rows = nodes.shape[0]
    owner_row = wide_row(owner)
    owner_column = wide_column(owner_row)
    square = (rows, rows)
    before = (owner_column == owner_row) & (iota(square, 0) < iota(square, 1))
    rank = jnp.sum(jnp.where(before, 1.0, 0.0), axis=0, keepdims=True).astype(jnp.int32)
    slot = owner_row * CAPACITY + rank
    slot_out[...] = slot
    place = hot(iota((sent.shape[0], rows), 0) == slot)
    sent[...] = dot(place, cotangent[...]).astype(BF)
    own_source[...] = dot(nodes[...], source_weight[...]).astype(BF)
    target_side[...] = dot(nodes[...], target_weight[...]).astype(BF)


def forward_kernel(
    halo_0, halo_1, halo_2, halo_3, own_source, target_side, nodes, edge_source, edge_target, slot,
    source_weight, edge_weight, inner_weight, outer_weight,
    edge_hidden, edge_slope, message_slope, aggregate, node_hidden, node_slope, refined, sent,
    sides, active, spread,
):
    rows, width = nodes.shape
    extended = rows + LANES
    edges = edge_hidden.shape[0]
    sides[:rows, :] = own_source[...]
    halo = jnp.concatenate([halo_0[...], halo_1[...], halo_2[...], halo_3[...]], axis=0)
    sides[rows:extended, :] = dot(halo, source_weight[...]).astype(BF)
    sides[extended:, :] = target_side[...]
    group = CHUNK // LANES

    def step(turn, carry):
        span = pl.ds(pl.multiple_of(turn * CHUNK, CHUNK), CHUNK)
        picks = []
        for k in range(group):
            at = turn * group + k
            senders = edge_source[pl.ds(at, 1), :]
            receivers = edge_target[pl.ds(at, 1), :]
            place = iota((LANES, extended + rows), 1)
            picks.append(hot((column(senders) == place) | (column(receivers) + extended == place)))
            lanes = pl.ds(pl.multiple_of(at * LANES, LANES), LANES)
            spread[:, lanes] = hot(iota((rows, LANES), 0) == receivers)
        hidden, slope = gates(dot(jnp.concatenate(picks, axis=0), sides[...]))
        hidden = hidden.astype(BF)
        edge_hidden[span, :] = hidden
        edge_slope[span, :] = slope.astype(BF)
        message, slope = gates(dot(hidden, edge_weight[...]))
        active[span, :] = message.astype(BF)
        message_slope[span, :] = slope.astype(BF)
        return carry

    lax.fori_loop(0, edges // CHUNK, step, 0)
    gathered = dot(spread[...], active[...]).astype(BF)
    aggregate[...] = gathered
    linear = dot(nodes[...], inner_weight[:width, :]) + dot(gathered, inner_weight[width:, :])
    hidden, slope = gates(linear)
    hidden = hidden.astype(BF)
    node_hidden[...] = hidden
    node_slope[...] = slope.astype(BF)
    result = (nodes[...].astype(F32) + dot(hidden, outer_weight[...])).astype(BF)
    refined[...] = result
    place = hot(iota((sent.shape[0], rows), 0) == slot[...])
    sent[...] = dot(place, result).astype(BF)


def members_kernel(arrived, table, members, totals, counts):
    coarse = members.shape[0]
    row = wide_row(table)
    inside = iota((coarse, row.shape[1]), 0) == row
    ones = jnp.where(inside, 1.0, 0.0)
    members[...] = ones.astype(BF)
    count = jnp.maximum(jnp.sum(ones, axis=1, keepdims=True), 1.0)
    counts[...] = jnp.broadcast_to(count, counts.shape)
    totals[...] = dot(ones.astype(BF), arrived[...])


def coarse_kernel(arrived, members, totals, counts, table, weight, share_out, update, coarse_out, grad_out):
    count = counts[:, :1]
    coarse = (dot(members[...], arrived[...]) / count).astype(BF)
    coarse_out[...] = coarse
    active, slope = gates(dot(coarse, weight[...]))
    update[...] = active.astype(BF)
    grad = (totals[...] * slope).astype(BF)
    grad_out[...] = grad
    share = (right_dot(grad, weight[...]) / count).astype(BF)
    picks = hot(wide_column(wide_row(table)) == iota((share_out.shape[0], coarse.shape[0]), 1))
    share_out[...] = dot(picks, share).astype(BF)


def coarse_rest_kernel(scale, update, coarse, grad, table, update_out, gradient):
    picks = hot(wide_column(wide_row(table)) == iota((update_out.shape[0], update.shape[0]), 1))
    update_out[...] = dot(picks, update[...]).astype(BF)
    gradient[...] = left_dot(coarse[...], grad[...]) * scale


def node_back_kernel(
    scale, returned, slot, cotangent, nodes, aggregate, node_hidden, node_slope, inner_weight, outer_weight,
    grad_aggregate, base, outer_gradient, inner_gradient,
):
    rows, width = nodes.shape
    picks = hot(wide_column(slot[...]) == iota((rows, returned.shape[0]), 1))
    grad = cotangent[...].astype(F32) + dot(picks, returned[...])
    low = grad.astype(BF)
    hidden = (right_dot(low, outer_weight[...]) * node_slope[...].astype(F32)).astype(BF)
    grad_aggregate[...] = right_dot(hidden, inner_weight[width:, :]).astype(BF)
    base[...] = grad + right_dot(hidden, inner_weight[:width, :])
    outer_gradient[...] = left_dot(node_hidden[...], low) * scale
    inner_gradient[:width, :] = left_dot(nodes[...], hidden) * scale
    inner_gradient[width:, :] = left_dot(aggregate[...], hidden) * scale


def edge_back_kernel(
    edge_source, edge_target, grad_aggregate, edge_slope, message_slope, edge_weight, source_weight,
    grad_message, grad_edges, grad_sources, back,
    spread,
):
    edges, width = edge_slope.shape
    rows = grad_aggregate.shape[0]
    extended = grad_sources.shape[0]
    group = CHUNK // LANES

    def step(turn, carry):
        span = pl.ds(pl.multiple_of(turn * CHUNK, CHUNK), CHUNK)
        picks = []
        for k in range(group):
            at = turn * group + k
            receivers = edge_target[pl.ds(at, 1), :]
            picks.append(hot(column(receivers) == iota((LANES, rows), 1)))
            lanes = pl.ds(pl.multiple_of(at * LANES, LANES), LANES)
            spread[:, lanes] = hot(iota((extended, LANES), 0) == edge_source[pl.ds(at, 1), :])
        taken = dot(jnp.concatenate(picks, axis=0), grad_aggregate[...])
        message = (taken * message_slope[span, :].astype(F32)).astype(BF)
        grad_message[span, :] = message
        grad = right_dot(message, edge_weight[...]) * edge_slope[span, :].astype(F32)
        grad_edges[span, :] = grad.astype(BF)
        return carry

    lax.fori_loop(0, edges // CHUNK, step, 0)
    sums = dot(spread[...], grad_edges[...]).astype(BF)
    grad_sources[...] = sums
    back[...] = right_dot(sums[rows:, :], source_weight[...]).astype(BF)


def weights_kernel(
    scale, edge_target, edge_hidden, grad_message, grad_edges, grad_sources, halo_0, halo_1, halo_2, halo_3,
    nodes, base, source_weight, target_weight,
    source_gradient, target_gradient, edge_gradient, partial,
    spread,
):
    rows, width = nodes.shape
    for k in range(edge_target.shape[0]):
        spread[:, k * LANES : (k + 1) * LANES] = hot(iota((rows, LANES), 0) == edge_target[k : k + 1, :])
    targets = dot(spread[...], grad_edges[...]).astype(BF)
    sources = grad_sources[...]
    halo = jnp.concatenate([halo_0[...], halo_1[...], halo_2[...], halo_3[...]], axis=0)
    edge_gradient[...] = left_dot(edge_hidden[...], grad_message[...]) * scale
    source_gradient[...] = (left_dot(nodes[...], sources[:rows, :]) + left_dot(halo, sources[rows:, :])) * scale
    target_gradient[...] = left_dot(nodes[...], targets) * scale
    partial[...] = base[...] + right_dot(targets, target_weight[...]) + right_dot(sources[:rows, :], source_weight[...])


def node_gradient_kernel(partial, lists, back_0, back_1, back_2, back_3, out):
    back = jnp.concatenate([back_0[...], back_1[...], back_2[...], back_3[...]], axis=0)
    places = hot(iota((partial.shape[0], LANES), 0) == lists[...])
    out[...] = partial[...] + dot(places, back)


def updated_kernel(refined, returned, slot, out):
    picks = hot(wide_column(slot[...]) == iota((refined.shape[0], returned.shape[0]), 1))
    out[...] = (refined[...].astype(F32) + dot(picks, returned[...])).astype(BF)


def call(kernel, outs, *args, scratch=(), **static):
    import functools

    body = functools.partial(kernel, *static.values()) if static else kernel
    return pl.pallas_call(
        body,
        out_shape=[jax.ShapeDtypeStruct(shape, dtype) for shape, dtype in outs],
        scratch_shapes=[pltpu.VMEM(shape, dtype) for shape, dtype in scratch],
        compiler_params=pltpu.CompilerParams(vmem_limit_bytes=60 * 2 ** 20),
        name=kernel.__name__,
    )(*args)


def passed_along(value, axis, steps):
    count = lax.axis_size(axis)
    initial, last = (max(0, -steps), min(count, count - steps))
    return lax.ppermute(value, axis, [(source, source + steps) for source in range(initial, last)])


def trade_halo(blocks, flip):
    moved = []
    for number, offset in enumerate((1, -1)):
        moved.append(passed_along(blocks[number], "row", offset * flip))
    for number, offset in enumerate((1, -1)):
        moved.append(passed_along(blocks[2 + number], "col", offset * flip))
    return moved


def trade_slots(buffer, devices):
    slots, width = buffer.shape
    shaped = buffer.reshape(devices, slots // devices, width)
    moved = lax.all_to_all(shaped, ("row", "col"), split_axis=0, concat_axis=0, tiled=True)
    return moved.reshape(slots, width)


def summed(parts):
    stacked = jnp.concatenate(parts, axis=0)
    narrow = lax.psum(stacked.astype(F16), ("row", "col")).astype(F32)
    sizes = []
    for part in range(stacked.shape[0] // 512):
        block = narrow[part * 512 : (part + 1) * 512]
        sizes.append(jnp.mean(block * block))
    sizes = jnp.stack(sizes)
    fits = jnp.all(sizes > LOW * LOW) & (jnp.max(jnp.abs(narrow)) < HIGH)
    return lax.cond(
        fits,
        lambda narrow, stacked: narrow,
        lambda narrow, stacked: lax.psum(stacked, ("row", "col")),
        narrow,
        stacked,
    )


def local(
    nodes,
    cotangent,
    edge_source,
    edge_target,
    halo_lists,
    pool_owner,
    pool_table,
    source_weight,
    target_weight,
    edge_weight,
    inner_weight,
    outer_weight,
    coarse_weight,
):
    devices = lax.axis_size("row") * lax.axis_size("col")
    rows, width = nodes.shape
    edges = edge_source.shape[0]
    halo_rows = halo_lists.shape[2]
    extended = rows + 4 * halo_rows
    slots = pool_table.shape[1]
    coarse_rows = rows // 4
    scale = 1.0 / math.sqrt(rows * devices)
    lists = halo_lists.reshape(1, 4 * halo_rows)
    owner = pool_owner.reshape(rows // LANES, LANES)
    table = pool_table.reshape(slots // LANES, LANES)
    senders = edge_source.reshape(edges // LANES, LANES)
    receivers = edge_target.reshape(edges // LANES, LANES)
    node_block, edge_block = (rows, width), (edges, width)
    square = ((width, width), F32)

    (halo_sent,) = call(halo_kernel, [((4 * halo_rows, width), BF)], nodes, lists)
    sent_blocks = [halo_sent[k * halo_rows : (k + 1) * halo_rows] for k in range(4)]
    halo = trade_halo(sent_blocks, 1)
    slot, cot_sent, own_source, target_side = call(
        prepare_kernel,
        [((1, rows), jnp.int32), ((slots, width), BF), (node_block, BF), (node_block, BF)],
        owner, cotangent, nodes, source_weight, target_weight,
    )
    cot_arrived = trade_slots(cot_sent, devices)
    edge_hidden, edge_slope, message_slope, aggregate, node_hidden, node_slope, refined, sent = call(
        forward_kernel,
        [(edge_block, BF)] * 3 + [(node_block, BF)] * 4 + [((slots, width), BF)],
        *halo, own_source, target_side, nodes, senders, receivers, slot,
        source_weight, edge_weight, inner_weight, outer_weight,
        scratch=[((extended + rows, width), BF), (edge_block, BF), ((rows, edges), BF)],
    )
    arrived = trade_slots(sent, devices)
    members, totals, counts = call(
        members_kernel,
        [((coarse_rows, slots), BF), ((coarse_rows, width), F32), ((coarse_rows, LANES), F32)],
        cot_arrived, table,
    )
    share_sent, update, coarse, grad_coarse = call(
        coarse_kernel,
        [((slots, width), BF)] + [((coarse_rows, width), BF)] * 3,
        arrived, members, totals, counts, table, coarse_weight,
    )
    share_returned = trade_slots(share_sent, devices)
    update_sent, coarse_gradient = call(
        coarse_rest_kernel, [((slots, width), BF), square], update, coarse, grad_coarse, table, scale=scale
    )
    update_sent, share_returned = lax.optimization_barrier((update_sent, share_returned))
    update_returned = trade_slots(update_sent, devices)
    grad_aggregate, base, outer_gradient, inner_gradient = call(
        node_back_kernel,
        [(node_block, BF), (node_block, F32), square, ((2 * width, width), F32)],
        share_returned, slot, cotangent, nodes, aggregate, node_hidden, node_slope, inner_weight, outer_weight,
        scale=scale,
    )
    grad_message, grad_edges, grad_sources, back = call(
        edge_back_kernel,
        [(edge_block, BF), (edge_block, BF), ((extended, width), BF), ((4 * halo_rows, width), BF)],
        senders, receivers, grad_aggregate, edge_slope, message_slope, edge_weight, source_weight,
        scratch=[((extended, edges), BF)],
    )
    returned = trade_halo([back[k * halo_rows : (k + 1) * halo_rows] for k in range(4)], -1)
    source_gradient, target_gradient, edge_gradient, partial = call(
        weights_kernel,
        [square, square, square, (node_block, F32)],
        receivers, edge_hidden, grad_message, grad_edges, grad_sources, *halo,
        nodes, base, source_weight, target_weight,
        scratch=[((rows, edges), BF)],
        scale=scale,
    )
    (node_gradient,) = call(node_gradient_kernel, [(node_block, F32)], partial, lists, *returned)
    parts = [source_gradient, target_gradient, edge_gradient, inner_gradient, outer_gradient, coarse_gradient]
    sums = summed(parts)
    (updated,) = call(updated_kernel, [(node_block, BF)], refined, update_returned, slot)
    results, at = [], 0
    for part in parts:
        results.append(sums[at : at + part.shape[0]])
        at += part.shape[0]
    return (updated, node_gradient, *results)


def solution(mesh):
    in_specs = (
        P(("row", "col"), None),
        P(("row", "col"), None),
        P(("row", "col")),
        P(("row", "col")),
        P(("row", "col"), None, None),
        P(("row", "col")),
        P(("row", "col"), None),
        P(),
        P(),
        P(),
        P(),
        P(),
        P(),
    )
    out_specs = (P(("row", "col"), None), P(("row", "col"), None), P(), P(), P(), P(), P(), P())
    return jax.shard_map(local, mesh=mesh, in_specs=in_specs, out_specs=out_specs, check_vma=False)
```

time: 425 us -> 319 us (0.75)
  waiting for transfers between devices: 192 us -> 33.4 us
  blocking collectives: 0 us -> 107 us
  other arithmetic: 69.8 us -> 10.7 us
  Pallas kernels: 0 us -> 58.5 us
  matrix products: 38 us -> 0 us
  local copies, waits for them, and re-layouts: 62 us -> 31.5 us
  starting transfers between devices: 46.9 us -> 55 us
  between operations: 14.8 us -> 20.2 us
    psum x1 -> x0, waiting for transfers between devices: 121 us -> none  [local(): lax.psum((source_gradient, target_gradient, edge_gradient, inner_gradient...]
    psum x0 -> x1, blocking collectives: none -> 107 us  [summed(): narrow = lax.psum(stacked.astype(F16), ('row', 'col')).astype(F32)]
    pallas_call x0 -> x11, Pallas kernels: none -> 58.5 us  [call(): pl.pallas_call(body, out_shape=[jax.ShapeDtypeStruct(shape, dtype) for sh...]
    gather x11 -> x0, local copies, waits for them, and re-layouts: 47.6 us -> none  [the longest x1 9.21 us: local(): jnp.take(grad_aggregate, edge_target, axis=0) * silu_slope(message_linear)]
    scatter-add x4 -> x0, other arithmetic: 43.6 us -> none  [the longest x1 14.6 us: local(): jax.ops.segment_sum(jax.nn.silu(message_linear), edge_target, count_rows)]
    all_to_all x4, waiting for transfers between devices: 70.4 us -> 32.4 us  [trade_slots(): lax.all_to_all(shaped, ('row', 'col'), split_axis=0, concat_axis=0, tiled...]
    dot_general x21 -> x0, matrix products: 38 us -> none  [the longest x6 13.9 us: left_product(): lax.dot_general(first, second, (((0,), (0,)), ((), ())), preferred_elemen...]
    mul x6 -> x0, other arithmetic: 9.57 us -> none  [the longest x1 2.44 us: local(): source_gradient * scale]
  transfers between devices with their start and end apart: 13 -> 12, of which waited for: 6 -> 4; matrix products, arithmetic and copies ran while one was open for 9% -> 10% of each run, Pallas kernels for 0% -> 15%
where the time goes in v1:
time: 319 us; the launch traced here: 316 us
  blocking collectives  107 us (34%)
  Pallas kernels  58.5 us (18%)
  starting transfers between devices  55 us (17%)
  waiting for transfers between devices  33.4 us (10%)
  local copies, waits for them, and re-layouts  31.5 us (10%)
  between operations  20.2 us (6%)
  other arithmetic  10.7 us (3%)
    psum x1, blocking collectives, summed(): narrow = lax.psum(stacked.astype(F16), ('row', 'col')).astype(F32)  107 us
    pallas_call x11, Pallas kernels, call(): pl.pallas_call(body, out_shape=[jax.ShapeDtypeStruct(shape, dtype) for sh...  58.5 us
    all_to_all x4, starting transfers between devices, trade_slots(): lax.all_to_all(shaped, ('row', 'col'), split_axis=0, concat_axis=0, tiled...  33.1 us
    all_to_all x4, waiting for transfers between devices, trade_slots(): lax.all_to_all(shaped, ('row', 'col'), split_axis=0, concat_axis=0, tiled...  32.4 us
    ppermute x8, starting transfers between devices, passed_along(): lax.ppermute(value, axis, [(source, source + steps) for source in range(i...  21.9 us
    unnamed x39, local copies, waits for them, and re-layouts  13.6 us
    slice x2, local copies, waits for them, and re-layouts, local(): results.append(sums[at:at + part.shape[0]])  7.99 us
    cond x1, local copies, waits for them, and re-layouts  6.87 us
  transfers between devices with their start and end apart: 12, of which 4 were waited for; matrix products, arithmetic and copies ran while one was open for 10% of the time, Pallas kernels for 15%

profile of v1, /device:TPU:1, one launch (start us, length us, event | category | flops | bytes accessed | tf_op | source)
XLA Modules:
  0.0 316.5 jit_solution(14376345870932056986)
XLA Ops:
  7.2 3.8 %prepare_kernel.1 = (s32[1,512]{1,0:T(1,128)}, bf16[1024,512]{1,0:T(8,128)(2,1)}, bf16[512,512]{1,0:T(8,128)(2,1)}, bf16[512,512]{1,0:T(8,128)(2,1)}) custom-call(s32[4,128]{1,0:T(4,128)} %bitcast.40, bf16[512,512]{1,0:T(8,128)(2,1)} %cotangent.3, bf16[512,512]{1,0:T(8,128)(2,1)} %nodes.9, bf16[512,512]{1,0:T(8,128)(2,1)} %source_weight.7, ...), custom_call_target="tpu_custom_call" | custom-call | tf_op jit(solution)/shard_map/prepare_kernel/pallas_call | solution.py:247
  10.9 11.5 %all-to-all-start.1 = ((bf16[128,8,512]{2,1,0:T(8,128)(2,1)}), bf16[128,8,512]{2,1,0:T(8,128)(2,1)S(1)}, u32[]{:S(2)}, u32[]{:S(2)}) async-start(bf16[128,8,512]{2,1,0:T(8,128)(2,1)} %bitcast.29), calls=%async_computation.1 | async-start | bytes 2097152 | tf_op jit(solution)/shard_map/all_to_all | solution.py:274
  22.4 1.3 reshape.55.lists
  23.8 2.0 halo_kernel.1
  25.8 0.8 fusion.9
  26.6 1.3 collective-permute-start.3
  27.9 4.0 %collective-permute-start.2 = (bf16[32,512]{1,0:T(8,128)(2,1)S(1)}, bf16[32,512]{1,0:T(8,128)(2,1)S(1)}, u32[]{:S(2)}, u32[]{:S(2)}) collective-permute-start(bf16[32,512]{1,0:T(8,128)(2,1)S(1)} %get-tuple-element.116), channel_id=1, source_target_pairs={{0,1},{1,2},{2,3},{3,4},{4,5},{5,6},{6,7},{7,8},{8,9},{9,10},{10,1... | collective-permute-start | bytes 98312 | tf_op jit(solution)/shard_map/ppermute | solution.py:259
  31.9 3.5 %collective-permute-start.1 = (bf16[32,512]{1,0:T(8,128)(2,1)S(1)}, bf16[32,512]{1,0:T(8,128)(2,1)S(1)}, u32[]{:S(2)}, u32[]{:S(2)}) collective-permute-start(bf16[32,512]{1,0:T(8,128)(2,1)S(1)} %get-tuple-element.117), channel_id=1, source_target_pairs={{16,0},{32,16},{48,32},{64,48},{80,64},{96,80},{112,96},{17,1},{33... | collective-permute-start | bytes 98312 | tf_op jit(solution)/shard_map/ppermute | solution.py:259
  35.4 2.6 collective-permute-start
  38.2 0.8 collective-permute-done.halo_0
  39.0 0.6 copy-done.12
  39.6 13.6 %forward_kernel.1 = (bf16[2048,512]{1,0:T(8,128)(2,1)}, bf16[2048,512]{1,0:T(8,128)(2,1)}, bf16[2048,512]{1,0:T(8,128)(2,1)}, bf16[512,512]{1,0:T(8,128)(2,1)}, ...) custom-call(bf16[32,512]{1,0:T(8,128)(2,1)} %copy-done.12, ...), custom_call_target="tpu_custom_call" | custom-call | tf_op jit(solution)/shard_map/forward_kernel/pallas_call | solution.py:247
  53.3 12.2 %all-to-all-start = ((bf16[128,8,512]{2,1,0:T(8,128)(2,1)}), bf16[128,8,512]{2,1,0:T(8,128)(2,1)S(1)}, u32[]{:S(2)}, u32[]{:S(2)}) async-start(bf16[128,8,512]{2,1,0:T(8,128)(2,1)} %bitcast.30), calls=%async_computation | async-start | bytes 2097152 | tf_op jit(solution)/shard_map/all_to_all | solution.py:274
  65.5 2.3 members_kernel.1
  67.8 16.5 %all-to-all-done = bf16[128,8,512]{2,1,0:T(8,128)(2,1)S(1)} async-done(((bf16[128,8,512]{2,1,0:T(8,128)(2,1)}), bf16[128,8,512]{2,1,0:T(8,128)(2,1)S(1)}, u32[]{:S(2)}, u32[]{:S(2)}) %all-to-all-start) | async-done | bytes 1048608 | tf_op jit(solution)/shard_map/all_to_all | solution.py:274
  84.3 1.0 copy-done.5
  85.3 3.7 %coarse_kernel.1 = (bf16[1024,512]{1,0:T(8,128)(2,1)}, bf16[128,512]{1,0:T(8,128)(2,1)}, bf16[128,512]{1,0:T(8,128)(2,1)}, bf16[128,512]{1,0:T(8,128)(2,1)}) custom-call(bf16[1024,512]{1,0:T(8,128)(2,1)} %bitcast.27, bf16[128,1024]{1,0:T(8,128)(2,1)} %get-tuple-element.70.members, f32[128,512]{1,0:T(8,128)} %get-tuple-element.71.totals, ...), custom_call_target="tpu_custom_call" | custom-call | tf_op jit(solution)/shard_map/coarse_kernel/pallas_call | solution.py:247
  89.0 4.7 %all-to-all-start.2 = ((bf16[128,8,512]{2,1,0:T(8,128)(2,1)}), bf16[128,8,512]{2,1,0:T(8,128)(2,1)S(1)}, u32[]{:S(2)}, u32[]{:S(2)}) async-start(bf16[128,8,512]{2,1,0:T(8,128)(2,1)} %bitcast.31), calls=%async_computation.2 | async-start | bytes 2097152 | tf_op jit(solution)/shard_map/all_to_all | solution.py:274
  93.7 3.1 coarse_rest_kernel.1
  96.8 15.8 %all-to-all-done.2 = bf16[128,8,512]{2,1,0:T(8,128)(2,1)S(1)} async-done(((bf16[128,8,512]{2,1,0:T(8,128)(2,1)}), bf16[128,8,512]{2,1,0:T(8,128)(2,1)S(1)}, u32[]{:S(2)}, u32[]{:S(2)}) %all-to-all-start.2) | async-done | bytes 1048608 | tf_op jit(solution)/shard_map/all_to_all | solution.py:274
  112.6 4.7 %all-to-all-start.3 = ((bf16[128,8,512]{2,1,0:T(8,128)(2,1)}), bf16[128,8,512]{2,1,0:T(8,128)(2,1)S(1)}, u32[]{:S(2)}, u32[]{:S(2)}) async-start(bf16[128,8,512]{2,1,0:T(8,128)(2,1)} %bitcast.28), calls=%async_computation.3 | async-start | bytes 2097152 | tf_op jit(solution)/shard_map/all_to_all | solution.py:274
  117.4 6.4 %node_back_kernel.1 = (bf16[512,512]{1,0:T(8,128)(2,1)}, f32[512,512]{1,0:T(8,128)}, f32[512,512]{1,0:T(8,128)}, f32[1024,512]{1,0:T(8,128)}) custom-call(bf16[1024,512]{1,0:T(8,128)(2,1)} %bitcast.24, s32[1,512]{1,0:T(1,128)} %get-tuple-element.66.slot, bf16[512,512]{1,0:T(8,128)(2,1)} %cotangent.3, bf16[512,512]{1,0:T(8,128)(2,1)} %nodes.9, ...), custom_call_target="tpu_custom_call" | custom-call | tf_op jit(solution)/shard_map/node_back_kernel/pallas_call | solution.py:247
  123.8 9.4 %edge_back_kernel.1 = (bf16[2048,512]{1,0:T(8,128)(2,1)}, bf16[2048,512]{1,0:T(8,128)(2,1)}, bf16[640,512]{1,0:T(8,128)(2,1)}, bf16[128,512]{1,0:T(8,128)(2,1)}) custom-call(s32[16,128]{1,0:T(8,128)} %bitcast.39, s32[16,128]{1,0:T(8,128)} %bitcast.33, bf16[512,512]{1,0:T(8,128)(2,1)} %get-tuple-element.84.grad_aggregate, ...), custom_call_target="tpu_custom_call" | custom-call | tf_op jit(solution)/shard_map/edge_back_kernel/pallas_call | solution.py:247
  133.2 0.8 fusion.8
  134.0 3.3 %collective-permute-start.7 = (bf16[32,512]{1,0:T(8,128)(2,1)S(1)}, bf16[32,512]{1,0:T(8,128)(2,1)S(1)}, u32[]{:S(2)}, u32[]{:S(2)}) collective-permute-start(bf16[32,512]{1,0:T(8,128)(2,1)S(1)} %get-tuple-element.111), channel_id=1, source_target_pairs={{0,1},{1,2},{2,3},{3,4},{4,5},{5,6},{6,7},{7,8},{8,9},{9,10},{10,1... | collective-permute-start | bytes 98312 | tf_op jit(solution)/shard_map/ppermute | solution.py:259
  137.4 1.3 collective-permute-start.6
  138.7 3.9 %collective-permute-start.5 = (bf16[32,512]{1,0:T(8,128)(2,1)S(1)}, bf16[32,512]{1,0:T(8,128)(2,1)S(1)}, u32[]{:S(2)}, u32[]{:S(2)}) collective-permute-start(bf16[32,512]{1,0:T(8,128)(2,1)S(1)} %get-tuple-element.113), channel_id=1, source_target_pairs={{0,16},{16,32},{32,48},{48,64},{64,80},{80,96},{96,112},{1,17},{17... | collective-permute-start | bytes 98312 | tf_op jit(solution)/shard_map/ppermute | solution.py:259
  142.6 1.9 collective-permute-start.4
  144.5 8.6 %weights_kernel.1 = (f32[512,512]{1,0:T(8,128)}, f32[512,512]{1,0:T(8,128)}, f32[512,512]{1,0:T(8,128)}, f32[512,512]{1,0:T(8,128)}) custom-call(s32[16,128]{1,0:T(8,128)} %bitcast.34, bf16[2048,512]{1,0:T(8,128)(2,1)} %get-tuple-element.79.edge_hidden, bf16[2048,512]{1,0:T(8,128)(2,1)} %get-tuple-element.87.grad_message, ...), custom_call_target="tpu_custom_call" | custom-call | tf_op jit(solution)/shard_map/weights_kernel/pallas_call | solution.py:247
  153.1 1.4 constant_dynamic-update-slice_fusion.5
  154.5 1.4 constant_dynamic-update-slice_fusion.4
  155.9 1.3 constant_dynamic-update-slice_fusion.3
  157.6 3.0 copy-done.1
  160.6 2.6 convert_element_type.12
  163.1 106.9 %all-reduce.4 = u32[4,229376]{1,0:T(4,128)} all-reduce(u32[4,229376]{1,0:T(4,128)} %bitcast.23), channel_id=1, replica_groups=mesh['row'=8,'col'=16] {'row','col'}, use_global_device_ids=true, to_apply=%region_0.0.clone | all-reduce | flops 917504 | bytes 7340032 | tf_op jit(solution)/shard_map/psum | solution.py:280
  270.1 3.1 convert_element_type.13
  273.2 3.0 copy-done
  276.2 1.3 fusion
  282.0 3.1 abs_reduce_fusion
  285.9 0.6 compare_reduce_fusion
  287.2 7.1 %conditional.1 = (f32[3584,512]{1,0:T(8,128)}) conditional(s32[]{:T(128)} %convert_element_type.14, f32[3584,512]{1,0:T(8,128)} %copy-done.1, f32[3584,512]{1,0:T(8,128)} %copy-done), branch_computations={%region_10.0_spmd, %region_12.0_spmd} | conditional | flops 1835008 | bytes 44040240 | solution.py:287
  287.4 6.9 %copy.29 = f32[3584,512]{1,0:T(8,128)} copy(f32[3584,512]{1,0:T(8,128)} %param.1) | data formatting | bytes 14680064 | tf_op jit(solution)/shard_map/cond
  294.3 4.9 %fusion.7 = (f32[512,512]{1,0:T(8,128)}, f32[512,512]{1,0:T(8,128)}, f32[512,512]{1,0:T(8,128)}, f32[512,512]{1,0:T(8,128)}, f32[512,512]{1,0:T(8,128)}) fusion(f32[3584,512]{1,0:T(8,128)} %get-tuple-element.119), kind=kLoop, calls=%fused_computation.22 | loop fusion | bytes 10485760 | tf_op jit(solution)/shard_map/slice | solution.py:387
  299.2 3.1 slice.134
  302.4 0.5 copy-done.13
  303.0 2.5 node_gradient_kernel.1
  305.5 1.0 copy-done.3
  306.5 3.2 updated_kernel.1
  (41 shorter events, 0.7 us)
Async XLA Ops:
  10.9 42.3 %all-to-all-start.1 = ((bf16[128,8,512]{2,1,0:T(8,128)(2,1)}), bf16[128,8,512]{2,1,0:T(8,128)(2,1)S(1)}, u32[]{:S(2)}, u32[]{:S(2)}) async-start(bf16[128,8,512]{2,1,0:T(8,128)(2,1)} %bitcast.29), calls=%async_computation.1 | async-start | bytes 2097152 | tf_op jit(solution)/shard_map/all_to_all | solution.py:274
  26.6 11.5 %collective-permute-start.3 = (bf16[32,512]{1,0:T(8,128)(2,1)S(1)}, bf16[32,512]{1,0:T(8,128)(2,1)S(1)}, u32[]{:S(2)}, u32[]{:S(2)}) collective-permute-start(bf16[32,512]{1,0:T(8,128)(2,1)S(1)} %get-tuple-element.115), channel_id=1, source_target_pairs={{1,0},{2,1},{3,2},{4,3},{5,4},{6,5},{7,6},{8,7},{9,8},{10,9},{11,1... | collective-permute-start | bytes 98312 | tf_op jit(solution)/shard_map/ppermute | solution.py:259
  27.9 10.2 %collective-permute-start.2 = (bf16[32,512]{1,0:T(8,128)(2,1)S(1)}, bf16[32,512]{1,0:T(8,128)(2,1)S(1)}, u32[]{:S(2)}, u32[]{:S(2)}) collective-permute-start(bf16[32,512]{1,0:T(8,128)(2,1)S(1)} %get-tuple-element.116), channel_id=1, source_target_pairs={{0,1},{1,2},{2,3},{3,4},{4,5},{5,6},{6,7},{7,8},{8,9},{9,10},{10,1... | collective-permute-start | bytes 98312 | tf_op jit(solution)/shard_map/ppermute | solution.py:259
  31.9 6.4 %collective-permute-start.1 = (bf16[32,512]{1,0:T(8,128)(2,1)S(1)}, bf16[32,512]{1,0:T(8,128)(2,1)S(1)}, u32[]{:S(2)}, u32[]{:S(2)}) collective-permute-start(bf16[32,512]{1,0:T(8,128)(2,1)S(1)} %get-tuple-element.117), channel_id=1, source_target_pairs={{16,0},{32,16},{48,32},{64,48},{80,64},{96,80},{112,96},{17,1},{33... | collective-permute-start | bytes 98312 | tf_op jit(solution)/shard_map/ppermute | solution.py:259
  35.4 3.6 %collective-permute-start = (bf16[32,512]{1,0:T(8,128)(2,1)S(1)}, bf16[32,512]{1,0:T(8,128)(2,1)S(1)}, u32[]{:S(2)}, u32[]{:S(2)}) collective-permute-start(bf16[32,512]{1,0:T(8,128)(2,1)S(1)} %get-tuple-element.118), channel_id=1, source_target_pairs={{0,16},{16,32},{32,48},{48,64},{64,80},{80,96},{96,112},{1,17},{17... | collective-permute-start | bytes 98312 | tf_op jit(solution)/shard_map/ppermute | solution.py:259
  38.0 1.0 copy-start.9
  38.1 1.0 copy-start.10
  38.2 0.8 copy-start.11
  39.0 0.6 copy-start.12
  53.3 12.2 %copy-start.4 = (bf16[128,8,512]{2,1,0:T(8,128)(2,1)}, bf16[128,8,512]{2,1,0:T(8,128)(2,1)S(1)}, u32[]{:S(2)}) copy-start(bf16[128,8,512]{2,1,0:T(8,128)(2,1)S(1)} %all-to-all-done.1) | copy-start | bytes 3145732
  53.3 31.1 %all-to-all-start = ((bf16[128,8,512]{2,1,0:T(8,128)(2,1)}), bf16[128,8,512]{2,1,0:T(8,128)(2,1)S(1)}, u32[]{:S(2)}, u32[]{:S(2)}) async-start(bf16[128,8,512]{2,1,0:T(8,128)(2,1)} %bitcast.30), calls=%async_computation | async-start | bytes 2097152 | tf_op jit(solution)/shard_map/all_to_all | solution.py:274
  84.3 1.0 copy-start.5
  89.0 23.7 %all-to-all-start.2 = ((bf16[128,8,512]{2,1,0:T(8,128)(2,1)}), bf16[128,8,512]{2,1,0:T(8,128)(2,1)S(1)}, u32[]{:S(2)}, u32[]{:S(2)}) async-start(bf16[128,8,512]{2,1,0:T(8,128)(2,1)} %bitcast.31), calls=%async_computation.2 | async-start | bytes 2097152 | tf_op jit(solution)/shard_map/all_to_all | solution.py:274
  112.6 4.7 %copy-start.2 = (bf16[128,8,512]{2,1,0:T(8,128)(2,1)}, bf16[128,8,512]{2,1,0:T(8,128)(2,1)S(1)}, u32[]{:S(2)}) copy-start(bf16[128,8,512]{2,1,0:T(8,128)(2,1)S(1)} %all-to-all-done.2) | copy-start | bytes 3145732
  112.6 192.8 %all-to-all-start.3 = ((bf16[128,8,512]{2,1,0:T(8,128)(2,1)}), bf16[128,8,512]{2,1,0:T(8,128)(2,1)S(1)}, u32[]{:S(2)}, u32[]{:S(2)}) async-start(bf16[128,8,512]{2,1,0:T(8,128)(2,1)} %bitcast.28), calls=%async_computation.3 | async-start | bytes 2097152 | tf_op jit(solution)/shard_map/all_to_all | solution.py:274
  134.0 168.3 %collective-permute-start.7 = (bf16[32,512]{1,0:T(8,128)(2,1)S(1)}, bf16[32,512]{1,0:T(8,128)(2,1)S(1)}, u32[]{:S(2)}, u32[]{:S(2)}) collective-permute-start(bf16[32,512]{1,0:T(8,128)(2,1)S(1)} %get-tuple-element.111), channel_id=1, source_target_pairs={{0,1},{1,2},{2,3},{3,4},{4,5},{5,6},{6,7},{7,8},{8,9},{9,10},{10,1... | collective-permute-start | bytes 98312 | tf_op jit(solution)/shard_map/ppermute | solution.py:259
  137.4 164.9 %collective-permute-start.6 = (bf16[32,512]{1,0:T(8,128)(2,1)S(1)}, bf16[32,512]{1,0:T(8,128)(2,1)S(1)}, u32[]{:S(2)}, u32[]{:S(2)}) collective-permute-start(bf16[32,512]{1,0:T(8,128)(2,1)S(1)} %get-tuple-element.112), channel_id=1, source_target_pairs={{1,0},{2,1},{3,2},{4,3},{5,4},{6,5},{7,6},{8,7},{9,8},{10,9},{11,1... | collective-permute-start | bytes 98312 | tf_op jit(solution)/shard_map/ppermute | solution.py:259
  138.7 163.7 %collective-permute-start.5 = (bf16[32,512]{1,0:T(8,128)(2,1)S(1)}, bf16[32,512]{1,0:T(8,128)(2,1)S(1)}, u32[]{:S(2)}, u32[]{:S(2)}) collective-permute-start(bf16[32,512]{1,0:T(8,128)(2,1)S(1)} %get-tuple-element.113), channel_id=1, source_target_pairs={{0,16},{16,32},{32,48},{48,64},{64,80},{80,96},{96,112},{1,17},{17... | collective-permute-start | bytes 98312 | tf_op jit(solution)/shard_map/ppermute | solution.py:259
  142.6 159.8 %collective-permute-start.4 = (bf16[32,512]{1,0:T(8,128)(2,1)S(1)}, bf16[32,512]{1,0:T(8,128)(2,1)S(1)}, u32[]{:S(2)}, u32[]{:S(2)}) collective-permute-start(bf16[32,512]{1,0:T(8,128)(2,1)S(1)} %get-tuple-element.114), channel_id=1, source_target_pairs={{16,0},{32,16},{48,32},{64,48},{80,64},{96,80},{112,96},{17,1},{33... | collective-permute-start | bytes 98312 | tf_op jit(solution)/shard_map/ppermute | solution.py:259
  153.1 4.2 %copy-start.6 = (f32[1024,512]{1,0:T(8,128)S(1)}, f32[1024,512]{1,0:T(8,128)}, u32[]{:S(2)}) copy-start(f32[1024,512]{1,0:T(8,128)} %get-tuple-element.96) | copy-start | bytes 6291460
  153.1 4.4 %copy-start.8 = (f32[512,512]{1,0:T(8,128)S(1)}, f32[512,512]{1,0:T(8,128)}, u32[]{:S(2)}) copy-start(f32[512,512]{1,0:T(8,128)} %get-tuple-element.97) | copy-start | bytes 3145732
  153.1 4.4 %copy-start.7 = (f32[512,512]{1,0:T(8,128)S(1)}, f32[512,512]{1,0:T(8,128)}, u32[]{:S(2)}) copy-start(f32[512,512]{1,0:T(8,128)} %get-tuple-element.98) | copy-start | bytes 3145732
  157.6 3.0 copy-start.1
  273.2 3.0 copy-start
  302.3 0.6 copy-start.13
  302.3 0.6 copy-start.14
  302.3 0.6 copy-start.15
  302.3 0.6 copy-start.16
  305.5 1.0 copy-start.3

commit v2 on v1

--- a/solution.py
+++ b/solution.py
@@ -1,3 +1,4 @@
+import functools
 import math
 
 import jax
@@ -5,16 +6,18 @@
 from jax import lax
 from jax.experimental import pallas as pl
 from jax.experimental.pallas import tpu as pltpu
+from jax.sharding import Mesh
 from jax.sharding import PartitionSpec as P
 
 BF = jnp.bfloat16
 F32 = jnp.float32
-F16 = jnp.float16
 LANES = 128
 CHUNK = 512
 CAPACITY = 8
-LOW = 2.0 ** -10
-HIGH = 2.0 ** 15
+ROW = ("z", "core")
+COL = ("x", "y")
+CHIPS = ("z", "x", "y")
+ALL = ROW + COL
 
 
 def dot(first, second):
@@ -157,15 +160,36 @@
     share_out[...] = dot(picks, share).astype(BF)
 
 
-def coarse_rest_kernel(scale, update, coarse, grad, table, update_out, gradient):
+def coarse_rest_kernel(update, table, update_out):
     picks = hot(wide_column(wide_row(table)) == iota((update_out.shape[0], update.shape[0]), 1))
     update_out[...] = dot(picks, update[...]).astype(BF)
-    gradient[...] = left_dot(coarse[...], grad[...]) * scale
+
+
+def half_of(ref, half):
+    columns = ref.shape[1] // 2
+    return ref[:, pl.ds(pl.multiple_of(half * columns, columns), columns)]
+
+
+def pack(out, at, value):
+    rows, width = value.shape
+    for k in range(width // LANES):
+        out[at * width // LANES + k * rows : at * width // LANES + (k + 1) * rows, :] = value[
+            :, k * LANES : (k + 1) * LANES
+        ].astype(BF)
+
+
+def halves(scale, core, keep, give, pairs):
+    at = 0
+    for first, second in pairs:
+        for out, half in ((keep, core[0]), (give, 1 - core[0])):
+            pack(out, at, left_dot(half_of(first, half), second) * scale)
+        at += first.shape[1] // 2
 
 
 def node_back_kernel(
-    scale, returned, slot, cotangent, nodes, aggregate, node_hidden, node_slope, inner_weight, outer_weight,
-    grad_aggregate, base, outer_gradient, inner_gradient,
+    scale, core, returned, slot, cotangent, nodes, aggregate, node_hidden, node_slope, coarse, grad_coarse,
+    inner_weight, outer_weight,
+    grad_aggregate, base, keep, give,
 ):
     rows, width = nodes.shape
     picks = hot(wide_column(slot[...]) == iota((rows, returned.shape[0]), 1))
@@ -174,9 +198,8 @@
     hidden = (right_dot(low, outer_weight[...]) * node_slope[...].astype(F32)).astype(BF)
     grad_aggregate[...] = right_dot(hidden, inner_weight[width:, :]).astype(BF)
     base[...] = grad + right_dot(hidden, inner_weight[:width, :])
-    outer_gradient[...] = left_dot(node_hidden[...], low) * scale
-    inner_gradient[:width, :] = left_dot(nodes[...], hidden) * scale
-    inner_gradient[width:, :] = left_dot(aggregate[...], hidden) * scale
+    pairs = ((node_hidden, low), (nodes, hidden), (aggregate, hidden), (coarse, grad_coarse[...]))
+    halves(scale, core, keep, give, pairs)
 
 
 def edge_back_kernel(
@@ -212,20 +235,20 @@
 
 
 def weights_kernel(
-    scale, edge_target, edge_hidden, grad_message, grad_edges, grad_sources, halo_0, halo_1, halo_2, halo_3,
+    scale, core, edge_target, edge_hidden, grad_message, grad_edges, grad_sources, halo_0, halo_1, halo_2, halo_3,
     nodes, base, source_weight, target_weight,
-    source_gradient, target_gradient, edge_gradient, partial,
-    spread,
+    keep, give, partial,
+    spread, extended,
 ):
     rows, width = nodes.shape
     for k in range(edge_target.shape[0]):
         spread[:, k * LANES : (k + 1) * LANES] = hot(iota((rows, LANES), 0) == edge_target[k : k + 1, :])
     targets = dot(spread[...], grad_edges[...]).astype(BF)
     sources = grad_sources[...]
-    halo = jnp.concatenate([halo_0[...], halo_1[...], halo_2[...], halo_3[...]], axis=0)
-    edge_gradient[...] = left_dot(edge_hidden[...], grad_message[...]) * scale
-    source_gradient[...] = (left_dot(nodes[...], sources[:rows, :]) + left_dot(halo, sources[rows:, :])) * scale
-    target_gradient[...] = left_dot(nodes[...], targets) * scale
+    extended[:rows, :] = nodes[...]
+    extended[rows:, :] = jnp.concatenate([halo_0[...], halo_1[...], halo_2[...], halo_3[...]], axis=0)
+    pairs = ((edge_hidden, grad_message[...]), (extended, sources), (nodes, targets))
+    halves(scale, core, keep, give, pairs)
     partial[...] = base[...] + right_dot(targets, target_weight[...]) + right_dot(sources[:rows, :], source_weight[...])
 
 
@@ -240,12 +263,47 @@
     out[...] = (refined[...].astype(F32) + dot(picks, returned[...])).astype(BF)
 
 
-def call(kernel, outs, *args, scratch=(), **static):
-    import functools
-
-    body = functools.partial(kernel, *static.values()) if static else kernel
+def pair_kernel(first, second, out):
+    out[...] = (first[...].astype(F32) + second[...].astype(F32)).astype(BF)
+
+
+def total_kernel(arrived, out):
+    out[...] = jnp.sum(arrived[...].astype(F32), axis=0).astype(BF)
+
+
+def spread_kernel(early, arrived, out):
+    late = jnp.sum(arrived[...].astype(F32), axis=0).astype(BF)
+    rows = early.shape[0]
+    peers = out.shape[0]
+    out[:, :rows, :] = jnp.broadcast_to(early[...][None], (peers, rows, LANES))
+    out[:, rows:, :] = jnp.broadcast_to(late[None], (peers,) + late.shape)
+
+
+def results_kernel(early, core, mine, other, source, target, edge, inner, outer, coarse):
+    width = outer.shape[0]
+    half = width // 2
+    blocks = width // LANES
+    for gathered, which in ((mine, core[0]), (other, 1 - core[0])):
+        peers, rows, lanes = gathered.shape
+        first = gathered[:, :early, :].astype(F32).reshape(peers * early, lanes)
+        second = gathered[:, early:, :].astype(F32).reshape(peers * (rows - early), lanes)
+        places = ((outer, 0, first), (inner, 0, first), (inner, width, first), (coarse, 0, first))
+        places += ((edge, 0, second), (source, 0, second), (target, 0, second))
+        for number, (out, base, values) in enumerate(places):
+            at = (number if number < 4 else number - 4) * blocks * half
+            span = pl.ds(pl.multiple_of(base + which * half, half), half)
+            for k in range(blocks):
+                out[span, k * LANES : (k + 1) * LANES] = values[at + k * half : at + (k + 1) * half, :]
+
+
+def call(kernel, outs, *args, scratch=(), core=None, **static):
+    body = functools.partial(kernel, *static.values())
+    specs = [pl.BlockSpec(memory_space=pltpu.VMEM)] * len(args)
+    if core is not None:
+        args, specs = (core,) + args, [pl.BlockSpec(memory_space=pltpu.SMEM)] + specs
     return pl.pallas_call(
         body,
+        in_specs=specs,
         out_shape=[jax.ShapeDtypeStruct(shape, dtype) for shape, dtype in outs],
         scratch_shapes=[pltpu.VMEM(shape, dtype) for shape, dtype in scratch],
         compiler_params=pltpu.CompilerParams(vmem_limit_bytes=60 * 2 ** 20),
@@ -254,7 +312,7 @@
 
 
 def passed_along(value, axis, steps):
-    count = lax.axis_size(axis)
+    count = math.prod(lax.axis_size(name) for name in axis)
     initial, last = (max(0, -steps), min(count, count - steps))
     return lax.ppermute(value, axis, [(source, source + steps) for source in range(initial, last)])
 
@@ -262,35 +320,25 @@
 def trade_halo(blocks, flip):
     moved = []
     for number, offset in enumerate((1, -1)):
-        moved.append(passed_along(blocks[number], "row", offset * flip))
+        moved.append(passed_along(blocks[number], ROW, offset * flip))
     for number, offset in enumerate((1, -1)):
-        moved.append(passed_along(blocks[2 + number], "col", offset * flip))
+        moved.append(passed_along(blocks[2 + number], COL, offset * flip))
     return moved
 
 
 def trade_slots(buffer, devices):
     slots, width = buffer.shape
     shaped = buffer.reshape(devices, slots // devices, width)
-    moved = lax.all_to_all(shaped, ("row", "col"), split_axis=0, concat_axis=0, tiled=True)
+    moved = lax.all_to_all(shaped, ALL, split_axis=0, concat_axis=0, tiled=True)
     return moved.reshape(slots, width)
 
 
-def summed(parts):
-    stacked = jnp.concatenate(parts, axis=0)
-    narrow = lax.psum(stacked.astype(F16), ("row", "col")).astype(F32)
-    sizes = []
-    for part in range(stacked.shape[0] // 512):
-        block = narrow[part * 512 : (part + 1) * 512]
-        sizes.append(jnp.mean(block * block))
-    sizes = jnp.stack(sizes)
-    fits = jnp.all(sizes > LOW * LOW) & (jnp.max(jnp.abs(narrow)) < HIGH)
-    return lax.cond(
-        fits,
-        lambda narrow, stacked: narrow,
-        lambda narrow, stacked: lax.psum(stacked, ("row", "col")),
-        narrow,
-        stacked,
-    )
+def across(value):
+    return lax.ppermute(value, "core", [(0, 1), (1, 0)])
+
+
+def trade_chips(value):
+    return lax.all_to_all(value, CHIPS, split_axis=0, concat_axis=0, tiled=True)
 
 
 def local(
@@ -308,7 +356,9 @@
     outer_weight,
     coarse_weight,
 ):
-    devices = lax.axis_size("row") * lax.axis_size("col")
+    chips = math.prod(lax.axis_size(name) for name in CHIPS)
+    devices = 2 * chips
+    core = lax.axis_index("core").reshape(1)
     rows, width = nodes.shape
     edges = edge_source.shape[0]
     halo_rows = halo_lists.shape[2]
@@ -323,6 +373,7 @@
     receivers = edge_target.reshape(edges // LANES, LANES)
     node_block, edge_block = (rows, width), (edges, width)
     square = ((width, width), F32)
+    packed = width // 2 * width // LANES
 
     (halo_sent,) = call(halo_kernel, [((4 * halo_rows, width), BF)], nodes, lists)
     sent_blocks = [halo_sent[k * halo_rows : (k + 1) * halo_rows] for k in range(4)]
@@ -352,58 +403,68 @@
         arrived, members, totals, counts, table, coarse_weight,
     )
     share_returned = trade_slots(share_sent, devices)
-    update_sent, coarse_gradient = call(
-        coarse_rest_kernel, [((slots, width), BF), square], update, coarse, grad_coarse, table, scale=scale
-    )
-    update_sent, share_returned = lax.optimization_barrier((update_sent, share_returned))
+    (update_sent,) = call(coarse_rest_kernel, [((slots, width), BF)], update, table)
     update_returned = trade_slots(update_sent, devices)
-    grad_aggregate, base, outer_gradient, inner_gradient = call(
+    grad_aggregate, base, keep, give = call(
         node_back_kernel,
-        [(node_block, BF), (node_block, F32), square, ((2 * width, width), F32)],
-        share_returned, slot, cotangent, nodes, aggregate, node_hidden, node_slope, inner_weight, outer_weight,
-        scale=scale,
-    )
+        [(node_block, BF), (node_block, F32), ((4 * packed, LANES), BF), ((4 * packed, LANES), BF)],
+        share_returned, slot, cotangent, nodes, aggregate, node_hidden, node_slope, coarse, grad_coarse,
+        inner_weight, outer_weight,
+        core=core, scale=scale,
+    )
+    taken = across(give)
     grad_message, grad_edges, grad_sources, back = call(
         edge_back_kernel,
         [(edge_block, BF), (edge_block, BF), ((extended, width), BF), ((4 * halo_rows, width), BF)],
         senders, receivers, grad_aggregate, edge_slope, message_slope, edge_weight, source_weight,
         scratch=[((extended, edges), BF)],
     )
+    (early,) = call(pair_kernel, [((4 * packed, LANES), BF)], keep, taken)
+    early_rows = 4 * packed // chips
+    early = trade_chips(early.reshape(chips, early_rows, LANES))
     returned = trade_halo([back[k * halo_rows : (k + 1) * halo_rows] for k in range(4)], -1)
-    source_gradient, target_gradient, edge_gradient, partial = call(
+    keep, give, partial = call(
         weights_kernel,
-        [square, square, square, (node_block, F32)],
+        [((3 * packed, LANES), BF), ((3 * packed, LANES), BF), (node_block, F32)],
         receivers, edge_hidden, grad_message, grad_edges, grad_sources, *halo,
         nodes, base, source_weight, target_weight,
-        scratch=[((rows, edges), BF)],
-        scale=scale,
-    )
+        scratch=[((rows, edges), BF), ((extended, width), BF)],
+        core=core, scale=scale,
+    )
+    (late,) = call(pair_kernel, [((3 * packed, LANES), BF)], keep, across(give))
+    late_rows = 3 * packed // chips
+    late = trade_chips(late.reshape(chips, late_rows, LANES))
+    (early,) = call(total_kernel, [((early_rows, LANES), BF)], early)
+    (sent,) = call(spread_kernel, [((chips, early_rows + late_rows, LANES), BF)], early, late)
+    mine = trade_chips(sent)
     (node_gradient,) = call(node_gradient_kernel, [(node_block, F32)], partial, lists, *returned)
-    parts = [source_gradient, target_gradient, edge_gradient, inner_gradient, outer_gradient, coarse_gradient]
-    sums = summed(parts)
     (updated,) = call(updated_kernel, [(node_block, BF)], refined, update_returned, slot)
-    results, at = [], 0
-    for part in parts:
-        results.append(sums[at : at + part.shape[0]])
-        at += part.shape[0]
+    results = call(
+        results_kernel,
+        [square, square, square, ((2 * width, width), F32), square, square],
+        mine, across(mine),
+        core=core, early=early_rows,
+    )
     return (updated, node_gradient, *results)
 
 
 def solution(mesh):
+    whole = mesh.devices.reshape(mesh.shape["row"] // 2, 2, -1, 4)
+    mesh = Mesh(whole, ALL)
     in_specs = (
-        P(("row", "col"), None),
-        P(("row", "col"), None),
-        P(("row", "col")),
-        P(("row", "col")),
-        P(("row", "col"), None, None),
-        P(("row", "col")),
-        P(("row", "col"), None),
-        P(),
-        P(),
-        P(),
-        P(),
-        P(),
-        P(),
-    )
-    out_specs = (P(("row", "col"), None), P(("row", "col"), None), P(), P(), P(), P(), P(), P())
+        P(ALL, None),
+        P(ALL, None),
+        P(ALL),
+        P(ALL),
+        P(ALL, None, None),
+        P(ALL),
+        P(ALL, None),
+        P(),
+        P(),
+        P(),
+        P(),
+        P(),
+        P(),
+    )
+    out_specs = (P(ALL, None), P(ALL, None), P(), P(), P(), P(), P(), P())
     return jax.shard_map(local, mesh=mesh, in_specs=in_specs, out_specs=out_specs, check_vma=False)

time: 319 us -> 251 us (0.79)
  blocking collectives: 107 us -> 29.2 us
  waiting for transfers between devices: 33.4 us -> 64.6 us
  local copies, waits for them, and re-layouts: 31.5 us -> 8.36 us
  between operations: 20.2 us -> 0.91 us
  starting transfers between devices: 55 us -> 73.6 us
  Pallas kernels: 58.5 us -> 73.4 us
  other arithmetic: 10.7 us -> 0 us
    psum x1 -> x0, blocking collectives: 107 us -> none  [summed(): narrow = lax.psum(stacked.astype(F16), ('row', 'col')).astype(F32)]
    all_to_all x0 -> x1, blocking collectives: none -> 29.2 us  [trade_chips(): return lax.all_to_all(value, CHIPS, split_axis=0, concat_axis=0, tiled=True)]
    all_to_all x4 -> x6, waiting for transfers between devices: 32.4 us -> 56.3 us  [the longest x4 43.4 us: trade_slots(): moved = lax.all_to_all(shaped, ALL, split_axis=0, concat_axis=0, tiled=True)]
    pallas_call x11 -> x16, Pallas kernels: 58.5 us -> 73.4 us  [call(): pl.pallas_call(body, in_specs=specs, out_shape=[jax.ShapeDtypeStruct(shap...]
    all_to_all x4 -> x6, starting transfers between devices: 33.1 us -> 47.6 us  [the longest x4 32.7 us: trade_slots(): moved = lax.all_to_all(shaped, ALL, split_axis=0, concat_axis=0, tiled=True)]
    slice x2 -> x0, local copies, waits for them, and re-layouts: 7.99 us -> none  [local(): results.append(sums[at:at + part.shape[0]])]
    cond x1 -> x0, local copies, waits for them, and re-layouts: 6.87 us -> none
    unnamed x39 -> x38, local copies, waits for them, and re-layouts: 13.6 us -> 6.88 us
  transfers between devices with their start and end apart: 12 -> 17, of which waited for: 4 -> 8; matrix products, arithmetic and copies ran while one was open for 10% -> 1% of each run, Pallas kernels for 15% -> 19%
where the time goes in v2:
time: 251 us; the launch traced here: 250 us
  starting transfers between devices  73.6 us (29%)
  Pallas kernels  73.4 us (29%)
  waiting for transfers between devices  64.6 us (26%)
  blocking collectives  29.2 us (12%)
  local copies, waits for them, and re-layouts  8.36 us (3%)
    pallas_call x16, Pallas kernels, call(): pl.pallas_call(body, in_specs=specs, out_shape=[jax.ShapeDtypeStruct(shap...  73.4 us
    all_to_all x4, waiting for transfers between devices, trade_slots(): moved = lax.all_to_all(shaped, ALL, split_axis=0, concat_axis=0, tiled=True)  43.4 us
    all_to_all x4, starting transfers between devices, trade_slots(): moved = lax.all_to_all(shaped, ALL, split_axis=0, concat_axis=0, tiled=True)  32.7 us
    all_to_all x1, blocking collectives, trade_chips(): return lax.all_to_all(value, CHIPS, split_axis=0, concat_axis=0, tiled=True)  29.2 us
    ppermute x8, starting transfers between devices, passed_along(): lax.ppermute(value, axis, [(source, source + steps) for source in range(i...  20.9 us
    all_to_all x2, starting transfers between devices, trade_chips(): return lax.all_to_all(value, CHIPS, split_axis=0, concat_axis=0, tiled=True)  14.9 us
    all_to_all x2, waiting for transfers between devices, trade_chips(): return lax.all_to_all(value, CHIPS, split_axis=0, concat_axis=0, tiled=True)  12.9 us
    unnamed x38, local copies, waits for them, and re-layouts  6.88 us
  transfers between devices with their start and end apart: 17, of which 8 were waited for; matrix products, arithmetic and copies ran while one was open for 1% of the time, Pallas kernels for 19%

profile of v2, /device:TPU:1, one launch (start us, length us, event | category | flops | bytes accessed | tf_op | source)
XLA Modules:
  0.0 250.1 jit_solution(8069145550544150282)
XLA Ops:
  0.6 3.8 %prepare_kernel.1 = (s32[1,512]{1,0:T(1,128)}, bf16[1024,512]{1,0:T(8,128)(2,1)}, bf16[512,512]{1,0:T(8,128)(2,1)}, bf16[512,512]{1,0:T(8,128)(2,1)}) custom-call(s32[4,128]{1,0:T(4,128)} %bitcast.33, bf16[512,512]{1,0:T(8,128)(2,1)} %cotangent.3, bf16[512,512]{1,0:T(8,128)(2,1)} %nodes.9, bf16[512,512]{1,0:T(8,128)(2,1)} %source_weight.7, ...), custom_call_target="tpu_custom_call" | custom-call | tf_op jit(solution)/shard_map/prepare_kernel/pallas_call | solution.py:304
  4.4 11.5 %all-to-all-start.1 = ((bf16[128,8,512]{2,1,0:T(8,128)(2,1)}), bf16[128,8,512]{2,1,0:T(8,128)(2,1)S(1)}, u32[]{:S(2)}, u32[]{:S(2)}) async-start(bf16[128,8,512]{2,1,0:T(8,128)(2,1)} %bitcast.22), calls=%async_computation.1 | async-start | bytes 2097152 | tf_op jit(solution)/shard_map/all_to_all | solution.py:332
  15.9 0.7 reshape.64.lists
  16.6 2.0 halo_kernel.1
  18.6 0.8 fusion.1
  19.4 3.7 %collective-permute-start = (bf16[32,512]{1,0:T(8,128)(2,1)S(1)}, bf16[32,512]{1,0:T(8,128)(2,1)S(1)}, u32[]{:S(2)}, u32[]{:S(2)}) collective-permute-start(bf16[32,512]{1,0:T(8,128)(2,1)S(1)} %get-tuple-element.87), channel_id=1, source_target_pairs={{0,16},{16,32},{32,48},{48,64},{64,80},{80,96},{96,112},{1,17},{17... | collective-permute-start | bytes 98312 | tf_op jit(solution)/shard_map/ppermute | solution.py:317
  23.1 1.9 collective-permute-start.1
  25.0 3.2 %collective-permute-start.2 = (bf16[32,512]{1,0:T(8,128)(2,1)S(1)}, bf16[32,512]{1,0:T(8,128)(2,1)S(1)}, u32[]{:S(2)}, u32[]{:S(2)}) collective-permute-start(bf16[32,512]{1,0:T(8,128)(2,1)S(1)} %get-tuple-element.85), channel_id=1, source_target_pairs={{0,1},{1,2},{2,3},{3,4},{4,5},{5,6},{6,7},{7,8},{8,9},{9,10},{10,1... | collective-permute-start | bytes 98312 | tf_op jit(solution)/shard_map/ppermute | solution.py:317
  28.1 1.3 collective-permute-start.3
  29.5 3.6 %collective-permute-done.3.halo_3 = bf16[32,512]{1,0:T(8,128)(2,1)S(1)} collective-permute-done((bf16[32,512]{1,0:T(8,128)(2,1)S(1)}, bf16[32,512]{1,0:T(8,128)(2,1)S(1)}, u32[]{:S(2)}, u32[]{:S(2)}) %collective-permute-start.3) | collective-permute-done | bytes 32800 | tf_op jit(solution)/shard_map/ppermute | solution.py:317
  33.7 13.6 %forward_kernel.1 = (bf16[2048,512]{1,0:T(8,128)(2,1)}, bf16[2048,512]{1,0:T(8,128)(2,1)}, bf16[2048,512]{1,0:T(8,128)(2,1)}, bf16[512,512]{1,0:T(8,128)(2,1)}, ...) custom-call(bf16[32,512]{1,0:T(8,128)(2,1)} %copy-done.9, ...), custom_call_target="tpu_custom_call" | custom-call | tf_op jit(solution)/shard_map/forward_kernel/pallas_call | solution.py:304
  47.4 12.2 %all-to-all-start = ((bf16[128,8,512]{2,1,0:T(8,128)(2,1)}), bf16[128,8,512]{2,1,0:T(8,128)(2,1)S(1)}, u32[]{:S(2)}, u32[]{:S(2)}) async-start(bf16[128,8,512]{2,1,0:T(8,128)(2,1)} %bitcast.23), calls=%async_computation | async-start | bytes 2097152 | tf_op jit(solution)/shard_map/all_to_all | solution.py:332
  59.6 2.3 members_kernel.1
  61.9 16.5 %all-to-all-done = bf16[128,8,512]{2,1,0:T(8,128)(2,1)S(1)} async-done(((bf16[128,8,512]{2,1,0:T(8,128)(2,1)}), bf16[128,8,512]{2,1,0:T(8,128)(2,1)S(1)}, u32[]{:S(2)}, u32[]{:S(2)}) %all-to-all-start) | async-done | bytes 1048608 | tf_op jit(solution)/shard_map/all_to_all | solution.py:332
  78.4 1.0 copy-done.4
  79.4 3.7 %coarse_kernel.1 = (bf16[1024,512]{1,0:T(8,128)(2,1)}, bf16[128,512]{1,0:T(8,128)(2,1)}, bf16[128,512]{1,0:T(8,128)(2,1)}, bf16[128,512]{1,0:T(8,128)(2,1)}) custom-call(bf16[1024,512]{1,0:T(8,128)(2,1)} %bitcast.19, bf16[128,1024]{1,0:T(8,128)(2,1)} %get-tuple-element.50.members, f32[128,512]{1,0:T(8,128)} %get-tuple-element.51.totals, ...), custom_call_target="tpu_custom_call" | custom-call | tf_op jit(solution)/shard_map/coarse_kernel/pallas_call | solution.py:304
  83.0 4.7 %all-to-all-start.3 = ((bf16[128,8,512]{2,1,0:T(8,128)(2,1)}), bf16[128,8,512]{2,1,0:T(8,128)(2,1)S(1)}, u32[]{:S(2)}, u32[]{:S(2)}) async-start(bf16[128,8,512]{2,1,0:T(8,128)(2,1)} %bitcast.24), calls=%async_computation.3 | async-start | bytes 2097152 | tf_op jit(solution)/shard_map/all_to_all | solution.py:332
  87.7 19.0 %all-to-all-done.3 = bf16[128,8,512]{2,1,0:T(8,128)(2,1)S(1)} async-done(((bf16[128,8,512]{2,1,0:T(8,128)(2,1)}), bf16[128,8,512]{2,1,0:T(8,128)(2,1)S(1)}, u32[]{:S(2)}, u32[]{:S(2)}) %all-to-all-start.3) | async-done | bytes 1048608 | tf_op jit(solution)/shard_map/all_to_all | solution.py:332
  106.7 1.0 copy-done.5
  107.7 6.6 %node_back_kernel.1 = (bf16[512,512]{1,0:T(8,128)(2,1)}, f32[512,512]{1,0:T(8,128)}, bf16[4096,128]{1,0:T(8,128)(2,1)}, bf16[4096,128]{1,0:T(8,128)(2,1)}) custom-call(s32[1]{0:T(128)} %bitcast.10.core, bf16[1024,512]{1,0:T(8,128)(2,1)} %bitcast.20, s32[1,512]{1,0:T(1,128)} %get-tuple-element.46.slot, bf16[512,512]{1,0:T(8,128)(2,1)} %cotangent.3, ...), custom_call_target="tpu_custom_call" | custom-call | tf_op jit(solution)/shard_map/node_back_kernel/pallas_call | solution.py:304
  114.2 1.3 collective-permute-start.8
  115.5 2.5 collective-permute-done.8.second
  118.0 1.0 copy-done.7
  119.0 2.7 %pair_kernel.2 = bf16[4096,128]{1,0:T(8,128)(2,1)} custom-call(bf16[4096,128]{1,0:T(8,128)(2,1)} %get-tuple-element.70.first, bf16[4096,128]{1,0:T(8,128)(2,1)} %copy-done.7), custom_call_target="tpu_custom_call" | custom-call | tf_op jit(solution)/shard_map/pair_kernel/pallas_call | solution.py:304
  121.7 4.8 %all-to-all-start.4 = ((bf16[64,64,128]{2,1,0:T(8,128)(2,1)}), bf16[64,64,128]{2,1,0:T(8,128)(2,1)S(1)}, u32[]{:S(2)}, u32[]{:S(2)}) async-start(bf16[64,64,128]{2,1,0:T(8,128)(2,1)} %bitcast.15), calls=%async_computation.4 | async-start | bytes 2097152 | tf_op jit(solution)/shard_map/all_to_all | solution.py:341
  126.6 9.4 %edge_back_kernel.1 = (bf16[2048,512]{1,0:T(8,128)(2,1)}, bf16[2048,512]{1,0:T(8,128)(2,1)}, bf16[640,512]{1,0:T(8,128)(2,1)}, bf16[128,512]{1,0:T(8,128)(2,1)}) custom-call(s32[16,128]{1,0:T(8,128)} %bitcast.32, s32[16,128]{1,0:T(8,128)} %bitcast.26, bf16[512,512]{1,0:T(8,128)(2,1)} %get-tuple-element.61.grad_aggregate, ...), custom_call_target="tpu_custom_call" | custom-call | tf_op jit(solution)/shard_map/edge_back_kernel/pallas_call | solution.py:304
  136.0 8.3 %weights_kernel.1 = (bf16[3072,128]{1,0:T(8,128)(2,1)}, bf16[3072,128]{1,0:T(8,128)(2,1)}, f32[512,512]{1,0:T(8,128)}) custom-call(s32[1]{0:T(128)} %bitcast.10.core, s32[16,128]{1,0:T(8,128)} %bitcast.27, bf16[2048,512]{1,0:T(8,128)(2,1)} %get-tuple-element.54.edge_hidden, bf16[2048,512]{1,0:T(8,128)(2,1)} %get-tuple-element.64.grad_message, ...), custom_call_target="tpu_custom_call" | custom-call | tf_op jit(solution)/shard_map/weights_kernel/pallas_call | solution.py:304
  144.7 2.1 collective-permute-done.9.second
  146.8 0.9 copy-done.8
  147.7 2.4 pair_kernel.3
  150.1 10.1 %all-to-all-start.5 = ((bf16[64,48,128]{2,1,0:T(8,128)(2,1)}), bf16[64,48,128]{2,1,0:T(8,128)(2,1)S(1)}, u32[]{:S(2)}, u32[]{:S(2)}) async-start(bf16[64,48,128]{2,1,0:T(8,128)(2,1)} %bitcast.21), calls=%async_computation.5 | async-start | bytes 1572864 | tf_op jit(solution)/shard_map/all_to_all | solution.py:341
  160.2 2.0 total_kernel.1.early
  162.2 12.9 %all-to-all-done.5.arrived = bf16[64,48,128]{2,1,0:T(8,128)(2,1)S(1)} async-done(((bf16[64,48,128]{2,1,0:T(8,128)(2,1)}), bf16[64,48,128]{2,1,0:T(8,128)(2,1)S(1)}, u32[]{:S(2)}, u32[]{:S(2)}) %all-to-all-start.5) | async-done | bytes 786464 | tf_op jit(solution)/shard_map/all_to_all | solution.py:341
  175.1 0.9 copy-done.6
  176.0 2.7 %spread_kernel.1 = bf16[64,112,128]{2,1,0:T(8,128)(2,1)} custom-call(bf16[64,128]{1,0:T(8,128)(2,1)} %total_kernel.1.early, bf16[64,48,128]{2,1,0:T(8,128)(2,1)} %copy-done.6), custom_call_target="tpu_custom_call" | custom-call | tf_op jit(solution)/shard_map/spread_kernel/pallas_call | solution.py:304
  178.6 29.2 %all_to_all.35.mine = bf16[64,112,128]{2,1,0:T(8,128)(2,1)S(1)} all-to-all(bf16[64,112,128]{2,1,0:T(8,128)(2,1)} %spread_kernel.1), channel_id=1, replica_groups=mesh['z'=4,'core'=2,'x'=4,'y'=4] {'z','x','y'}, dimensions={0} | all-to-all | bytes 3670016 | tf_op jit(solution)/shard_map/all_to_all | solution.py:341
  207.9 3.5 %collective-permute-start.10 = (bf16[64,112,128]{2,1,0:T(8,128)(2,1)S(1)}, bf16[64,112,128]{2,1,0:T(8,128)(2,1)}, u32[]{:S(2)}, u32[]{:S(2)}) collective-permute-start(bf16[64,112,128]{2,1,0:T(8,128)(2,1)S(1)} %all_to_all.35.mine), channel_id=1, source_target_pairs={{0,16},{16,0},{1,17},{17,1},{2,18},{18,2},{3,19},{19,3},{4,20},{20... | collective-permute-start | bytes 5505032 | tf_op jit(solution)/shard_map/ppermute | solution.py:337
  211.4 2.6 %coarse_rest_kernel.1 = bf16[1024,512]{1,0:T(8,128)(2,1)} custom-call(bf16[128,512]{1,0:T(8,128)(2,1)} %get-tuple-element.53.update, s32[8,128]{1,0:T(8,128)} %bitcast.30), custom_call_target="tpu_custom_call" | custom-call | tf_op jit(solution)/shard_map/coarse_rest_kernel/pallas_call | solution.py:304
  214.0 4.3 %all-to-all-start.2 = ((bf16[128,8,512]{2,1,0:T(8,128)(2,1)}), bf16[128,8,512]{2,1,0:T(8,128)(2,1)S(1)}, u32[]{:S(2)}, u32[]{:S(2)}) async-start(bf16[128,8,512]{2,1,0:T(8,128)(2,1)} %bitcast.18), calls=%async_computation.2 | async-start | bytes 2097152 | tf_op jit(solution)/shard_map/all_to_all | solution.py:332
  218.3 3.0 %collective-permute-start.4 = (bf16[32,512]{1,0:T(8,128)(2,1)S(1)}, bf16[32,512]{1,0:T(8,128)(2,1)S(1)}, u32[]{:S(2)}, u32[]{:S(2)}) collective-permute-start(bf16[32,512]{1,0:T(8,128)(2,1)S(1)} %get-tuple-element.83), channel_id=1, source_target_pairs={{16,0},{32,16},{48,32},{64,48},{80,64},{96,80},{112,96},{17,1},{33... | collective-permute-start | bytes 98312 | tf_op jit(solution)/shard_map/ppermute | solution.py:317
  221.3 2.6 %collective-permute-start.5 = (bf16[32,512]{1,0:T(8,128)(2,1)S(1)}, bf16[32,512]{1,0:T(8,128)(2,1)S(1)}, u32[]{:S(2)}, u32[]{:S(2)}) collective-permute-start(bf16[32,512]{1,0:T(8,128)(2,1)S(1)} %get-tuple-element.82), channel_id=1, source_target_pairs={{0,16},{16,32},{32,48},{48,64},{64,80},{80,96},{96,112},{1,17},{17... | collective-permute-start | bytes 98312 | tf_op jit(solution)/shard_map/ppermute | solution.py:317
  223.9 1.3 collective-permute-start.6
  225.2 4.0 %collective-permute-start.7 = (bf16[32,512]{1,0:T(8,128)(2,1)S(1)}, bf16[32,512]{1,0:T(8,128)(2,1)S(1)}, u32[]{:S(2)}, u32[]{:S(2)}) collective-permute-start(bf16[32,512]{1,0:T(8,128)(2,1)S(1)} %get-tuple-element.80), channel_id=1, source_target_pairs={{0,1},{1,2},{2,3},{3,4},{4,5},{5,6},{6,7},{7,8},{8,9},{9,10},{10,1... | collective-permute-start | bytes 98312 | tf_op jit(solution)/shard_map/ppermute | solution.py:317
  229.2 7.9 %all-to-all-done.2 = bf16[128,8,512]{2,1,0:T(8,128)(2,1)S(1)} async-done(((bf16[128,8,512]{2,1,0:T(8,128)(2,1)}), bf16[128,8,512]{2,1,0:T(8,128)(2,1)S(1)}, u32[]{:S(2)}, u32[]{:S(2)}) %all-to-all-start.2) | async-done | bytes 1048608 | tf_op jit(solution)/shard_map/all_to_all | solution.py:332
  237.1 1.0 copy-done.1
  238.1 3.2 %updated_kernel.1 = bf16[512,512]{1,0:T(8,128)(2,1)} custom-call(bf16[512,512]{1,0:T(8,128)(2,1)} %get-tuple-element.47.refined, bf16[1024,512]{1,0:T(8,128)(2,1)} %bitcast.16, s32[1,512]{1,0:T(1,128)} %get-tuple-element.46.slot), custom_call_target="tpu_custom_call" | custom-call | tf_op jit(solution)/shard_map/updated_kernel/pallas_call | solution.py:304
  241.9 2.5 node_gradient_kernel.1
  244.4 5.7 %results_kernel.1 = (f32[512,512]{1,0:T(8,128)}, f32[512,512]{1,0:T(8,128)}, f32[512,512]{1,0:T(8,128)}, f32[1024,512]{1,0:T(8,128)}, f32[512,512]{1,0:T(8,128)}, /*index=5*/f32[512,512]{1,0:T(8,128)}) custom-call(s32[1]{0:T(128)} %bitcast.10.core, bf16[64,112,128]{2,1,0:T(8,128)(2,1)} %copy-done, bf16[64,112,128]{2,1,0:T(8,128)(2,1)} %collective-permute-done.10.other), custom_call_target="tpu_custom_call" | custom-call | tf_op jit(solution)/shard_map/results_kernel/pallas_call | solution.py:304
  (44 shorter events, 1.7 us)
Async XLA Ops:
  0.6 15.3 %copy-start.18 = (s32[1,4,32]{2,1,0:T(4,128)S(1)}, s32[1,4,32]{2,1,0:T(4,128)}, u32[]{:S(2)}) copy-start(s32[1,4,32]{2,1,0:T(4,128)} %param.17) | copy-start | bytes 1540
  4.4 42.9 %all-to-all-start.1 = ((bf16[128,8,512]{2,1,0:T(8,128)(2,1)}), bf16[128,8,512]{2,1,0:T(8,128)(2,1)S(1)}, u32[]{:S(2)}, u32[]{:S(2)}) async-start(bf16[128,8,512]{2,1,0:T(8,128)(2,1)} %bitcast.22), calls=%async_computation.1 | async-start | bytes 2097152 | tf_op jit(solution)/shard_map/all_to_all | solution.py:332
  19.4 10.1 %collective-permute-start = (bf16[32,512]{1,0:T(8,128)(2,1)S(1)}, bf16[32,512]{1,0:T(8,128)(2,1)S(1)}, u32[]{:S(2)}, u32[]{:S(2)}) collective-permute-start(bf16[32,512]{1,0:T(8,128)(2,1)S(1)} %get-tuple-element.87), channel_id=1, source_target_pairs={{0,16},{16,32},{32,48},{48,64},{64,80},{80,96},{96,112},{1,17},{17... | collective-permute-start | bytes 98312 | tf_op jit(solution)/shard_map/ppermute | solution.py:317
  23.1 6.5 %collective-permute-start.1 = (bf16[32,512]{1,0:T(8,128)(2,1)S(1)}, bf16[32,512]{1,0:T(8,128)(2,1)S(1)}, u32[]{:S(2)}, u32[]{:S(2)}) collective-permute-start(bf16[32,512]{1,0:T(8,128)(2,1)S(1)} %get-tuple-element.86), channel_id=1, source_target_pairs={{16,0},{32,16},{48,32},{64,48},{80,64},{96,80},{112,96},{17,1},{33... | collective-permute-start | bytes 98312 | tf_op jit(solution)/shard_map/ppermute | solution.py:317
  25.0 4.6 %collective-permute-start.2 = (bf16[32,512]{1,0:T(8,128)(2,1)S(1)}, bf16[32,512]{1,0:T(8,128)(2,1)S(1)}, u32[]{:S(2)}, u32[]{:S(2)}) collective-permute-start(bf16[32,512]{1,0:T(8,128)(2,1)S(1)} %get-tuple-element.85), channel_id=1, source_target_pairs={{0,1},{1,2},{2,3},{3,4},{4,5},{5,6},{6,7},{7,8},{8,9},{9,10},{10,1... | collective-permute-start | bytes 98312 | tf_op jit(solution)/shard_map/ppermute | solution.py:317
  28.1 5.0 %collective-permute-start.3 = (bf16[32,512]{1,0:T(8,128)(2,1)S(1)}, bf16[32,512]{1,0:T(8,128)(2,1)S(1)}, u32[]{:S(2)}, u32[]{:S(2)}) collective-permute-start(bf16[32,512]{1,0:T(8,128)(2,1)S(1)} %get-tuple-element.84), channel_id=1, source_target_pairs={{1,0},{2,1},{3,2},{4,3},{5,4},{6,5},{7,6},{8,7},{9,8},{10,9},{11,1... | collective-permute-start | bytes 98312 | tf_op jit(solution)/shard_map/ppermute | solution.py:317
  29.5 3.6 %copy-start.9 = (bf16[32,512]{1,0:T(8,128)(2,1)}, bf16[32,512]{1,0:T(8,128)(2,1)S(1)}, u32[]{:S(2)}) copy-start(bf16[32,512]{1,0:T(8,128)(2,1)S(1)} %collective-permute-done.halo_0) | copy-start | bytes 98308
  29.5 3.6 %copy-start.10 = (bf16[32,512]{1,0:T(8,128)(2,1)}, bf16[32,512]{1,0:T(8,128)(2,1)S(1)}, u32[]{:S(2)}) copy-start(bf16[32,512]{1,0:T(8,128)(2,1)S(1)} %collective-permute-done.1.halo_1) | copy-start | bytes 98308
  29.5 3.6 %copy-start.11 = (bf16[32,512]{1,0:T(8,128)(2,1)}, bf16[32,512]{1,0:T(8,128)(2,1)S(1)}, u32[]{:S(2)}) copy-start(bf16[32,512]{1,0:T(8,128)(2,1)S(1)} %collective-permute-done.2.halo_2) | copy-start | bytes 98308
  33.1 0.6 copy-start.12
  47.3 12.2 %copy-start.2 = (bf16[128,8,512]{2,1,0:T(8,128)(2,1)}, bf16[128,8,512]{2,1,0:T(8,128)(2,1)S(1)}, u32[]{:S(2)}) copy-start(bf16[128,8,512]{2,1,0:T(8,128)(2,1)S(1)} %all-to-all-done.1) | copy-start | bytes 3145732
  47.4 31.1 %all-to-all-start = ((bf16[128,8,512]{2,1,0:T(8,128)(2,1)}), bf16[128,8,512]{2,1,0:T(8,128)(2,1)S(1)}, u32[]{:S(2)}, u32[]{:S(2)}) async-start(bf16[128,8,512]{2,1,0:T(8,128)(2,1)} %bitcast.23), calls=%async_computation | async-start | bytes 2097152 | tf_op jit(solution)/shard_map/all_to_all | solution.py:332
  78.4 1.0 copy-start.4
  83.0 23.7 %all-to-all-start.3 = ((bf16[128,8,512]{2,1,0:T(8,128)(2,1)}), bf16[128,8,512]{2,1,0:T(8,128)(2,1)S(1)}, u32[]{:S(2)}, u32[]{:S(2)}) async-start(bf16[128,8,512]{2,1,0:T(8,128)(2,1)} %bitcast.24), calls=%async_computation.3 | async-start | bytes 2097152 | tf_op jit(solution)/shard_map/all_to_all | solution.py:332
  106.7 1.0 copy-start.5
  114.2 3.8 %collective-permute-start.8 = (bf16[4096,128]{1,0:T(8,128)(2,1)}, bf16[4096,128]{1,0:T(8,128)(2,1)S(1)}, u32[]{:S(2)}, u32[]{:S(2)}) collective-permute-start(bf16[4096,128]{1,0:T(8,128)(2,1)} %get-tuple-element.71), channel_id=1, source_target_pairs={{0,16},{16,0},{1,17},{17,1},{2,18},{18,2},{3,19},{19,3},{4,20},{20... | collective-permute-start | bytes 3145736 | tf_op jit(solution)/shard_map/ppermute | solution.py:337
  118.0 1.0 copy-start.7
  121.7 28.4 %all-to-all-start.4 = ((bf16[64,64,128]{2,1,0:T(8,128)(2,1)}), bf16[64,64,128]{2,1,0:T(8,128)(2,1)S(1)}, u32[]{:S(2)}, u32[]{:S(2)}) async-start(bf16[64,64,128]{2,1,0:T(8,128)(2,1)} %bitcast.15), calls=%async_computation.4 | async-start | bytes 2097152 | tf_op jit(solution)/shard_map/all_to_all | solution.py:341
  144.3 2.5 collective-permute-start.9
  146.8 0.9 copy-start.8
  150.1 10.1 %copy-start.3 = (bf16[64,64,128]{2,1,0:T(8,128)(2,1)}, bf16[64,64,128]{2,1,0:T(8,128)(2,1)S(1)}, u32[]{:S(2)}) copy-start(bf16[64,64,128]{2,1,0:T(8,128)(2,1)S(1)} %all-to-all-done.4.arrived) | copy-start | bytes 3145732
  150.1 25.0 %all-to-all-start.5 = ((bf16[64,48,128]{2,1,0:T(8,128)(2,1)}), bf16[64,48,128]{2,1,0:T(8,128)(2,1)S(1)}, u32[]{:S(2)}, u32[]{:S(2)}) async-start(bf16[64,48,128]{2,1,0:T(8,128)(2,1)} %bitcast.21), calls=%async_computation.5 | async-start | bytes 1572864 | tf_op jit(solution)/shard_map/all_to_all | solution.py:341
  175.1 0.9 copy-start.6
  207.9 33.4 %copy-start = (bf16[64,112,128]{2,1,0:T(8,128)(2,1)}, bf16[64,112,128]{2,1,0:T(8,128)(2,1)S(1)}, u32[]{:S(2)}) copy-start(bf16[64,112,128]{2,1,0:T(8,128)(2,1)S(1)} %all_to_all.35.mine) | copy-start | bytes 5505028
  207.9 10.4 %copy-start.13 = (bf16[128,512]{1,0:T(8,128)(2,1)S(1)}, bf16[128,512]{1,0:T(8,128)(2,1)}, u32[]{:S(2)}) copy-start(bf16[128,512]{1,0:T(8,128)(2,1)} %get-tuple-element.69) | copy-start | bytes 393220
  207.9 36.5 %collective-permute-start.10 = (bf16[64,112,128]{2,1,0:T(8,128)(2,1)S(1)}, bf16[64,112,128]{2,1,0:T(8,128)(2,1)}, u32[]{:S(2)}, u32[]{:S(2)}) collective-permute-start(bf16[64,112,128]{2,1,0:T(8,128)(2,1)S(1)} %all_to_all.35.mine), channel_id=1, source_target_pairs={{0,16},{16,0},{1,17},{17,1},{2,18},{18,2},{3,19},{19,3},{4,20},{20... | collective-permute-start | bytes 5505032 | tf_op jit(solution)/shard_map/ppermute | solution.py:337
  214.0 23.1 %all-to-all-start.2 = ((bf16[128,8,512]{2,1,0:T(8,128)(2,1)}), bf16[128,8,512]{2,1,0:T(8,128)(2,1)S(1)}, u32[]{:S(2)}, u32[]{:S(2)}) async-start(bf16[128,8,512]{2,1,0:T(8,128)(2,1)} %bitcast.18), calls=%async_computation.2 | async-start | bytes 2097152 | tf_op jit(solution)/shard_map/all_to_all | solution.py:332
  218.3 22.9 %collective-permute-start.4 = (bf16[32,512]{1,0:T(8,128)(2,1)S(1)}, bf16[32,512]{1,0:T(8,128)(2,1)S(1)}, u32[]{:S(2)}, u32[]{:S(2)}) collective-permute-start(bf16[32,512]{1,0:T(8,128)(2,1)S(1)} %get-tuple-element.83), channel_id=1, source_target_pairs={{16,0},{32,16},{48,32},{64,48},{80,64},{96,80},{112,96},{17,1},{33... | collective-permute-start | bytes 98312 | tf_op jit(solution)/shard_map/ppermute | solution.py:317
  221.3 20.0 %collective-permute-start.5 = (bf16[32,512]{1,0:T(8,128)(2,1)S(1)}, bf16[32,512]{1,0:T(8,128)(2,1)S(1)}, u32[]{:S(2)}, u32[]{:S(2)}) collective-permute-start(bf16[32,512]{1,0:T(8,128)(2,1)S(1)} %get-tuple-element.82), channel_id=1, source_target_pairs={{0,16},{16,32},{32,48},{48,64},{64,80},{80,96},{96,112},{1,17},{17... | collective-permute-start | bytes 98312 | tf_op jit(solution)/shard_map/ppermute | solution.py:317
  223.9 17.4 %collective-permute-start.6 = (bf16[32,512]{1,0:T(8,128)(2,1)S(1)}, bf16[32,512]{1,0:T(8,128)(2,1)S(1)}, u32[]{:S(2)}, u32[]{:S(2)}) collective-permute-start(bf16[32,512]{1,0:T(8,128)(2,1)S(1)} %get-tuple-element.81), channel_id=1, source_target_pairs={{1,0},{2,1},{3,2},{4,3},{5,4},{6,5},{7,6},{8,7},{9,8},{10,9},{11,1... | collective-permute-start | bytes 98312 | tf_op jit(solution)/shard_map/ppermute | solution.py:317
  225.2 16.1 %collective-permute-start.7 = (bf16[32,512]{1,0:T(8,128)(2,1)S(1)}, bf16[32,512]{1,0:T(8,128)(2,1)S(1)}, u32[]{:S(2)}, u32[]{:S(2)}) collective-permute-start(bf16[32,512]{1,0:T(8,128)(2,1)S(1)} %get-tuple-element.80), channel_id=1, source_target_pairs={{0,1},{1,2},{2,3},{3,4},{4,5},{5,6},{6,7},{7,8},{8,9},{9,10},{10,1... | collective-permute-start | bytes 98312 | tf_op jit(solution)/shard_map/ppermute | solution.py:317
  237.1 1.0 copy-start.1
  241.2 0.6 copy-start.14
  241.3 0.6 copy-start.15
  241.3 0.6 copy-start.16
  241.3 0.6 copy-start.17

commit v3 on v2

--- a/solution.py
+++ b/solution.py
@@ -8,6 +8,7 @@
 from jax.experimental.pallas import tpu as pltpu
 from jax.sharding import Mesh
 from jax.sharding import PartitionSpec as P
+
 
 BF = jnp.bfloat16
 F32 = jnp.float32
@@ -147,22 +148,16 @@
     totals[...] = dot(ones.astype(BF), arrived[...])
 
 
-def coarse_kernel(arrived, members, totals, counts, table, weight, share_out, update, coarse_out, grad_out):
+def coarse_kernel(arrived, members, totals, counts, table, weight, out, coarse_out, grad_out):
     count = counts[:, :1]
     coarse = (dot(members[...], arrived[...]) / count).astype(BF)
     coarse_out[...] = coarse
     active, slope = gates(dot(coarse, weight[...]))
-    update[...] = active.astype(BF)
     grad = (totals[...] * slope).astype(BF)
     grad_out[...] = grad
     share = (right_dot(grad, weight[...]) / count).astype(BF)
-    picks = hot(wide_column(wide_row(table)) == iota((share_out.shape[0], coarse.shape[0]), 1))
-    share_out[...] = dot(picks, share).astype(BF)
-
-
-def coarse_rest_kernel(update, table, update_out):
-    picks = hot(wide_column(wide_row(table)) == iota((update_out.shape[0], update.shape[0]), 1))
-    update_out[...] = dot(picks, update[...]).astype(BF)
+    picks = hot(wide_column(wide_row(table)) == iota((out.shape[0], coarse.shape[0]), 1))
+    out[...] = dot(picks, jnp.concatenate([share, active.astype(BF)], axis=1)).astype(BF)
 
 
 def half_of(ref, half):
@@ -193,7 +188,7 @@
 ):
     rows, width = nodes.shape
     picks = hot(wide_column(slot[...]) == iota((rows, returned.shape[0]), 1))
-    grad = cotangent[...].astype(F32) + dot(picks, returned[...])
+    grad = cotangent[...].astype(F32) + dot(picks, returned[:, :width])
     low = grad.astype(BF)
     hidden = (right_dot(low, outer_weight[...]) * node_slope[...].astype(F32)).astype(BF)
     grad_aggregate[...] = right_dot(hidden, inner_weight[width:, :]).astype(BF)
@@ -207,7 +202,7 @@
     grad_message, grad_edges, grad_sources, back,
     spread,
 ):
-    edges, width = edge_slope.shape
+    edges, _ = edge_slope.shape
     rows = grad_aggregate.shape[0]
     extended = grad_sources.shape[0]
     group = CHUNK // LANES
@@ -240,7 +235,7 @@
     keep, give, partial,
     spread, extended,
 ):
-    rows, width = nodes.shape
+    rows, _ = nodes.shape
     for k in range(edge_target.shape[0]):
         spread[:, k * LANES : (k + 1) * LANES] = hot(iota((rows, LANES), 0) == edge_target[k : k + 1, :])
     targets = dot(spread[...], grad_edges[...]).astype(BF)
@@ -259,24 +254,9 @@
 
 
 def updated_kernel(refined, returned, slot, out):
-    picks = hot(wide_column(slot[...]) == iota((refined.shape[0], returned.shape[0]), 1))
-    out[...] = (refined[...].astype(F32) + dot(picks, returned[...])).astype(BF)
-
-
-def pair_kernel(first, second, out):
-    out[...] = (first[...].astype(F32) + second[...].astype(F32)).astype(BF)
-
-
-def total_kernel(arrived, out):
-    out[...] = jnp.sum(arrived[...].astype(F32), axis=0).astype(BF)
-
-
-def spread_kernel(early, arrived, out):
-    late = jnp.sum(arrived[...].astype(F32), axis=0).astype(BF)
-    rows = early.shape[0]
-    peers = out.shape[0]
-    out[:, :rows, :] = jnp.broadcast_to(early[...][None], (peers, rows, LANES))
-    out[:, rows:, :] = jnp.broadcast_to(late[None], (peers,) + late.shape)
+    rows, width = refined.shape
+    picks = hot(wide_column(slot[...]) == iota((rows, returned.shape[0]), 1))
+    out[...] = (refined[...].astype(F32) + dot(picks, returned[:, width:])).astype(BF)
 
 
 def results_kernel(early, core, mine, other, source, target, edge, inner, outer, coarse):
@@ -307,7 +287,6 @@
         out_shape=[jax.ShapeDtypeStruct(shape, dtype) for shape, dtype in outs],
         scratch_shapes=[pltpu.VMEM(shape, dtype) for shape, dtype in scratch],
         compiler_params=pltpu.CompilerParams(vmem_limit_bytes=60 * 2 ** 20),
-        name=kernel.__name__,
     )(*args)
 
 
@@ -319,10 +298,8 @@
 
 def trade_halo(blocks, flip):
     moved = []
-    for number, offset in enumerate((1, -1)):
-        moved.append(passed_along(blocks[number], ROW, offset * flip))
-    for number, offset in enumerate((1, -1)):
-        moved.append(passed_along(blocks[2 + number], COL, offset * flip))
+    for number, (axis, offset) in enumerate(((ROW, 1), (ROW, -1), (COL, 1), (COL, -1))):
+        moved.append(passed_along(blocks[number], axis, offset * flip))
     return moved
 
 
@@ -337,8 +314,16 @@
     return lax.ppermute(value, "core", [(0, 1), (1, 0)])
 
 
+def paired(keep, give):
+    return (keep.astype(F32) + across(give).astype(F32)).astype(BF)
+
+
 def trade_chips(value):
     return lax.all_to_all(value, CHIPS, split_axis=0, concat_axis=0, tiled=True)
+
+
+def total(arrived):
+    return jnp.sum(arrived.astype(F32), axis=0).astype(BF)
 
 
 def local(
@@ -397,32 +382,29 @@
         [((coarse_rows, slots), BF), ((coarse_rows, width), F32), ((coarse_rows, LANES), F32)],
         cot_arrived, table,
     )
-    share_sent, update, coarse, grad_coarse = call(
+    sent, coarse, grad_coarse = call(
         coarse_kernel,
-        [((slots, width), BF)] + [((coarse_rows, width), BF)] * 3,
+        [((slots, 2 * width), BF)] + [((coarse_rows, width), BF)] * 2,
         arrived, members, totals, counts, table, coarse_weight,
     )
-    share_returned = trade_slots(share_sent, devices)
-    (update_sent,) = call(coarse_rest_kernel, [((slots, width), BF)], update, table)
-    update_returned = trade_slots(update_sent, devices)
+    returned = trade_slots(sent, devices)
     grad_aggregate, base, keep, give = call(
         node_back_kernel,
         [(node_block, BF), (node_block, F32), ((4 * packed, LANES), BF), ((4 * packed, LANES), BF)],
-        share_returned, slot, cotangent, nodes, aggregate, node_hidden, node_slope, coarse, grad_coarse,
+        returned, slot, cotangent, nodes, aggregate, node_hidden, node_slope, coarse, grad_coarse,
         inner_weight, outer_weight,
         core=core, scale=scale,
     )
-    taken = across(give)
+    early = paired(keep, give)
     grad_message, grad_edges, grad_sources, back = call(
         edge_back_kernel,
         [(edge_block, BF), (edge_block, BF), ((extended, width), BF), ((4 * halo_rows, width), BF)],
         senders, receivers, grad_aggregate, edge_slope, message_slope, edge_weight, source_weight,
         scratch=[((extended, edges), BF)],
     )
-    (early,) = call(pair_kernel, [((4 * packed, LANES), BF)], keep, taken)
     early_rows = 4 * packed // chips
-    early = trade_chips(early.reshape(chips, early_rows, LANES))
-    returned = trade_halo([back[k * halo_rows : (k + 1) * halo_rows] for k in range(4)], -1)
+    early = total(trade_chips(early.reshape(chips, early_rows, LANES)))
+    halo_back = trade_halo([back[k * halo_rows : (k + 1) * halo_rows] for k in range(4)], -1)
     keep, give, partial = call(
         weights_kernel,
         [((3 * packed, LANES), BF), ((3 * packed, LANES), BF), (node_block, F32)],
@@ -431,14 +413,14 @@
         scratch=[((rows, edges), BF), ((extended, width), BF)],
         core=core, scale=scale,
     )
-    (late,) = call(pair_kernel, [((3 * packed, LANES), BF)], keep, across(give))
+    late = paired(keep, give)
     late_rows = 3 * packed // chips
-    late = trade_chips(late.reshape(chips, late_rows, LANES))
-    (early,) = call(total_kernel, [((early_rows, LANES), BF)], early)
-    (sent,) = call(spread_kernel, [((chips, early_rows + late_rows, LANES), BF)], early, late)
+    late = total(trade_chips(late.reshape(chips, late_rows, LANES)))
+    sent = jnp.concatenate([early, late], axis=0)
+    sent = jnp.broadcast_to(sent[None], (chips,) + sent.shape)
     mine = trade_chips(sent)
-    (node_gradient,) = call(node_gradient_kernel, [(node_block, F32)], partial, lists, *returned)
-    (updated,) = call(updated_kernel, [(node_block, BF)], refined, update_returned, slot)
+    (node_gradient,) = call(node_gradient_kernel, [(node_block, F32)], partial, lists, *halo_back)
+    (updated,) = call(updated_kernel, [(node_block, BF)], refined, returned, slot)
     results = call(
         results_kernel,
         [square, square, square, ((2 * width, width), F32), square, square],
@@ -467,4 +449,5 @@
         P(),
     )
     out_specs = (P(ALL, None), P(ALL, None), P(), P(), P(), P(), P(), P())
+
     return jax.shard_map(local, mesh=mesh, in_specs=in_specs, out_specs=out_specs, check_vma=False)

time: 251 us -> 247 us (0.984)
  waiting for transfers between devices: 64.6 us -> 79.3 us
  starting transfers between devices: 73.6 us -> 62.2 us
  Pallas kernels: 73.4 us -> 62.3 us
  other arithmetic: 0 us -> 3.79 us
    all_to_all x2, waiting for transfers between devices: 12.9 us -> 29.9 us  [trade_chips(): return lax.all_to_all(value, CHIPS, split_axis=0, concat_axis=0, tiled=True)]
    pallas_call x16 -> x11, Pallas kernels: 73.4 us -> 62.3 us  [call(): pl.pallas_call(body, in_specs=specs, out_shape=[jax.ShapeDtypeStruct(shap...]
    all_to_all x2, starting transfers between devices: 14.9 us -> 9.41 us  [trade_chips(): return lax.all_to_all(value, CHIPS, split_axis=0, concat_axis=0, tiled=True)]
    all_to_all x4 -> x3, starting transfers between devices: 32.7 us -> 28.4 us  [trade_slots(): moved = lax.all_to_all(shaped, ALL, split_axis=0, concat_axis=0, tiled=True)]
    convert_element_type x0 -> x2, other arithmetic: none -> 3.46 us  [paired(): return (keep.astype(F32) + across(give).astype(F32)).astype(BF)]
    all_to_all x4 -> x3, waiting for transfers between devices: 43.4 us -> 46.4 us  [trade_slots(): moved = lax.all_to_all(shaped, ALL, split_axis=0, concat_axis=0, tiled=True)]
    ppermute x8, waiting for transfers between devices: 3.64 us -> 0.97 us  [passed_along(): lax.ppermute(value, axis, [(source, source + steps) for source in range(i...]
    ppermute x3, waiting for transfers between devices: 4.62 us -> 2.04 us  [across(): return lax.ppermute(value, 'core', [(0, 1), (1, 0)])]
  transfers between devices with their start and end apart: 17 -> 16, of which waited for: 8 -> 7; matrix products, arithmetic and copies ran while one was open for 1% -> 2% of each run, Pallas kernels for 19% -> 10%
where the time goes in v3:
time: 247 us; the launch traced here: 244 us
  waiting for transfers between devices  79.3 us (32%)
  Pallas kernels  62.3 us (25%)
  starting transfers between devices  62.2 us (25%)
  blocking collectives  29.2 us (12%)
  local copies, waits for them, and re-layouts  6.55 us (3%)
  other arithmetic  3.79 us (2%)
    pallas_call x11, Pallas kernels, call(): pl.pallas_call(body, in_specs=specs, out_shape=[jax.ShapeDtypeStruct(shap...  62.3 us
    all_to_all x3, waiting for transfers between devices, trade_slots(): moved = lax.all_to_all(shaped, ALL, split_axis=0, concat_axis=0, tiled=True)  46.4 us
    all_to_all x2, waiting for transfers between devices, trade_chips(): return lax.all_to_all(value, CHIPS, split_axis=0, concat_axis=0, tiled=True)  29.9 us
    all_to_all x1, blocking collectives, trade_chips(): return lax.all_to_all(value, CHIPS, split_axis=0, concat_axis=0, tiled=True)  29.2 us
    all_to_all x3, starting transfers between devices, trade_slots(): moved = lax.all_to_all(shaped, ALL, split_axis=0, concat_axis=0, tiled=True)  28.4 us
    ppermute x8, starting transfers between devices, passed_along(): lax.ppermute(value, axis, [(source, source + steps) for source in range(i...  19.5 us
    all_to_all x2, starting transfers between devices, trade_chips(): return lax.all_to_all(value, CHIPS, split_axis=0, concat_axis=0, tiled=True)  9.41 us
  transfers between devices with their start and end apart: 16, of which 7 were waited for; matrix products, arithmetic and copies ran while one was open for 2% of the time, Pallas kernels for 10%

profile of v3, /device:TPU:1, one launch (start us, length us, event | category | flops | bytes accessed | tf_op | source)
XLA Modules:
  0.0 244.2 jit_solution(10297793420749183486)
XLA Ops:
  0.6 3.8 %shard_map.189 = (s32[1,512]{1,0:T(1,128)}, bf16[1024,512]{1,0:T(8,128)(2,1)}, bf16[512,512]{1,0:T(8,128)(2,1)}, bf16[512,512]{1,0:T(8,128)(2,1)}) custom-call(s32[4,128]{1,0:T(4,128)} %bitcast.27, bf16[512,512]{1,0:T(8,128)(2,1)} %cotangent.3, bf16[512,512]{1,0:T(8,128)(2,1)} %nodes.9, bf16[512,512]{1,0:T(8,128)(2,1)} %source_weight.7, ...), custom_call_target="tpu_custom_call" | custom-call | tf_op jit(solution)/shard_map/pallas_call | solution.py:284
  4.4 11.5 %all-to-all-start.1 = ((bf16[128,8,512]{2,1,0:T(8,128)(2,1)}), bf16[128,8,512]{2,1,0:T(8,128)(2,1)S(1)}, u32[]{:S(2)}, u32[]{:S(2)}) async-start(bf16[128,8,512]{2,1,0:T(8,128)(2,1)} %bitcast.18), calls=%async_computation.1 | async-start | bytes 2097152 | tf_op jit(solution)/shard_map/all_to_all | solution.py:309
  15.9 0.7 reshape.59.lists
  16.6 2.0 shard_map.188
  18.6 0.8 fusion.1
  19.4 1.3 collective-permute-start.3
  20.7 4.0 %collective-permute-start.2 = (bf16[32,512]{1,0:T(8,128)(2,1)S(1)}, bf16[32,512]{1,0:T(8,128)(2,1)S(1)}, u32[]{:S(2)}, u32[]{:S(2)}) collective-permute-start(bf16[32,512]{1,0:T(8,128)(2,1)S(1)} %get-tuple-element.83), channel_id=1, source_target_pairs={{0,1},{1,2},{2,3},{3,4},{4,5},{5,6},{6,7},{7,8},{8,9},{9,10},{10,1... | collective-permute-start | bytes 98312 | tf_op jit(solution)/shard_map/ppermute | solution.py:296
  24.7 3.5 %collective-permute-start.1 = (bf16[32,512]{1,0:T(8,128)(2,1)S(1)}, bf16[32,512]{1,0:T(8,128)(2,1)S(1)}, u32[]{:S(2)}, u32[]{:S(2)}) collective-permute-start(bf16[32,512]{1,0:T(8,128)(2,1)S(1)} %get-tuple-element.84), channel_id=1, source_target_pairs={{16,0},{32,16},{48,32},{64,48},{80,64},{96,80},{112,96},{17,1},{33... | collective-permute-start | bytes 98312 | tf_op jit(solution)/shard_map/ppermute | solution.py:296
  28.2 2.6 %collective-permute-start = (bf16[32,512]{1,0:T(8,128)(2,1)S(1)}, bf16[32,512]{1,0:T(8,128)(2,1)S(1)}, u32[]{:S(2)}, u32[]{:S(2)}) collective-permute-start(bf16[32,512]{1,0:T(8,128)(2,1)S(1)} %get-tuple-element.85), channel_id=1, source_target_pairs={{0,16},{16,32},{32,48},{48,64},{64,80},{80,96},{96,112},{1,17},{17... | collective-permute-start | bytes 98312 | tf_op jit(solution)/shard_map/ppermute | solution.py:296
  30.9 0.5 collective-permute-done.1.halo_1
  31.4 0.5 collective-permute-done.halo_0
  31.9 0.2 copy-done.8
  32.0 0.4 copy-done.9
  32.5 13.6 %shard_map.190 = (bf16[2048,512]{1,0:T(8,128)(2,1)}, bf16[2048,512]{1,0:T(8,128)(2,1)}, bf16[2048,512]{1,0:T(8,128)(2,1)}, bf16[512,512]{1,0:T(8,128)(2,1)}, bf1...) custom-call(bf16[32,512]{1,0:T(8,128)(2,1)} %copy-done.9, ...), custom_call_target="tpu_custom_call" | custom-call | tf_op jit(solution)/shard_map/pallas_call | solution.py:284
  46.1 12.2 %all-to-all-start = ((bf16[128,8,512]{2,1,0:T(8,128)(2,1)}), bf16[128,8,512]{2,1,0:T(8,128)(2,1)S(1)}, u32[]{:S(2)}, u32[]{:S(2)}) async-start(bf16[128,8,512]{2,1,0:T(8,128)(2,1)} %bitcast.19), calls=%async_computation | async-start | bytes 2097152 | tf_op jit(solution)/shard_map/all_to_all | solution.py:309
  58.3 2.3 shard_map.191
  60.6 16.5 %all-to-all-done = bf16[128,8,512]{2,1,0:T(8,128)(2,1)S(1)} async-done(((bf16[128,8,512]{2,1,0:T(8,128)(2,1)}), bf16[128,8,512]{2,1,0:T(8,128)(2,1)S(1)}, u32[]{:S(2)}, u32[]{:S(2)}) %all-to-all-start) | async-done | bytes 1048608 | tf_op jit(solution)/shard_map/all_to_all | solution.py:309
  77.2 1.0 copy-done.3
  78.1 4.3 %shard_map.192 = (bf16[1024,1024]{1,0:T(8,128)(2,1)}, bf16[128,512]{1,0:T(8,128)(2,1)}, bf16[128,512]{1,0:T(8,128)(2,1)}) custom-call(bf16[1024,512]{1,0:T(8,128)(2,1)} %bitcast.16, bf16[128,1024]{1,0:T(8,128)(2,1)} %get-tuple-element.49.members, f32[128,512]{1,0:T(8,128)} %get-tuple-element.50.totals, f32[128,128]{1,0:T(8,128)} %get-tuple-element.51.counts, ...), custom_call_target="tpu_custom_call" | custom-call | tf_op jit(solution)/shard_map/pallas_call | solution.py:284
  82.4 4.7 %all-to-all-start.2 = ((bf16[128,8,1024]{2,1,0:T(8,128)(2,1)}), bf16[128,8,1024]{2,1,0:T(8,128)(2,1)S(1)}, u32[]{:S(2)}, u32[]{:S(2)}) async-start(bf16[128,8,1024]{2,1,0:T(8,128)(2,1)} %bitcast.17), calls=%async_computation.2 | async-start | bytes 4194304 | tf_op jit(solution)/shard_map/all_to_all | solution.py:309
  87.2 29.9 %all-to-all-done.2 = bf16[128,8,1024]{2,1,0:T(8,128)(2,1)S(1)} async-done(((bf16[128,8,1024]{2,1,0:T(8,128)(2,1)}), bf16[128,8,1024]{2,1,0:T(8,128)(2,1)S(1)}, u32[]{:S(2)}, u32[]{:S(2)}) %all-to-all-start.2) | async-done | bytes 2097184 | tf_op jit(solution)/shard_map/all_to_all | solution.py:309
  117.0 1.4 copy-done
  118.4 6.9 %shard_map.194 = (bf16[512,512]{1,0:T(8,128)(2,1)}, f32[512,512]{1,0:T(8,128)}, bf16[4096,128]{1,0:T(8,128)(2,1)}, bf16[4096,128]{1,0:T(8,128)(2,1)}) custom-call(s32[1]{0:T(128)} %bitcast.10.core, bf16[1024,1024]{1,0:T(8,128)(2,1)} %bitcast.13, s32[1,512]{1,0:T(1,128)} %get-tuple-element.45.slot, bf16[512,512]{1,0:T(8,128)(2,1)} %cotangent.3, ...), custom_call_target="tpu_custom_call" | custom-call | tf_op jit(solution)/shard_map/pallas_call | solution.py:284
  125.3 9.5 %shard_map.195 = (bf16[2048,512]{1,0:T(8,128)(2,1)}, bf16[2048,512]{1,0:T(8,128)(2,1)}, bf16[640,512]{1,0:T(8,128)(2,1)}, bf16[128,512]{1,0:T(8,128)(2,1)}) custom-call(s32[16,128]{1,0:T(8,128)} %bitcast.24, s32[16,128]{1,0:T(8,128)} %bitcast.21, bf16[512,512]{1,0:T(8,128)(2,1)} %get-tuple-element.59.grad_aggregate, ...), custom_call_target="tpu_custom_call" | custom-call | tf_op jit(solution)/shard_map/pallas_call | solution.py:284
  134.7 8.3 %shard_map.196 = (bf16[3072,128]{1,0:T(8,128)(2,1)}, bf16[3072,128]{1,0:T(8,128)(2,1)}, f32[512,512]{1,0:T(8,128)}) custom-call(s32[1]{0:T(128)} %bitcast.10.core, s32[16,128]{1,0:T(8,128)} %bitcast.22, bf16[2048,512]{1,0:T(8,128)(2,1)} %get-tuple-element.53.edge_hidden, bf16[2048,512]{1,0:T(8,128)(2,1)} %get-tuple-element.62.grad_message, ...), custom_call_target="tpu_custom_call" | custom-call | tf_op jit(solution)/shard_map/pallas_call | solution.py:284
  143.1 1.1 collective-permute-start.9
  144.2 0.1 collective-permute-start.8
  144.2 2.0 collective-permute-done.9
  146.3 2.2 add_convert_fusion.1
  148.5 4.6 %all-to-all-start.4 = ((bf16[64,48,128]{2,1,0:T(8,128)(2,1)}), bf16[64,48,128]{2,1,0:T(8,128)(2,1)S(1)}, u32[]{:S(2)}, u32[]{:S(2)}) async-start(bf16[64,48,128]{2,1,0:T(8,128)(2,1)} %bitcast.12), calls=%async_computation.4 | async-start | bytes 1572864 | tf_op jit(solution)/shard_map/all_to_all | solution.py:322
  153.2 1.2 add_convert_fusion
  154.4 13.7 %all-to-all-done.4 = bf16[64,48,128]{2,1,0:T(8,128)(2,1)S(1)} async-done(((bf16[64,48,128]{2,1,0:T(8,128)(2,1)}), bf16[64,48,128]{2,1,0:T(8,128)(2,1)S(1)}, u32[]{:S(2)}, u32[]{:S(2)}) %all-to-all-start.4) | async-done | bytes 786464 | tf_op jit(solution)/shard_map/all_to_all | solution.py:322
  168.2 4.8 %all-to-all-start.3 = ((bf16[64,64,128]{2,1,0:T(8,128)(2,1)}), bf16[64,64,128]{2,1,0:T(8,128)(2,1)S(1)}, u32[]{:S(2)}, u32[]{:S(2)}) async-start(bf16[64,64,128]{2,1,0:T(8,128)(2,1)} %bitcast.11), calls=%async_computation.3 | async-start | bytes 2097152 | tf_op jit(solution)/shard_map/all_to_all | solution.py:322
  172.9 0.1 reduce_sum.25
  173.1 16.1 %all-to-all-done.3 = bf16[64,64,128]{2,1,0:T(8,128)(2,1)S(1)} async-done(((bf16[64,64,128]{2,1,0:T(8,128)(2,1)}), bf16[64,64,128]{2,1,0:T(8,128)(2,1)S(1)}, u32[]{:S(2)}, u32[]{:S(2)}) %all-to-all-start.3) | async-done | bytes 1048608 | tf_op jit(solution)/shard_map/all_to_all | solution.py:322
  189.2 0.2 reduce_sum.24
  189.4 0.2 broadcast_in_dim.2
  189.6 29.2 %all_to_all.30.mine = bf16[64,112,128]{2,1,0:T(8,128)(2,1)S(1)} all-to-all(bf16[64,112,128]{2,1,0:T(8,128)(2,1)S(1)} %broadcast_in_dim.2), channel_id=1, replica_groups=mesh['z'=4,'core'=2,'x'=4,'y'=4] {'z','x','y'}, dimensions={0} | all-to-all | bytes 3670016 | tf_op jit(solution)/shard_map/all_to_all | solution.py:322
  218.8 3.6 %collective-permute-start.10 = (bf16[64,112,128]{2,1,0:T(8,128)(2,1)S(1)}, bf16[64,112,128]{2,1,0:T(8,128)(2,1)S(1)}, u32[]{:S(2)}, u32[]{:S(2)}) collective-permute-start(bf16[64,112,128]{2,1,0:T(8,128)(2,1)S(1)} %all_to_all.30.mine), channel_id=1, source_target_pairs={{0,16},{16,0},{1,17},{17,1},{2,18},{18,2},{3,19},{19,3},{4,20},{20... | collective-permute-start | bytes 5505032 | tf_op jit(solution)/shard_map/ppermute | solution.py:314
  222.5 2.5 %collective-permute-start.7 = (bf16[32,512]{1,0:T(8,128)(2,1)S(1)}, bf16[32,512]{1,0:T(8,128)(2,1)S(1)}, u32[]{:S(2)}, u32[]{:S(2)}) collective-permute-start(bf16[32,512]{1,0:T(8,128)(2,1)S(1)} %get-tuple-element.78), channel_id=1, source_target_pairs={{0,1},{1,2},{2,3},{3,4},{4,5},{5,6},{6,7},{7,8},{8,9},{9,10},{10,1... | collective-permute-start | bytes 98312 | tf_op jit(solution)/shard_map/ppermute | solution.py:296
  225.0 1.3 collective-permute-start.6
  226.3 1.9 collective-permute-start.5
  228.2 2.4 collective-permute-start.4
  230.6 3.5 %shard_map.193 = bf16[512,512]{1,0:T(8,128)(2,1)} custom-call(bf16[512,512]{1,0:T(8,128)(2,1)} %get-tuple-element.46.refined, bf16[1024,1024]{1,0:T(8,128)(2,1)} %bitcast.14, s32[1,512]{1,0:T(1,128)} %get-tuple-element.45.slot), custom_call_target="tpu_custom_call" | custom-call | tf_op jit(solution)/shard_map/pallas_call | solution.py:284
  234.2 0.6 copy-done.11
  234.8 2.5 %shard_map.197 = f32[512,512]{1,0:T(8,128)} custom-call(f32[512,512]{1,0:T(8,128)} %get-tuple-element.66.partial, s32[1,128]{1,0:T(1,128)} %reshape.59.lists, bf16[32,512]{1,0:T(8,128)(2,1)} %copy-done.14, bf16[32,512]{1,0:T(8,128)(2,1)} %copy-done.13, bf16[32,512]{1,0:T(8,128)(2,1)} %copy-done.12, bf16[32,512]{1,0:T(8,128)(2,1)} %copy-done.11), custom_call_target="tpu_custom_call" | custom-call | tf_op jit(solution)/shard_map/pallas_call | solution.py:284
  237.3 1.3 copy-done.4
  238.5 5.7 %shard_map.198 = (f32[512,512]{1,0:T(8,128)}, f32[512,512]{1,0:T(8,128)}, f32[512,512]{1,0:T(8,128)}, f32[1024,512]{1,0:T(8,128)}, f32[512,512]{1,0:T(8,128)}, /*index=5*/f32[512,512]{1,0:T(8,128)}) custom-call(s32[1]{0:T(128)} %bitcast.10.core, bf16[64,112,128]{2,1,0:T(8,128)(2,1)} %copy-done.1, bf16[64,112,128]{2,1,0:T(8,128)(2,1)} %copy-done.4), custom_call_target="tpu_custom_call" | custom-call | tf_op jit(solution)/shard_map/pallas_call | solution.py:284
  (37 shorter events, 0.1 us)
Async XLA Ops:
  0.6 15.3 %copy-start.15 = (s32[1,4,32]{2,1,0:T(4,128)S(1)}, s32[1,4,32]{2,1,0:T(4,128)}, u32[]{:S(2)}) copy-start(s32[1,4,32]{2,1,0:T(4,128)} %param.17) | copy-start | bytes 1540
  4.4 41.7 %all-to-all-start.1 = ((bf16[128,8,512]{2,1,0:T(8,128)(2,1)}), bf16[128,8,512]{2,1,0:T(8,128)(2,1)S(1)}, u32[]{:S(2)}, u32[]{:S(2)}) async-start(bf16[128,8,512]{2,1,0:T(8,128)(2,1)} %bitcast.18), calls=%async_computation.1 | async-start | bytes 2097152 | tf_op jit(solution)/shard_map/all_to_all | solution.py:309
  19.4 11.5 %collective-permute-start.3 = (bf16[32,512]{1,0:T(8,128)(2,1)S(1)}, bf16[32,512]{1,0:T(8,128)(2,1)S(1)}, u32[]{:S(2)}, u32[]{:S(2)}) collective-permute-start(bf16[32,512]{1,0:T(8,128)(2,1)S(1)} %get-tuple-element.82), channel_id=1, source_target_pairs={{1,0},{2,1},{3,2},{4,3},{5,4},{6,5},{7,6},{8,7},{9,8},{10,9},{11,1... | collective-permute-start | bytes 98312 | tf_op jit(solution)/shard_map/ppermute | solution.py:296
  20.7 10.2 %collective-permute-start.2 = (bf16[32,512]{1,0:T(8,128)(2,1)S(1)}, bf16[32,512]{1,0:T(8,128)(2,1)S(1)}, u32[]{:S(2)}, u32[]{:S(2)}) collective-permute-start(bf16[32,512]{1,0:T(8,128)(2,1)S(1)} %get-tuple-element.83), channel_id=1, source_target_pairs={{0,1},{1,2},{2,3},{3,4},{4,5},{5,6},{6,7},{7,8},{8,9},{9,10},{10,1... | collective-permute-start | bytes 98312 | tf_op jit(solution)/shard_map/ppermute | solution.py:296
  24.7 6.7 %collective-permute-start.1 = (bf16[32,512]{1,0:T(8,128)(2,1)S(1)}, bf16[32,512]{1,0:T(8,128)(2,1)S(1)}, u32[]{:S(2)}, u32[]{:S(2)}) collective-permute-start(bf16[32,512]{1,0:T(8,128)(2,1)S(1)} %get-tuple-element.84), channel_id=1, source_target_pairs={{16,0},{32,16},{48,32},{64,48},{80,64},{96,80},{112,96},{17,1},{33... | collective-permute-start | bytes 98312 | tf_op jit(solution)/shard_map/ppermute | solution.py:296
  28.2 3.6 %collective-permute-start = (bf16[32,512]{1,0:T(8,128)(2,1)S(1)}, bf16[32,512]{1,0:T(8,128)(2,1)S(1)}, u32[]{:S(2)}, u32[]{:S(2)}) collective-permute-start(bf16[32,512]{1,0:T(8,128)(2,1)S(1)} %get-tuple-element.85), channel_id=1, source_target_pairs={{0,16},{16,32},{32,48},{48,64},{64,80},{80,96},{96,112},{1,17},{17... | collective-permute-start | bytes 98312 | tf_op jit(solution)/shard_map/ppermute | solution.py:296
  30.9 1.0 copy-start.6
  30.9 1.0 copy-start.7
  31.4 0.6 copy-start.8
  31.9 0.6 copy-start.9
  46.1 12.2 %copy-start.2 = (bf16[128,8,512]{2,1,0:T(8,128)(2,1)}, bf16[128,8,512]{2,1,0:T(8,128)(2,1)S(1)}, u32[]{:S(2)}) copy-start(bf16[128,8,512]{2,1,0:T(8,128)(2,1)S(1)} %all-to-all-done.1) | copy-start | bytes 3145732
  46.1 31.1 %all-to-all-start = ((bf16[128,8,512]{2,1,0:T(8,128)(2,1)}), bf16[128,8,512]{2,1,0:T(8,128)(2,1)S(1)}, u32[]{:S(2)}, u32[]{:S(2)}) async-start(bf16[128,8,512]{2,1,0:T(8,128)(2,1)} %bitcast.19), calls=%async_computation | async-start | bytes 2097152 | tf_op jit(solution)/shard_map/all_to_all | solution.py:309
  77.2 1.0 copy-start.3
  82.4 34.6 %all-to-all-start.2 = ((bf16[128,8,1024]{2,1,0:T(8,128)(2,1)}), bf16[128,8,1024]{2,1,0:T(8,128)(2,1)S(1)}, u32[]{:S(2)}, u32[]{:S(2)}) async-start(bf16[128,8,1024]{2,1,0:T(8,128)(2,1)} %bitcast.17), calls=%async_computation.2 | async-start | bytes 4194304 | tf_op jit(solution)/shard_map/all_to_all | solution.py:309
  117.0 1.4 copy-start
  143.1 10.1 %copy-start.5 = (bf16[4096,128]{1,0:T(8,128)(2,1)S(1)}, bf16[4096,128]{1,0:T(8,128)(2,1)}, u32[]{:S(2)}) copy-start(bf16[4096,128]{1,0:T(8,128)(2,1)} %get-tuple-element.68) | copy-start | bytes 3145732
  143.1 3.2 %collective-permute-start.9 = (bf16[3072,128]{1,0:T(8,128)(2,1)}, bf16[3072,128]{1,0:T(8,128)(2,1)S(1)}, u32[]{:S(2)}, u32[]{:S(2)}) collective-permute-start(bf16[3072,128]{1,0:T(8,128)(2,1)} %get-tuple-element.71), channel_id=1, source_target_pairs={{0,16},{16,0},{1,17},{17,1},{2,18},{18,2},{3,19},{19,3},{4,20},{20... | collective-permute-start | bytes 2359304 | tf_op jit(solution)/shard_map/ppermute | solution.py:314
  144.2 9.0 %collective-permute-start.8 = (bf16[4096,128]{1,0:T(8,128)(2,1)}, bf16[4096,128]{1,0:T(8,128)(2,1)S(1)}, u32[]{:S(2)}, u32[]{:S(2)}) collective-permute-start(bf16[4096,128]{1,0:T(8,128)(2,1)} %get-tuple-element.69), channel_id=1, source_target_pairs={{0,16},{16,0},{1,17},{17,1},{2,18},{18,2},{3,19},{19,3},{4,20},{20... | collective-permute-start | bytes 3145736 | tf_op jit(solution)/shard_map/ppermute | solution.py:314
  148.5 19.7 %all-to-all-start.4 = ((bf16[64,48,128]{2,1,0:T(8,128)(2,1)}), bf16[64,48,128]{2,1,0:T(8,128)(2,1)S(1)}, u32[]{:S(2)}, u32[]{:S(2)}) async-start(bf16[64,48,128]{2,1,0:T(8,128)(2,1)} %bitcast.12), calls=%async_computation.4 | async-start | bytes 1572864 | tf_op jit(solution)/shard_map/all_to_all | solution.py:322
  168.2 21.0 %all-to-all-start.3 = ((bf16[64,64,128]{2,1,0:T(8,128)(2,1)}), bf16[64,64,128]{2,1,0:T(8,128)(2,1)S(1)}, u32[]{:S(2)}, u32[]{:S(2)}) async-start(bf16[64,64,128]{2,1,0:T(8,128)(2,1)} %bitcast.11), calls=%async_computation.3 | async-start | bytes 2097152 | tf_op jit(solution)/shard_map/all_to_all | solution.py:322
  189.6 32.8 %copy-start.10 = (bf16[128,512]{1,0:T(8,128)(2,1)S(1)}, bf16[128,512]{1,0:T(8,128)(2,1)}, u32[]{:S(2)}) copy-start(bf16[128,512]{1,0:T(8,128)(2,1)} %get-tuple-element.67) | copy-start | bytes 393220
  218.8 18.4 %copy-start.1 = (bf16[64,112,128]{2,1,0:T(8,128)(2,1)}, bf16[64,112,128]{2,1,0:T(8,128)(2,1)S(1)}, u32[]{:S(2)}) copy-start(bf16[64,112,128]{2,1,0:T(8,128)(2,1)S(1)} %all_to_all.30.mine) | copy-start | bytes 5505028
  218.8 18.4 %collective-permute-start.10 = (bf16[64,112,128]{2,1,0:T(8,128)(2,1)S(1)}, bf16[64,112,128]{2,1,0:T(8,128)(2,1)S(1)}, u32[]{:S(2)}, u32[]{:S(2)}) collective-permute-start(bf16[64,112,128]{2,1,0:T(8,128)(2,1)S(1)} %all_to_all.30.mine), channel_id=1, source_target_pairs={{0,16},{16,0},{1,17},{17,1},{2,18},{18,2},{3,19},{19,3},{4,20},{20... | collective-permute-start | bytes 5505032 | tf_op jit(solution)/shard_map/ppermute | solution.py:314
  222.5 11.6 %collective-permute-start.7 = (bf16[32,512]{1,0:T(8,128)(2,1)S(1)}, bf16[32,512]{1,0:T(8,128)(2,1)S(1)}, u32[]{:S(2)}, u32[]{:S(2)}) collective-permute-start(bf16[32,512]{1,0:T(8,128)(2,1)S(1)} %get-tuple-element.78), channel_id=1, source_target_pairs={{0,1},{1,2},{2,3},{3,4},{4,5},{5,6},{6,7},{7,8},{8,9},{9,10},{10,1... | collective-permute-start | bytes 98312 | tf_op jit(solution)/shard_map/ppermute | solution.py:296
  225.0 9.1 %collective-permute-start.6 = (bf16[32,512]{1,0:T(8,128)(2,1)S(1)}, bf16[32,512]{1,0:T(8,128)(2,1)S(1)}, u32[]{:S(2)}, u32[]{:S(2)}) collective-permute-start(bf16[32,512]{1,0:T(8,128)(2,1)S(1)} %get-tuple-element.79), channel_id=1, source_target_pairs={{1,0},{2,1},{3,2},{4,3},{5,4},{6,5},{7,6},{8,7},{9,8},{10,9},{11,1... | collective-permute-start | bytes 98312 | tf_op jit(solution)/shard_map/ppermute | solution.py:296
  226.3 7.8 %collective-permute-start.5 = (bf16[32,512]{1,0:T(8,128)(2,1)S(1)}, bf16[32,512]{1,0:T(8,128)(2,1)S(1)}, u32[]{:S(2)}, u32[]{:S(2)}) collective-permute-start(bf16[32,512]{1,0:T(8,128)(2,1)S(1)} %get-tuple-element.80), channel_id=1, source_target_pairs={{0,16},{16,32},{32,48},{48,64},{64,80},{80,96},{96,112},{1,17},{17... | collective-permute-start | bytes 98312 | tf_op jit(solution)/shard_map/ppermute | solution.py:296
  228.2 5.9 %collective-permute-start.4 = (bf16[32,512]{1,0:T(8,128)(2,1)S(1)}, bf16[32,512]{1,0:T(8,128)(2,1)S(1)}, u32[]{:S(2)}, u32[]{:S(2)}) collective-permute-start(bf16[32,512]{1,0:T(8,128)(2,1)S(1)} %get-tuple-element.81), channel_id=1, source_target_pairs={{16,0},{32,16},{48,32},{64,48},{80,64},{96,80},{112,96},{17,1},{33... | collective-permute-start | bytes 98312 | tf_op jit(solution)/shard_map/ppermute | solution.py:296
  234.1 0.6 copy-start.11
  234.1 0.6 copy-start.12
  234.1 0.6 copy-start.13
  234.1 0.6 copy-start.14
  237.3 1.3 copy-start.4

commit v4 on v3

v4 whole, which is shorter than its diff:
```python
import functools
import math

import jax
import jax.numpy as jnp
from jax import lax
from jax.experimental import pallas as pl
from jax.experimental.pallas import tpu as pltpu
from jax.sharding import Mesh
from jax.sharding import PartitionSpec as P


BF = jnp.bfloat16
F32 = jnp.float32
LANES = 128
CHUNK = 512
CAPACITY = 8
ROW = ("z", "core")
COL = ("x", "y")
CHIPS = ("z", "x", "y")
ALL = ROW + COL


def dot(first, second):
    return jnp.dot(first, second, preferred_element_type=F32)


def left_dot(first, second):
    return lax.dot_general(
        first, second, (((0,), (0,)), ((), ())), preferred_element_type=F32
    )


def right_dot(first, second):
    return lax.dot_general(
        first, second, (((1,), (1,)), ((), ())), preferred_element_type=F32
    )


def iota(shape, axis):
    return lax.broadcasted_iota(jnp.int32, shape, axis)


def column(row):
    square = (LANES, LANES)
    eye = iota(square, 0) == iota(square, 1)
    spread = jnp.broadcast_to(row.astype(F32), square)
    return jnp.sum(jnp.where(eye, spread, 0.0), axis=1, keepdims=True).astype(jnp.int32)


def hot(mask):
    return jnp.where(mask, 1.0, 0.0).astype(BF)


def wide_column(row):
    return jnp.concatenate(
        [column(row[:, k : k + LANES]) for k in range(0, row.shape[1], LANES)], axis=0
    )


def wide_row(ref):
    return jnp.concatenate([ref[k : k + 1, :] for k in range(ref.shape[0])], axis=1)


def gates(value):
    sigma = 0.5 * jnp.tanh(0.5 * value) + 0.5
    active = value * sigma
    return active, sigma + active * (1.0 - sigma)


def halo_kernel(nodes, lists, out):
    picks = hot(column(lists[...]) == iota((LANES, nodes.shape[0]), 1))
    out[...] = dot(picks, nodes[...]).astype(BF)


def prepare_kernel(owner, nodes, source_weight, target_weight, slot_out, own_source, target_side):
    rows = nodes.shape[0]
    owner_row = wide_row(owner)
    owner_column = wide_column(owner_row)
    square = (rows, rows)
    before = (owner_column == owner_row) & (iota(square, 0) < iota(square, 1))
    rank = jnp.sum(jnp.where(before, 1.0, 0.0), axis=0, keepdims=True).astype(jnp.int32)
    slot_out[...] = owner_row * CAPACITY + rank
    own_source[...] = dot(nodes[...], source_weight[...]).astype(BF)
    target_side[...] = dot(nodes[...], target_weight[...]).astype(BF)


def chunk(turn):
    return slice(turn * CHUNK, (turn + 1) * CHUNK)


def forward_kernel(
    halo_0, halo_1, halo_2, halo_3, own_source, target_side, nodes, cotangent, edge_source, edge_target, slot,
    source_weight, edge_weight, inner_far, outer_far,
    edge_hidden, edge_slope, message_slope, aggregate, node_hidden, node_slope, refined, sent,
    sides, active, spread, inner_weight, outer_weight, hidden_kept, slope_kept, message_kept, weight_sems, sems,
):
    fetches = [
        pltpu.make_async_copy(inner_far, inner_weight, weight_sems.at[0]),
        pltpu.make_async_copy(outer_far, outer_weight, weight_sems.at[1]),
    ]
    for fetch in fetches:
        fetch.start()
    rows, width = nodes.shape
    extended = rows + LANES
    edges = hidden_kept.shape[0]
    sides[:rows, :] = own_source[...]
    halo = jnp.concatenate([halo_0[...], halo_1[...], halo_2[...], halo_3[...]], axis=0)
    sides[rows:extended, :] = dot(halo, source_weight[...]).astype(BF)
    sides[extended:, :] = target_side[...]
    group = CHUNK // LANES
    stores = []
    for turn in range(edges // CHUNK):
        span = chunk(turn)
        picks = []
        for at in range(turn * group, (turn + 1) * group):
            senders = edge_source[at : at + 1, :]
            receivers = edge_target[at : at + 1, :]
            sender_hot = hot(column(senders) == iota((LANES, extended), 1))
            receiver_hot = hot(column(receivers) == iota((LANES, rows), 1))
            picks.append(jnp.concatenate([sender_hot, receiver_hot], axis=1))
            spread[:, at * LANES : (at + 1) * LANES] = hot(iota((rows, LANES), 0) == receivers)
        hidden, slope = gates(dot(jnp.concatenate(picks, axis=0), sides[...]))
        hidden = hidden.astype(BF)
        hidden_kept[span, :] = hidden
        slope_kept[span, :] = slope.astype(BF)
        message, slope = gates(dot(hidden, edge_weight[...]))
        active[span, :] = message.astype(BF)
        message_kept[span, :] = slope.astype(BF)
        pairs = ((hidden_kept, edge_hidden), (slope_kept, edge_slope), (message_kept, message_slope))
        for number, (kept, out) in enumerate(pairs):
            stores.append(pltpu.make_async_copy(kept.at[span, :], out.at[span, :], sems.at[number, turn]))
            stores[-1].start()
    gathered = dot(spread[...], active[...]).astype(BF)
    aggregate[...] = gathered
    for fetch in fetches:
        fetch.wait()
    linear = dot(nodes[...], inner_weight[:width, :]) + dot(gathered, inner_weight[width:, :])
    hidden, slope = gates(linear)
    hidden = hidden.astype(BF)
    node_hidden[...] = hidden
    node_slope[...] = slope.astype(BF)
    result = (nodes[...].astype(F32) + dot(hidden, outer_weight[...])).astype(BF)
    refined[...] = result
    place = hot(iota((sent.shape[0], rows), 0) == slot[...])
    sent[:, :width] = dot(place, result).astype(BF)
    sent[:, width:] = dot(place, cotangent[...]).astype(BF)
    for store in stores:
        store.wait()


def members_kernel(table, members, picks, counts):
    coarse = members.shape[0]
    row = wide_row(table)
    inside = iota((coarse, row.shape[1]), 0) == row
    ones = jnp.where(inside, 1.0, 0.0)
    members[...] = ones.astype(BF)
    count = jnp.maximum(jnp.sum(ones, axis=1, keepdims=True), 1.0)
    counts[...] = jnp.broadcast_to(count, counts.shape)
    picks[...] = hot(wide_column(row) == iota((row.shape[1], coarse), 1))


def coarse_kernel(arrived, members, picks, counts, weight, out, coarse_out, grad_out):
    width = weight.shape[0]
    count = counts[:, :1]
    totals = dot(members[...], arrived[...])
    coarse = (totals[:, :width] / count).astype(BF)
    coarse_out[...] = coarse
    active, slope = gates(dot(coarse, weight[...]))
    grad = (totals[:, width:] * slope).astype(BF)
    grad_out[...] = grad
    share = (right_dot(grad, weight[...]) / count).astype(BF)
    out[:, :width] = dot(picks[...], share).astype(BF)
    out[:, width:] = dot(picks[...], active.astype(BF)).astype(BF)


def half_of(ref, half):
    columns = ref.shape[1] // 2
    return ref[:, pl.ds(pl.multiple_of(half * columns, columns), columns)]


def pack(out, at, value):
    rows, width = value.shape
    for k in range(width // LANES):
        out[at * width // LANES + k * rows : at * width // LANES + (k + 1) * rows, :] = value[
            :, k * LANES : (k + 1) * LANES
        ].astype(BF)


def halves(scale, core, keep, give, pairs):
    at = 0
    for first, second in pairs:
        for out, half in ((keep, core[0]), (give, 1 - core[0])):
            pack(out, at, left_dot(half_of(first, half), second) * scale)
        at += first.shape[1] // 2


def node_back_kernel(
    scale, core, returned, slot, cotangent, nodes, aggregate, node_hidden, node_slope, coarse, grad_coarse,
    inner_weight, outer_weight,
    grad_aggregate, grad_hidden, keep, give,
):
    rows, width = nodes.shape
    picks = hot(wide_column(slot[...]) == iota((rows, returned.shape[0]), 1))
    grad = cotangent[...].astype(F32) + dot(picks, returned[:, :width])
    low = grad.astype(BF)
    hidden = (right_dot(low, outer_weight[...]) * node_slope[...].astype(F32)).astype(BF)
    grad_hidden[...] = hidden
    grad_aggregate[...] = right_dot(hidden, inner_weight[width:, :]).astype(BF)
    pairs = ((node_hidden, low), (nodes, hidden), (aggregate, hidden), (coarse, grad_coarse[...]))
    halves(scale, core, keep, give, pairs)


def edge_back_kernel(
    scale, core, edge_source, edge_target, grad_aggregate, halo_0, halo_1, halo_2, halo_3, nodes, edge_weight,
    source_weight, edge_slope, message_slope, edge_hidden,
    keep, give, grad_sources, grad_targets, back,
    slope_kept, message_kept, hidden_kept, grad_message, grad_edges, source_spread, target_spread, extended, sems,
):
    rows, _ = nodes.shape
    table = grad_sources.shape[0]
    edges = slope_kept.shape[0]
    turns = edges // CHUNK
    group = CHUNK // LANES
    fetches = []
    for turn in range(turns):
        span = chunk(turn)
        for number, (far, kept) in enumerate(((message_slope, message_kept), (edge_slope, slope_kept))):
            fetches.append(pltpu.make_async_copy(far.at[span, :], kept.at[span, :], sems.at[number, turn]))
    fetches.append(pltpu.make_async_copy(edge_hidden, hidden_kept, sems.at[2, 0]))
    for fetch in fetches:
        fetch.start()
    extended[:rows, :] = nodes[...]
    extended[rows:, :] = jnp.concatenate([halo_0[...], halo_1[...], halo_2[...], halo_3[...]], axis=0)
    for turn in range(turns):
        span = chunk(turn)
        picks = []
        for at in range(turn * group, (turn + 1) * group):
            senders = edge_source[at : at + 1, :]
            receivers = edge_target[at : at + 1, :]
            lanes = slice(at * LANES, (at + 1) * LANES)
            picks.append(hot(column(receivers) == iota((LANES, rows), 1)))
            source_spread[:, lanes] = hot(iota((table, LANES), 0) == senders)
            target_spread[:, lanes] = hot(iota((rows, LANES), 0) == receivers)
        taken = dot(jnp.concatenate(picks, axis=0), grad_aggregate[...])
        fetches[2 * turn].wait()
        message = (taken * message_kept[span, :].astype(F32)).astype(BF)
        grad_message[span, :] = message
        fetches[2 * turn + 1].wait()
        grad = right_dot(message, edge_weight[...]) * slope_kept[span, :].astype(F32)
        grad_edges[span, :] = grad.astype(BF)
    sources = dot(source_spread[...], grad_edges[...]).astype(BF)
    targets = dot(target_spread[...], grad_edges[...]).astype(BF)
    grad_sources[...] = sources
    grad_targets[...] = targets
    back[...] = right_dot(sources[rows:, :], source_weight[...]).astype(BF)
    fetches[-1].wait()
    pairs = ((hidden_kept, grad_message[...]), (extended, sources), (nodes, targets))
    halves(scale, core, keep, give, pairs)


def finish_kernel(
    returned, slot, cotangent, refined, grad_hidden, grad_sources, grad_targets, lists,
    back_0, back_1, back_2, back_3, inner_weight, source_weight, target_weight,
    updated, node_gradient,
):
    rows, width = refined.shape
    picks = hot(wide_column(slot[...]) == iota((rows, returned.shape[0]), 1))
    updated[...] = (refined[...].astype(F32) + dot(picks, returned[:, width:])).astype(BF)
    back = jnp.concatenate([back_0[...], back_1[...], back_2[...], back_3[...]], axis=0)
    places = hot(iota((rows, LANES), 0) == lists[...])
    node_gradient[...] = (
        cotangent[...].astype(F32)
        + dot(picks, returned[:, :width])
        + right_dot(grad_hidden[...], inner_weight[:width, :])
        + right_dot(grad_targets[...], target_weight[...])
        + right_dot(grad_sources[:rows, :], source_weight[...])
        + dot(places, back)
    )


def results_kernel(early, other, core, gathered, *refs):
    outs, wide, sems = refs[-8:-2], refs[-2], refs[-1]
    source, target, edge, inner, outer, coarse = outs
    which = 1 - core[0] if other else core[0]
    width = wide.shape[1]
    half = width // 2
    blocks = width // LANES
    peers, rows, lanes = gathered.shape
    first = gathered[:, :early, :].astype(F32).reshape(peers * early, lanes)
    second = gathered[:, early:, :].astype(F32).reshape(peers * (rows - early), lanes)
    places = ((outer, 0, first, 0), (inner, 0, first, 1), (inner, width, first, 2), (coarse, 0, first, 3))
    places += ((edge, 0, second, 0), (source, 0, second, 1), (target, 0, second, 2))
    stores = []
    for number, (out, base, values, at) in enumerate(places):
        own = slice(number * half, (number + 1) * half)
        for k in range(blocks):
            start = (at * blocks + k) * half
            wide[own, k * LANES : (k + 1) * LANES] = values[start : start + half, :]
        span = pl.ds(pl.multiple_of(base + which * half, half), half)
        stores.append(pltpu.make_async_copy(wide.at[own, :], out.at[span, :], sems.at[number]))
        stores[-1].start()
    for store in stores:
        store.wait()


def call(kernel, outs, *args, far_in=0, far_out=0, scratch=(), sems=(), core=None, aliases=0, **static):
    body = functools.partial(kernel, *static.values())
    near, far = pl.BlockSpec(memory_space=pltpu.VMEM), pl.BlockSpec(memory_space=pl.ANY)
    specs = [near] * (len(args) - far_in) + [far] * far_in
    if core is not None:
        args, specs = (core,) + args, [pl.BlockSpec(memory_space=pltpu.SMEM)] + specs
    return pl.pallas_call(
        body,
        in_specs=specs,
        out_specs=[far] * far_out + [near] * (len(outs) - far_out),
        out_shape=[jax.ShapeDtypeStruct(shape, dtype) for shape, dtype in outs],
        scratch_shapes=[pltpu.VMEM(shape, dtype) for shape, dtype in scratch]
        + [pltpu.SemaphoreType.DMA(shape) for shape in sems],
        compiler_params=pltpu.CompilerParams(vmem_limit_bytes=60 * 2 ** 20),
        input_output_aliases={len(args) - aliases + k: k for k in range(aliases)},
    )(*args)


def passed_along(value, axis, steps):
    count = math.prod(lax.axis_size(name) for name in axis)
    initial, last = (max(0, -steps), min(count, count - steps))
    return lax.ppermute(value, axis, [(source, source + steps) for source in range(initial, last)])


def trade_halo(blocks, flip):
    moved = []
    for number, (axis, offset) in enumerate(((ROW, 1), (ROW, -1), (COL, 1), (COL, -1))):
        moved.append(passed_along(blocks[number], axis, offset * flip))
    return moved


def trade_slots(buffer, devices):
    slots, width = buffer.shape
    shaped = buffer.reshape(devices, slots // devices, width)
    moved = lax.all_to_all(shaped, ALL, split_axis=0, concat_axis=0, tiled=True)
    return moved.reshape(slots, width)


def across(value):
    return lax.ppermute(value, "core", [(0, 1), (1, 0)])


def paired(keep, give):
    return (keep.astype(F32) + across(give).astype(F32)).astype(BF)


def trade_chips(value):
    return lax.all_to_all(value, CHIPS, split_axis=0, concat_axis=0, tiled=True)


def total(arrived):
    return jnp.sum(arrived.astype(F32), axis=0).astype(BF)


def local(
    nodes,
    cotangent,
    edge_source,
    edge_target,
    halo_lists,
    pool_owner,
    pool_table,
    source_weight,
    target_weight,
    edge_weight,
    inner_weight,
    outer_weight,
    coarse_weight,
):
    chips = math.prod(lax.axis_size(name) for name in CHIPS)
    devices = 2 * chips
    core = lax.axis_index("core").reshape(1)
    rows, width = nodes.shape
    edges = edge_source.shape[0]
    halo_rows = halo_lists.shape[2]
    extended = rows + 4 * halo_rows
    slots = pool_table.shape[1]
    coarse_rows = rows // 4
    scale = 1.0 / math.sqrt(rows * devices)
    lists = halo_lists.reshape(1, 4 * halo_rows)
    owner = pool_owner.reshape(rows // LANES, LANES)
    table = pool_table.reshape(slots // LANES, LANES)
    senders = edge_source.reshape(edges // LANES, LANES)
    receivers = edge_target.reshape(edges // LANES, LANES)
    node_block, edge_block = (rows, width), (edges, width)
    square = ((width, width), F32)
    packed = width // 2 * width // LANES

    (halo_sent,) = call(halo_kernel, [((4 * halo_rows, width), BF)], nodes, lists)
    sent_blocks = [halo_sent[k * halo_rows : (k + 1) * halo_rows] for k in range(4)]
    halo = trade_halo(sent_blocks, 1)
    slot, own_source, target_side = call(
        prepare_kernel,
        [((1, rows), jnp.int32), (node_block, BF), (node_block, BF)],
        owner, nodes, source_weight, target_weight,
    )
    edge_hidden, edge_slope, message_slope, aggregate, node_hidden, node_slope, refined, sent = call(
        forward_kernel,
        [(edge_block, BF)] * 3 + [(node_block, BF)] * 4 + [((slots, 2 * width), BF)],
        *halo, own_source, target_side, nodes, cotangent, senders, receivers, slot,
        source_weight, edge_weight, inner_weight, outer_weight,
        far_in=2, far_out=3,
        scratch=[((extended + rows, width), BF), (edge_block, BF), ((rows, edges), BF)]
        + [((2 * width, width), BF), ((width, width), BF)] + [(edge_block, BF)] * 3,
        sems=[(2,), (3, edges // CHUNK)],
    )
    arrived = trade_slots(sent, devices)
    members, picks, counts = call(
        members_kernel,
        [((coarse_rows, slots), BF), ((slots, coarse_rows), BF), ((coarse_rows, LANES), F32)],
        table,
    )
    sent, coarse, grad_coarse = call(
        coarse_kernel,
        [((slots, 2 * width), BF)] + [((coarse_rows, width), BF)] * 2,
        arrived, members, picks, counts, coarse_weight,
    )
    returned = trade_slots(sent, devices)
    grad_aggregate, grad_hidden, keep, give = call(
        node_back_kernel,
        [(node_block, BF), (node_block, BF), ((4 * packed, LANES), BF), ((4 * packed, LANES), BF)],
        returned, slot, cotangent, nodes, aggregate, node_hidden, node_slope, coarse, grad_coarse,
        inner_weight, outer_weight,
        core=core, scale=scale,
    )
    early = paired(keep, give)
    early_rows = 4 * packed // chips
    early = total(trade_chips(early.reshape(chips, early_rows, LANES)))
    keep, give, grad_sources, grad_targets, back = call(
        edge_back_kernel,
        [((3 * packed, LANES), BF)] * 2 + [((extended, width), BF), (node_block, BF), ((4 * halo_rows, width), BF)],
        senders, receivers, grad_aggregate, *halo, nodes, edge_weight, source_weight,
        edge_slope, message_slope, edge_hidden,
        far_in=3,
        scratch=[(edge_block, BF)] * 5 + [((extended, edges), BF), ((rows, edges), BF), ((extended, width), BF)],
        sems=[(3, edges // CHUNK)],
        core=core, scale=scale,
    )
    halo_back = trade_halo([back[k * halo_rows : (k + 1) * halo_rows] for k in range(4)], -1)
    late = paired(keep, give)
    late_rows = 3 * packed // chips
    late = total(trade_chips(late.reshape(chips, late_rows, LANES)))
    sent = jnp.concatenate([early, late], axis=0)
    sent = jnp.broadcast_to(sent[None], (chips,) + sent.shape)
    mine = trade_chips(sent)
    updated, node_gradient = call(
        finish_kernel,
        [(node_block, BF), (node_block, F32)],
        returned, slot, cotangent, refined, grad_hidden, grad_sources, grad_targets, lists, *halo_back,
        inner_weight, source_weight, target_weight,
    )
    shapes = [square, square, square, ((2 * width, width), F32), square, square]
    buffers = {"scratch": [((7 * width // 2, width), F32)], "sems": [(7,)], "far_out": 6, "core": core}
    results = call(results_kernel, shapes, mine, **buffers, early=early_rows, other=False)
    results = call(
        results_kernel, shapes, across(mine), *results, far_in=6, aliases=6,
        **buffers, early=early_rows, other=True,
    )
    return (updated, node_gradient, *results)


def solution(mesh):
    whole = mesh.devices.reshape(mesh.shape["row"] // 2, 2, -1, 4)
    mesh = Mesh(whole, ALL)
    in_specs = (
        P(ALL, None),
        P(ALL, None),
        P(ALL),
        P(ALL),
        P(ALL, None, None),
        P(ALL),
        P(ALL, None),
        P(),
        P(),
        P(),
        P(),
        P(),
        P(),
    )
    out_specs = (P(ALL, None), P(ALL, None), P(), P(), P(), P(), P(), P())

    return jax.shard_map(local, mesh=mesh, in_specs=in_specs, out_specs=out_specs, check_vma=False)
```

time: 247 us -> 246 us (level)
  waiting for transfers between devices: 79.3 us -> 92.4 us
  starting transfers between devices: 62.2 us -> 51.4 us
  Pallas kernels: 62.3 us -> 57.7 us
    all_to_all x3 -> x2, starting transfers between devices: 28.4 us -> 16.1 us  [trade_slots(): moved = lax.all_to_all(shaped, ALL, split_axis=0, concat_axis=0, tiled=True)]
    all_to_all x3 -> x2, waiting for transfers between devices: 46.4 us -> 57.7 us  [trade_slots(): moved = lax.all_to_all(shaped, ALL, split_axis=0, concat_axis=0, tiled=True)]
    pallas_call x11 -> x10, Pallas kernels: 62.3 us -> 57.7 us  [call(): pl.pallas_call(body, in_specs=specs, out_specs=[far] * far_out + [near] *...]
    unnamed x32 -> x28, local copies, waits for them, and re-layouts: 4.82 us -> 5.25 us
  transfers between devices with their start and end apart: 16 -> 15, of which waited for: 7 -> 6; matrix products, arithmetic and copies ran while one was open for 2% -> 1% of each run, Pallas kernels for 10% -> 6%
where the time goes in v4:
time: 246 us; the launch traced here: 243 us
  waiting for transfers between devices  92.4 us (38%)
  Pallas kernels  57.7 us (23%)
  starting transfers between devices  51.4 us (21%)
  blocking collectives  29.2 us (12%)
  local copies, waits for them, and re-layouts  7.59 us (3%)
  other arithmetic  3.79 us (2%)
    all_to_all x2, waiting for transfers between devices, trade_slots(): moved = lax.all_to_all(shaped, ALL, split_axis=0, concat_axis=0, tiled=True)  57.7 us
    pallas_call x10, Pallas kernels, call(): pl.pallas_call(body, in_specs=specs, out_specs=[far] * far_out + [near] *...  57.7 us
    all_to_all x2, waiting for transfers between devices, trade_chips(): return lax.all_to_all(value, CHIPS, split_axis=0, concat_axis=0, tiled=True)  29.9 us
    all_to_all x1, blocking collectives, trade_chips(): return lax.all_to_all(value, CHIPS, split_axis=0, concat_axis=0, tiled=True)  29.2 us
    ppermute x8, starting transfers between devices, passed_along(): lax.ppermute(value, axis, [(source, source + steps) for source in range(i...  20.8 us
    all_to_all x2, starting transfers between devices, trade_slots(): moved = lax.all_to_all(shaped, ALL, split_axis=0, concat_axis=0, tiled=True)  16.1 us
    all_to_all x2, starting transfers between devices, trade_chips(): return lax.all_to_all(value, CHIPS, split_axis=0, concat_axis=0, tiled=True)  9.62 us
    unnamed x28, local copies, waits for them, and re-layouts  5.25 us
  transfers between devices with their start and end apart: 15, of which 6 were waited for; matrix products, arithmetic and copies ran while one was open for 1% of the time, Pallas kernels for 6%

profile of v4, /device:TPU:1, one launch (start us, length us, event | category | flops | bytes accessed | tf_op | source)
XLA Modules:
  0.0 243.2 jit_solution(4628729487586409497)
XLA Ops:
  0.6 1.3 reshape.53.lists
  1.9 2.0 shard_map.188
  3.9 0.8 fusion.1
  4.7 1.3 collective-permute-start.3
  6.0 4.6 %collective-permute-start.2 = (bf16[32,512]{1,0:T(8,128)(2,1)S(1)}, bf16[32,512]{1,0:T(8,128)(2,1)S(1)}, u32[]{:S(2)}, u32[]{:S(2)}) collective-permute-start(bf16[32,512]{1,0:T(8,128)(2,1)S(1)} %get-tuple-element.93), channel_id=1, source_target_pairs={{0,1},{1,2},{2,3},{3,4},{4,5},{5,6},{6,7},{7,8},{8,9},{9,10},{10,1... | collective-permute-start | bytes 98312 | tf_op jit(solution)/shard_map/ppermute | solution.py:328
  10.7 3.2 %collective-permute-start.1 = (bf16[32,512]{1,0:T(8,128)(2,1)S(1)}, bf16[32,512]{1,0:T(8,128)(2,1)S(1)}, u32[]{:S(2)}, u32[]{:S(2)}) collective-permute-start(bf16[32,512]{1,0:T(8,128)(2,1)S(1)} %get-tuple-element.94), channel_id=1, source_target_pairs={{16,0},{32,16},{48,32},{64,48},{80,64},{96,80},{112,96},{17,1},{33... | collective-permute-start | bytes 98312 | tf_op jit(solution)/shard_map/ppermute | solution.py:328
  13.9 3.6 %collective-permute-start = (bf16[32,512]{1,0:T(8,128)(2,1)S(1)}, bf16[32,512]{1,0:T(8,128)(2,1)S(1)}, u32[]{:S(2)}, u32[]{:S(2)}) collective-permute-start(bf16[32,512]{1,0:T(8,128)(2,1)S(1)} %get-tuple-element.95), channel_id=1, source_target_pairs={{0,16},{16,32},{32,48},{48,64},{64,80},{80,96},{96,112},{1,17},{17... | collective-permute-start | bytes 98312 | tf_op jit(solution)/shard_map/ppermute | solution.py:328
  17.4 2.9 %shard_map.189 = (s32[1,512]{1,0:T(1,128)}, bf16[512,512]{1,0:T(8,128)(2,1)}, bf16[512,512]{1,0:T(8,128)(2,1)}) custom-call(s32[4,128]{1,0:T(4,128)} %bitcast.21, bf16[512,512]{1,0:T(8,128)(2,1)} %nodes.9, bf16[512,512]{1,0:T(8,128)(2,1)} %source_weight.7, bf16[512,512]{1,0:T(8,128)(2,1)} %target_weight.3), custom_call_target="tpu_custom_call" | custom-call | tf_op jit(solution)/shard_map/pallas_call | solution.py:313
  20.4 0.6 copy-done.5
  21.0 0.0 copy-done.6
  21.0 0.0 copy-done.7
  21.0 0.0 copy-done.8
  21.0 12.9 %shard_map.190 = (bf16[2048,512]{1,0:T(8,128)(2,1)}, bf16[2048,512]{1,0:T(8,128)(2,1)}, bf16[2048,512]{1,0:T(8,128)(2,1)}, bf16[512,512]{1,0:T(8,128)(2,1)}, bf1...) custom-call(bf16[32,512]{1,0:T(8,128)(2,1)} %copy-done.8, ...), custom_call_target="tpu_custom_call" | custom-call | tf_op jit(solution)/shard_map/pallas_call | solution.py:313
  34.0 11.6 %all-to-all-start = ((bf16[128,8,1024]{2,1,0:T(8,128)(2,1)}), bf16[128,8,1024]{2,1,0:T(8,128)(2,1)S(1)}, u32[]{:S(2)}, u32[]{:S(2)}) async-start(bf16[128,8,1024]{2,1,0:T(8,128)(2,1)} %bitcast.15), calls=%async_computation | async-start | bytes 4194304 | tf_op jit(solution)/shard_map/all_to_all | solution.py:341
  45.6 1.9 shard_map.191
  47.4 27.9 %all-to-all-done = bf16[128,8,1024]{2,1,0:T(8,128)(2,1)S(1)} async-done(((bf16[128,8,1024]{2,1,0:T(8,128)(2,1)}), bf16[128,8,1024]{2,1,0:T(8,128)(2,1)S(1)}, u32[]{:S(2)}, u32[]{:S(2)}) %all-to-all-start) | async-done | bytes 2097184 | tf_op jit(solution)/shard_map/all_to_all | solution.py:341
  75.3 1.4 copy-done.1
  76.7 4.7 %shard_map.192 = (bf16[1024,1024]{1,0:T(8,128)(2,1)}, bf16[128,512]{1,0:T(8,128)(2,1)}, bf16[128,512]{1,0:T(8,128)(2,1)}) custom-call(bf16[1024,1024]{1,0:T(8,128)(2,1)} %bitcast.13, bf16[128,1024]{1,0:T(8,128)(2,1)} %get-tuple-element.52.members, bf16[1024,128]{1,0:T(8,128)(2,1)} %get-tuple-element.53.picks, f32[128,128]{1,0:T(8,128)} %get-tuple-element.54.counts, ...), custom_call_target="tpu_custom_call" | custom-call | tf_op jit(solution)/shard_map/pallas_call | solution.py:313
  81.4 4.6 %all-to-all-start.1 = ((bf16[128,8,1024]{2,1,0:T(8,128)(2,1)}), bf16[128,8,1024]{2,1,0:T(8,128)(2,1)S(1)}, u32[]{:S(2)}, u32[]{:S(2)}) async-start(bf16[128,8,1024]{2,1,0:T(8,128)(2,1)} %bitcast.14), calls=%async_computation.1 | async-start | bytes 4194304 | tf_op jit(solution)/shard_map/all_to_all | solution.py:341
  85.9 29.9 %all-to-all-done.1 = bf16[128,8,1024]{2,1,0:T(8,128)(2,1)S(1)} async-done(((bf16[128,8,1024]{2,1,0:T(8,128)(2,1)}), bf16[128,8,1024]{2,1,0:T(8,128)(2,1)S(1)}, u32[]{:S(2)}, u32[]{:S(2)}) %all-to-all-start.1) | async-done | bytes 2097184 | tf_op jit(solution)/shard_map/all_to_all | solution.py:341
  115.8 1.4 copy-done
  117.2 6.6 %shard_map.193 = (bf16[512,512]{1,0:T(8,128)(2,1)}, bf16[512,512]{1,0:T(8,128)(2,1)}, bf16[4096,128]{1,0:T(8,128)(2,1)}, bf16[4096,128]{1,0:T(8,128)(2,1)}) custom-call(s32[1]{0:T(128)} %bitcast.8.core, bf16[1024,1024]{1,0:T(8,128)(2,1)} %bitcast.11, s32[1,512]{1,0:T(1,128)} %get-tuple-element.50.slot, bf16[512,512]{1,0:T(8,128)(2,1)} %cotangent.5, ...), custom_call_target="tpu_custom_call" | custom-call | tf_op jit(solution)/shard_map/pallas_call | solution.py:313
  123.7 13.4 %shard_map.194 = (bf16[3072,128]{1,0:T(8,128)(2,1)}, bf16[3072,128]{1,0:T(8,128)(2,1)}, bf16[640,512]{1,0:T(8,128)(2,1)}, bf16[512,512]{1,0:T(8,128)(2,1)}, bf16[128,512]{1,0:T(8,128)(2,1)}) custom-call(s32[1]{0:T(128)} %bitcast.8.core, s32[16,128]{1,0:T(8,128)} %bitcast.17, s32[16,128]{1,0:T(8,128)} %bitcast.19, ...), custom_call_target="tpu_custom_call" | custom-call | tf_op jit(solution)/shard_map/pallas_call | solution.py:313
  137.1 0.0 copy-start.4
  137.1 1.2 collective-permute-start.9
  138.3 0.1 collective-permute-start.8
  138.4 2.0 collective-permute-done.9
  140.4 2.2 add_convert_fusion.1
  142.6 4.6 %all-to-all-start.3 = ((bf16[64,48,128]{2,1,0:T(8,128)(2,1)}), bf16[64,48,128]{2,1,0:T(8,128)(2,1)S(1)}, u32[]{:S(2)}, u32[]{:S(2)}) async-start(bf16[64,48,128]{2,1,0:T(8,128)(2,1)} %bitcast.10), calls=%async_computation.3 | async-start | bytes 1572864 | tf_op jit(solution)/shard_map/all_to_all | solution.py:354
  147.3 1.2 add_convert_fusion
  148.6 13.7 %all-to-all-done.3 = bf16[64,48,128]{2,1,0:T(8,128)(2,1)S(1)} async-done(((bf16[64,48,128]{2,1,0:T(8,128)(2,1)}), bf16[64,48,128]{2,1,0:T(8,128)(2,1)S(1)}, u32[]{:S(2)}, u32[]{:S(2)}) %all-to-all-start.3) | async-done | bytes 786464 | tf_op jit(solution)/shard_map/all_to_all | solution.py:354
  162.3 5.0 %all-to-all-start.2 = ((bf16[64,64,128]{2,1,0:T(8,128)(2,1)}), bf16[64,64,128]{2,1,0:T(8,128)(2,1)S(1)}, u32[]{:S(2)}, u32[]{:S(2)}) async-start(bf16[64,64,128]{2,1,0:T(8,128)(2,1)} %bitcast.9), calls=%async_computation.2 | async-start | bytes 2097152 | tf_op jit(solution)/shard_map/all_to_all | solution.py:354
  167.3 0.1 reduce_sum.25
  167.4 16.1 %all-to-all-done.2 = bf16[64,64,128]{2,1,0:T(8,128)(2,1)S(1)} async-done(((bf16[64,64,128]{2,1,0:T(8,128)(2,1)}), bf16[64,64,128]{2,1,0:T(8,128)(2,1)S(1)}, u32[]{:S(2)}, u32[]{:S(2)}) %all-to-all-start.2) | async-done | bytes 1048608 | tf_op jit(solution)/shard_map/all_to_all | solution.py:354
  183.6 0.2 reduce_sum.24
  183.7 0.2 broadcast_in_dim.2
  184.0 29.2 %all_to_all.25.gathered = bf16[64,112,128]{2,1,0:T(8,128)(2,1)S(1)} all-to-all(bf16[64,112,128]{2,1,0:T(8,128)(2,1)S(1)} %broadcast_in_dim.2), channel_id=1, replica_groups=mesh['z'=4,'core'=2,'x'=4,'y'=4] {'z','x','y'}, dimensions={0} | all-to-all | bytes 3670016 | tf_op jit(solution)/shard_map/all_to_all | solution.py:354
  213.2 3.6 %collective-permute-start.10 = (bf16[64,112,128]{2,1,0:T(8,128)(2,1)S(1)}, bf16[64,112,128]{2,1,0:T(8,128)(2,1)S(1)}, u32[]{:S(2)}, u32[]{:S(2)}) collective-permute-start(bf16[64,112,128]{2,1,0:T(8,128)(2,1)S(1)} %all_to_all.25.gathered), channel_id=1, source_target_pairs={{0,16},{16,0},{1,17},{17,1},{2,18},{18,2},{3,19},{19,3},{4,20},{20... | collective-permute-start | bytes 5505032 | tf_op jit(solution)/shard_map/ppermute | solution.py:346
  216.8 2.5 %collective-permute-start.7 = (bf16[32,512]{1,0:T(8,128)(2,1)S(1)}, bf16[32,512]{1,0:T(8,128)(2,1)S(1)}, u32[]{:S(2)}, u32[]{:S(2)}) collective-permute-start(bf16[32,512]{1,0:T(8,128)(2,1)S(1)} %get-tuple-element.88), channel_id=1, source_target_pairs={{0,1},{1,2},{2,3},{3,4},{4,5},{5,6},{6,7},{7,8},{8,9},{9,10},{10,1... | collective-permute-start | bytes 98312 | tf_op jit(solution)/shard_map/ppermute | solution.py:328
  219.3 1.3 collective-permute-start.6
  220.6 1.9 collective-permute-start.5
  222.6 2.4 collective-permute-start.4
  225.0 2.8 %collective-permute-done.4.back_0 = bf16[32,512]{1,0:T(8,128)(2,1)S(1)} collective-permute-done((bf16[32,512]{1,0:T(8,128)(2,1)S(1)}, bf16[32,512]{1,0:T(8,128)(2,1)S(1)}, u32[]{:S(2)}, u32[]{:S(2)}) %collective-permute-start.4) | collective-permute-done | bytes 32800 | tf_op jit(solution)/shard_map/ppermute | solution.py:328
  227.8 0.6 copy-done.13
  228.4 6.5 %shard_map.195 = (bf16[512,512]{1,0:T(8,128)(2,1)}, f32[512,512]{1,0:T(8,128)}) custom-call(bf16[1024,1024]{1,0:T(8,128)(2,1)} %bitcast.12, s32[1,512]{1,0:T(1,128)} %get-tuple-element.50.slot, bf16[512,512]{1,0:T(8,128)(2,1)} %cotangent.5, bf16[512,512]{1,0:T(8,128)(2,1)} %get-tuple-element.56.refined, bf16[512,512]{1,0:T(8,128)(2,1)} %get-tuple-element.62.grad_hidden, ...), custom_call_target="tpu_custom_call" | custom-call | tf_op jit(solution)/shard_map/pallas_call | solution.py:313
  234.9 3.4 %shard_map.196 = (f32[512,512]{1,0:T(8,128)}, f32[512,512]{1,0:T(8,128)}, f32[512,512]{1,0:T(8,128)}, f32[1024,512]{1,0:T(8,128)}, f32[512,512]{1,0:T(8,128)}, /*index=5*/f32[512,512]{1,0:T(8,128)}) custom-call(s32[1]{0:T(128)} %bitcast.8.core, bf16[64,112,128]{2,1,0:T(8,128)(2,1)} %copy-done.2), custom_call_target="tpu_custom_call" | custom-call | tf_op jit(solution)/shard_map/pallas_call | solution.py:313
  238.4 1.2 copy-done.3
  239.6 3.4 %shard_map.197 = (f32[512,512]{1,0:T(8,128)}, f32[512,512]{1,0:T(8,128)}, f32[512,512]{1,0:T(8,128)}, f32[1024,512]{1,0:T(8,128)}, f32[512,512]{1,0:T(8,128)}, /*index=5*/f32[512,512]{1,0:T(8,128)}) custom-call(s32[1]{0:T(128)} %bitcast.8.core, ...), custom_call_target="tpu_custom_call", output_to_operand_aliasing={{0}: (2, {}), {1}: (3, {}), {2}: (4, {}), {3}: (5, {}), {4}... | custom-call | tf_op jit(solution)/shard_map/pallas_call | solution.py:313
  (30 shorter events, 0.1 us)
Async XLA Ops:
  4.7 15.7 %collective-permute-start.3 = (bf16[32,512]{1,0:T(8,128)(2,1)S(1)}, bf16[32,512]{1,0:T(8,128)(2,1)S(1)}, u32[]{:S(2)}, u32[]{:S(2)}) collective-permute-start(bf16[32,512]{1,0:T(8,128)(2,1)S(1)} %get-tuple-element.92), channel_id=1, source_target_pairs={{1,0},{2,1},{3,2},{4,3},{5,4},{6,5},{7,6},{8,7},{9,8},{10,9},{11,1... | collective-permute-start | bytes 98312 | tf_op jit(solution)/shard_map/ppermute | solution.py:328
  6.0 14.4 %collective-permute-start.2 = (bf16[32,512]{1,0:T(8,128)(2,1)S(1)}, bf16[32,512]{1,0:T(8,128)(2,1)S(1)}, u32[]{:S(2)}, u32[]{:S(2)}) collective-permute-start(bf16[32,512]{1,0:T(8,128)(2,1)S(1)} %get-tuple-element.93), channel_id=1, source_target_pairs={{0,1},{1,2},{2,3},{3,4},{4,5},{5,6},{6,7},{7,8},{8,9},{9,10},{10,1... | collective-permute-start | bytes 98312 | tf_op jit(solution)/shard_map/ppermute | solution.py:328
  10.7 9.7 %collective-permute-start.1 = (bf16[32,512]{1,0:T(8,128)(2,1)S(1)}, bf16[32,512]{1,0:T(8,128)(2,1)S(1)}, u32[]{:S(2)}, u32[]{:S(2)}) collective-permute-start(bf16[32,512]{1,0:T(8,128)(2,1)S(1)} %get-tuple-element.94), channel_id=1, source_target_pairs={{16,0},{32,16},{48,32},{64,48},{80,64},{96,80},{112,96},{17,1},{33... | collective-permute-start | bytes 98312 | tf_op jit(solution)/shard_map/ppermute | solution.py:328
  13.9 6.6 %collective-permute-start = (bf16[32,512]{1,0:T(8,128)(2,1)S(1)}, bf16[32,512]{1,0:T(8,128)(2,1)S(1)}, u32[]{:S(2)}, u32[]{:S(2)}) collective-permute-start(bf16[32,512]{1,0:T(8,128)(2,1)S(1)} %get-tuple-element.95), channel_id=1, source_target_pairs={{0,16},{16,32},{32,48},{48,64},{64,80},{80,96},{96,112},{1,17},{17... | collective-permute-start | bytes 98312 | tf_op jit(solution)/shard_map/ppermute | solution.py:328
  20.4 0.6 copy-start.5
  20.4 0.6 copy-start.6
  20.4 0.6 copy-start.7
  20.4 0.6 copy-start.8
  34.0 41.3 %all-to-all-start = ((bf16[128,8,1024]{2,1,0:T(8,128)(2,1)}), bf16[128,8,1024]{2,1,0:T(8,128)(2,1)S(1)}, u32[]{:S(2)}, u32[]{:S(2)}) async-start(bf16[128,8,1024]{2,1,0:T(8,128)(2,1)} %bitcast.15), calls=%async_computation | async-start | bytes 4194304 | tf_op jit(solution)/shard_map/all_to_all | solution.py:341
  75.3 1.4 copy-start.1
  81.4 34.4 %all-to-all-start.1 = ((bf16[128,8,1024]{2,1,0:T(8,128)(2,1)}), bf16[128,8,1024]{2,1,0:T(8,128)(2,1)S(1)}, u32[]{:S(2)}, u32[]{:S(2)}) async-start(bf16[128,8,1024]{2,1,0:T(8,128)(2,1)} %bitcast.14), calls=%async_computation.1 | async-start | bytes 4194304 | tf_op jit(solution)/shard_map/all_to_all | solution.py:341
  115.8 1.4 copy-start
  137.1 10.2 %copy-start.4 = (bf16[4096,128]{1,0:T(8,128)(2,1)S(1)}, bf16[4096,128]{1,0:T(8,128)(2,1)}, u32[]{:S(2)}) copy-start(bf16[4096,128]{1,0:T(8,128)(2,1)} %get-tuple-element.72) | copy-start | bytes 3145732
  137.1 3.3 %collective-permute-start.9 = (bf16[3072,128]{1,0:T(8,128)(2,1)}, bf16[3072,128]{1,0:T(8,128)(2,1)S(1)}, u32[]{:S(2)}, u32[]{:S(2)}) collective-permute-start(bf16[3072,128]{1,0:T(8,128)(2,1)} %get-tuple-element.75), channel_id=1, source_target_pairs={{0,16},{16,0},{1,17},{17,1},{2,18},{18,2},{3,19},{19,3},{4,20},{20... | collective-permute-start | bytes 2359304 | tf_op jit(solution)/shard_map/ppermute | solution.py:346
  138.3 9.0 %collective-permute-start.8 = (bf16[4096,128]{1,0:T(8,128)(2,1)}, bf16[4096,128]{1,0:T(8,128)(2,1)S(1)}, u32[]{:S(2)}, u32[]{:S(2)}) collective-permute-start(bf16[4096,128]{1,0:T(8,128)(2,1)} %get-tuple-element.73), channel_id=1, source_target_pairs={{0,16},{16,0},{1,17},{17,1},{2,18},{18,2},{3,19},{19,3},{4,20},{20... | collective-permute-start | bytes 3145736 | tf_op jit(solution)/shard_map/ppermute | solution.py:346
  142.6 19.7 %all-to-all-start.3 = ((bf16[64,48,128]{2,1,0:T(8,128)(2,1)}), bf16[64,48,128]{2,1,0:T(8,128)(2,1)S(1)}, u32[]{:S(2)}, u32[]{:S(2)}) async-start(bf16[64,48,128]{2,1,0:T(8,128)(2,1)} %bitcast.10), calls=%async_computation.3 | async-start | bytes 1572864 | tf_op jit(solution)/shard_map/all_to_all | solution.py:354
  162.3 21.2 %all-to-all-start.2 = ((bf16[64,64,128]{2,1,0:T(8,128)(2,1)}), bf16[64,64,128]{2,1,0:T(8,128)(2,1)S(1)}, u32[]{:S(2)}, u32[]{:S(2)}) async-start(bf16[64,64,128]{2,1,0:T(8,128)(2,1)} %bitcast.9), calls=%async_computation.2 | async-start | bytes 2097152 | tf_op jit(solution)/shard_map/all_to_all | solution.py:354
  184.0 32.8 %copy-start.9 = (bf16[128,512]{1,0:T(8,128)(2,1)S(1)}, bf16[128,512]{1,0:T(8,128)(2,1)}, u32[]{:S(2)}) copy-start(bf16[128,512]{1,0:T(8,128)(2,1)} %get-tuple-element.69) | copy-start | bytes 393220
  213.2 21.7 %copy-start.2 = (bf16[64,112,128]{2,1,0:T(8,128)(2,1)}, bf16[64,112,128]{2,1,0:T(8,128)(2,1)S(1)}, u32[]{:S(2)}) copy-start(bf16[64,112,128]{2,1,0:T(8,128)(2,1)S(1)} %all_to_all.25.gathered) | copy-start | bytes 5505028
  213.2 25.1 %collective-permute-start.10 = (bf16[64,112,128]{2,1,0:T(8,128)(2,1)S(1)}, bf16[64,112,128]{2,1,0:T(8,128)(2,1)S(1)}, u32[]{:S(2)}, u32[]{:S(2)}) collective-permute-start(bf16[64,112,128]{2,1,0:T(8,128)(2,1)S(1)} %all_to_all.25.gathered), channel_id=1, source_target_pairs={{0,16},{16,0},{1,17},{17,1},{2,18},{18,2},{3,19},{19,3},{4,20},{20... | collective-permute-start | bytes 5505032 | tf_op jit(solution)/shard_map/ppermute | solution.py:346
  216.8 8.2 %collective-permute-start.7 = (bf16[32,512]{1,0:T(8,128)(2,1)S(1)}, bf16[32,512]{1,0:T(8,128)(2,1)S(1)}, u32[]{:S(2)}, u32[]{:S(2)}) collective-permute-start(bf16[32,512]{1,0:T(8,128)(2,1)S(1)} %get-tuple-element.88), channel_id=1, source_target_pairs={{0,1},{1,2},{2,3},{3,4},{4,5},{5,6},{6,7},{7,8},{8,9},{9,10},{10,1... | collective-permute-start | bytes 98312 | tf_op jit(solution)/shard_map/ppermute | solution.py:328
  219.3 5.7 %collective-permute-start.6 = (bf16[32,512]{1,0:T(8,128)(2,1)S(1)}, bf16[32,512]{1,0:T(8,128)(2,1)S(1)}, u32[]{:S(2)}, u32[]{:S(2)}) collective-permute-start(bf16[32,512]{1,0:T(8,128)(2,1)S(1)} %get-tuple-element.89), channel_id=1, source_target_pairs={{1,0},{2,1},{3,2},{4,3},{5,4},{6,5},{7,6},{8,7},{9,8},{10,9},{11,1... | collective-permute-start | bytes 98312 | tf_op jit(solution)/shard_map/ppermute | solution.py:328
  220.6 4.4 %collective-permute-start.5 = (bf16[32,512]{1,0:T(8,128)(2,1)S(1)}, bf16[32,512]{1,0:T(8,128)(2,1)S(1)}, u32[]{:S(2)}, u32[]{:S(2)}) collective-permute-start(bf16[32,512]{1,0:T(8,128)(2,1)S(1)} %get-tuple-element.90), channel_id=1, source_target_pairs={{0,16},{16,32},{32,48},{48,64},{64,80},{80,96},{96,112},{1,17},{17... | collective-permute-start | bytes 98312 | tf_op jit(solution)/shard_map/ppermute | solution.py:328
  222.6 5.2 %collective-permute-start.4 = (bf16[32,512]{1,0:T(8,128)(2,1)S(1)}, bf16[32,512]{1,0:T(8,128)(2,1)S(1)}, u32[]{:S(2)}, u32[]{:S(2)}) collective-permute-start(bf16[32,512]{1,0:T(8,128)(2,1)S(1)} %get-tuple-element.91), channel_id=1, source_target_pairs={{16,0},{32,16},{48,32},{64,48},{80,64},{96,80},{112,96},{17,1},{33... | collective-permute-start | bytes 98312 | tf_op jit(solution)/shard_map/ppermute | solution.py:328
  225.0 2.8 %copy-start.10 = (bf16[32,512]{1,0:T(8,128)(2,1)}, bf16[32,512]{1,0:T(8,128)(2,1)S(1)}, u32[]{:S(2)}) copy-start(bf16[32,512]{1,0:T(8,128)(2,1)S(1)} %collective-permute-done.7.back_3) | copy-start | bytes 98308
  225.0 2.8 %copy-start.11 = (bf16[32,512]{1,0:T(8,128)(2,1)}, bf16[32,512]{1,0:T(8,128)(2,1)S(1)}, u32[]{:S(2)}) copy-start(bf16[32,512]{1,0:T(8,128)(2,1)S(1)} %collective-permute-done.6.back_2) | copy-start | bytes 98308
  225.0 2.8 %copy-start.12 = (bf16[32,512]{1,0:T(8,128)(2,1)}, bf16[32,512]{1,0:T(8,128)(2,1)S(1)}, u32[]{:S(2)}) copy-start(bf16[32,512]{1,0:T(8,128)(2,1)S(1)} %collective-permute-done.5.back_1) | copy-start | bytes 98308
  227.8 0.6 copy-start.13
  238.3 1.2 copy-start.3
